TPU v7x, 32 devices: a whole 2x2x4 slice. The times are simulated.
32 devices in a mesh: ctx: 8 (over y, x, core), tp: 4 (over z).
Axes of the slice: x: 2, y: 2, z: 4, core: 2. Of those that a mesh axis runs over, the one named last changes fastest.
Arguments:
- queries: bfloat16 [2048, 4096], P('ctx', 'tp'), may hold values from -100 to 100
- key_pages: bfloat16 [32, 64, 1024], P('ctx', None, 'tp'), may hold values from -5 to 5
- value_pages: bfloat16 [32, 64, 1024], P('ctx', None, 'tp'), may hold values from -6 to 6
- mixer_input: bfloat16 [2048, 4096], P('ctx', 'tp'), may hold values from -6 to 6
- state_write: bfloat16 [2048, 1024], P('ctx', 'tp'), may hold values from -0.029907227 to 0.029907227
- state_read: bfloat16 [2048, 1024], P('ctx', 'tp'), may hold values from -6 to 6
- log_decay: float32 [32, 2048], P('tp', 'ctx'), may hold values from -1 to 0
- skip_gain: float32 [32], P('tp'), may hold values from 0.5 to 1.5
- doc_lengths: int32 [4], replicated, may hold values from 1 to 1024, 2048 in all
- page_table: int32 [32], replicated, may hold values from 0 to 31, as said below
- attention_weight: bfloat16 [4096, 4096], P('tp'), may hold values from -0.75 to 0.75
- mixer_weight: bfloat16 [4096, 4096], P('tp'), may hold values from -0.09375 to 0.09375
Outputs:
- mixed: bfloat16 [2048, 4096], P(('ctx', 'tp'))
Inputs may be any that keep to these rules, and one draw needn't show every extreme that they name: `doc_lengths`: the lengths sum to 2048; the longest is exactly 1024. `page_table`: A permutation: every physical page holds exactly one logical page.
All inputs are finite; a program needn't handle non-finite values.
Results may differ from a plain program's by a relative error of at most 0.007.
Values may be sent and summed in bfloat16 or wider, within the bound.
No kernel may reach another device: no remote copies, remote signals or barrier semaphores. Data moves between devices by JAX's collectives and lax.ppermute only.
A program may use at most 256 MiB of HBM per device.

v0:
```python
import jax
import jax.numpy as jnp
from jax import lax
from jax.sharding import PartitionSpec as P

HEAD_DIM = 128
SSM_HEAD_DIM = 128
STATE = 128


def entering(array, axis, join, neutral):
    place = lax.axis_index(axis)
    gathered = jax.tree.map(
        lambda a, kind: lax.all_gather(a.astype(kind), axis), array, (jnp.bfloat16, jnp.bfloat16)
    )
    state = jax.tree.map(lambda a, e: jnp.zeros_like(a) + jnp.asarray(e, a.dtype), array, neutral)

    def one(lap, state):
        return join(
            state,
            jax.tree.map(
                lambda a, own: lax.dynamic_index_in_dim(a, lap, 0, False).astype(own.dtype),
                gathered,
                array,
            ),
        )

    return lax.fori_loop(0, place, one, state)


def segment_of(positions, doc_ends):
    return jnp.sum((positions[:, None] >= doc_ends[None, :]).astype(jnp.int32), axis=1)


def mixer_local(head_input, write_rows, read_rows, decay_rows, block_seg, prev_seg, per_group):
    tok_rows = head_input.shape[0]
    decay_sum = jnp.cumsum(decay_rows, axis=1)
    token_order = jnp.arange(tok_rows, dtype=jnp.int32)
    visible = (token_order[None, :] <= token_order[:, None]) & (
        block_seg[None, :] == block_seg[:, None]
    )
    decay_diff = decay_sum[:, :, None] - decay_sum[:, None, :]
    decay_mat = jnp.where(visible[None], jnp.exp(jnp.minimum(decay_diff, 0.0)), 0.0)
    inner_prod = jnp.einsum(
        "tgn,sgn->gts", read_rows, write_rows, preferred_element_type=jnp.float32
    )
    mixing = (decay_mat * jnp.repeat(inner_prod, per_group, axis=0)).astype(jnp.bfloat16)
    intra_out = jnp.einsum("hts,shp->thp", mixing, head_input, preferred_element_type=jnp.float32)
    end_seg = block_seg[-1]
    end_weight = jnp.where(
        (block_seg == end_seg)[None, :], jnp.exp(decay_sum[:, -1:] - decay_sum), 0.0
    )
    write_heads = jnp.repeat(write_rows, per_group, axis=1)
    end_write = (jnp.transpose(end_weight)[:, :, None] * write_heads).astype(jnp.bfloat16)
    block_state = jnp.einsum(
        "thn,thp->hnp", end_write, head_input, preferred_element_type=jnp.float32
    )
    block_gain = jnp.where(end_seg == prev_seg, jnp.exp(decay_sum[:, -1]), 0.0)
    return (intra_out, block_gain, block_state, decay_sum)


def mixer_entry(
    intra_out, decay_sum, read_rows, head_input, skip_gain, block_seg, prev_seg, state_in, per_group
):
    read_heads = jnp.repeat(read_rows, per_group, axis=1).astype(jnp.float32)
    inter_out = jnp.einsum("thn,hnp->thp", read_heads, state_in, precision=lax.Precision.HIGHEST)
    entry_gain = jnp.where((block_seg == prev_seg)[None, :], jnp.exp(decay_sum), 0.0)
    return (
        intra_out
        + jnp.transpose(entry_gain)[:, :, None] * inter_out
        + skip_gain[None, :, None] * head_input.astype(jnp.float32)
    )


def compose_states(earlier, later):
    return (earlier[0] * later[0], later[0][:, None, None] * earlier[1] + later[1])


def shards(
    queries,
    key_pages,
    value_pages,
    mixer_input,
    state_write,
    state_read,
    log_decay,
    skip_gain,
    doc_lengths,
    page_table,
    attention_weight,
    mixer_weight,
):
    my_block = lax.axis_index("ctx")
    tok_rows = queries.shape[0]
    doc_ends = jnp.cumsum(doc_lengths)
    first_pos = my_block * tok_rows
    positions = first_pos + jnp.arange(tok_rows, dtype=jnp.int32)
    query_seg = segment_of(positions, doc_ends)
    head_local = queries.shape[1] // HEAD_DIM
    kv_local = key_pages.shape[2] // HEAD_DIM
    group_size = head_local // kv_local
    page_len = key_pages.shape[1]
    page_total = page_table.shape[0]
    page_ids = jnp.arange(page_total, dtype=jnp.int32)
    logical_of = jnp.sum(
        jnp.where(page_table[:, None] == page_ids[None, :], page_ids[:, None], 0), axis=0
    )
    query_heads = queries.reshape(tok_rows, kv_local, group_size, HEAD_DIM)
    stat_shape = (tok_rows, kv_local, group_size)
    key_rows = lax.all_gather(key_pages, "ctx", axis=0, tiled=True)
    page_count = key_rows.shape[0]
    key_pos = (
        logical_of[:, None] * page_len + jnp.arange(page_len, dtype=jnp.int32)[None, :]
    ).reshape(-1)
    key_seg = segment_of(key_pos, doc_ends)
    visible = (key_pos[None, :] <= positions[:, None]) & (key_seg[None, :] == query_seg[:, None])
    flat_keys = key_rows.reshape(page_count * page_len, kv_local, HEAD_DIM)
    flat_values = lax.all_gather(value_pages, "ctx", axis=0, tiled=True).reshape(
        page_count * page_len, kv_local, HEAD_DIM
    )
    run_max = jnp.full(stat_shape, -1e30, jnp.float32)
    scores = jnp.einsum(
        "tgjd,sgd->tgjs", query_heads, flat_keys, preferred_element_type=jnp.float32
    ) * HEAD_DIM ** (-0.5)
    shown = visible[:, None, None, :]
    new_max = jnp.maximum(run_max, jnp.max(jnp.where(shown, scores, -1e30), axis=3))
    weights = jnp.where(shown, jnp.exp(scores - new_max[..., None]), 0.0)
    new_sum = jnp.sum(weights, axis=3)
    probabilities = weights.astype(jnp.bfloat16)
    new_acc = jnp.einsum(
        "tgjs,sgd->tgjd", probabilities, flat_values, preferred_element_type=jnp.float32
    )
    attention_out = (
        (new_acc / new_sum[..., None]).reshape(tok_rows, head_local * HEAD_DIM).astype(jnp.bfloat16)
    )
    ssm_local = mixer_input.shape[1] // SSM_HEAD_DIM
    group_local = state_write.shape[1] // STATE
    per_group = ssm_local // group_local
    head_input = mixer_input.reshape(tok_rows, ssm_local, SSM_HEAD_DIM)
    write_rows = state_write.reshape(tok_rows, group_local, STATE)
    read_rows = state_read.reshape(tok_rows, group_local, STATE)
    before_pos = jnp.reshape(first_pos - 1, (1,))
    prev_seg = jnp.where(first_pos > 0, segment_of(before_pos, doc_ends)[0], -1)
    intra_out, block_gain, block_state, decay_sum = mixer_local(
        head_input, write_rows, read_rows, log_decay, query_seg, prev_seg, per_group
    )
    gain_in, state_in = entering(
        (block_gain, block_state),
        "ctx",
        compose_states,
        (jnp.ones_like(block_gain), jnp.zeros_like(block_state)),
    )
    mixer_rows = mixer_entry(
        intra_out,
        decay_sum,
        read_rows,
        head_input,
        skip_gain,
        query_seg,
        prev_seg,
        state_in,
        per_group,
    )
    mixer_out = mixer_rows.reshape(tok_rows, ssm_local * SSM_HEAD_DIM).astype(jnp.bfloat16)
    mixed = lax.psum_scatter(
        jnp.dot(attention_out, attention_weight, preferred_element_type=jnp.float32)
        + jnp.dot(mixer_out, mixer_weight, preferred_element_type=jnp.float32),
        "tp",
        scatter_dimension=0,
        tiled=True,
    )
    return mixed.astype(jnp.bfloat16)


def solution(mesh):
    placed = (
        P("ctx", "tp"),
        P("ctx", None, "tp"),
        P("ctx", None, "tp"),
        P("ctx", "tp"),
        P("ctx", "tp"),
        P("ctx", "tp"),
        P("tp", "ctx"),
        P("tp"),
        P(),
        P(),
        P("tp", None),
        P("tp", None),
    )
    return jax.shard_map(
        shards, mesh=mesh, in_specs=placed, out_specs=P(("ctx", "tp"), None), check_vma=False
    )
```

profile of v0, /device:TPU:0, one launch (start us, length us, event | category | flops | bytes accessed | tf_op | source)
XLA Modules:
  0.0 194.3 jit_solution(17334929127929989161)
XLA Ops:
  6.5 0.7 all-gather.6.cloned.1.call-update
  7.3 0.7 all-gather.8.cloned.1.call-update
  8.1 0.8 reduce-window.10
  9.0 0.6 slice.15
  9.6 1.2 reduce-window.11
  11.0 1.2 copy.66
  12.3 0.9 reshape.265
  13.3 0.6 fusion.30
  14.6 0.7 broadcast_compare_fusion
  15.7 1.0 convolution_convert_fusion
  17.6 1.1 fusion.26
  18.7 0.7 select_reduce_fusion
  19.7 1.4 compare_and_fusion
  21.2 2.2 %reshape.260 = bf16[256,2,4,128]{3,2,1,0:T(4,128)(2,1)} reshape(bf16[256,1024]{1,0:T(8,128)(2,1)} %param.14) | data formatting | bytes 1048576 | tf_op jit(solution)/shard_map/reshape | solution.py:108
  23.4 0.5 fusion.8
  23.9 0.5 convolution_bitcast_fusion.1
  24.6 0.7 dynamic-slice
  26.0 0.2 dynamic-update-slice
  26.2 15.3 %all-reduce = bf16[64]{0:T(256)(128)(2,1)S(1)} all-reduce(bf16[64]{0:T(256)(128)(2,1)S(1)} %dynamic-update-slice), channel_id=2, replica_groups=mesh['ctx'=8,'tp'=4] {'ctx'}, use_global_device_ids=true, to_apply=%add | all-reduce | flops 64 | bytes 256
  41.7 1.3 reshape.259
  43.0 8.3 %fusion = (f32[256,2,4]{0,2,1:T(4,128)S(1)}, f32[2,2048,256,4]{2,1,3,0:T(8,128)}) fusion(pred[256,2048]{0,1:T(8,128)(4,1)S(1)} %compare_and_fusion, bf16[256,2,4,128]{3,2,1,0:T(4,128)(2,1)} %reshape.260, bf16[2048,2,128,1]{2,1,0,3:T(2,128)(2,1)S(1)} %bitcast.103), kind=kOutput, calls=%fused_computation.4 | convolution fusion | flops 1086322688 | bytes 18882560 | tf_op jit(solution)/shard_map/tgjd,sgd->tgjs/dot_general | solution.py:122
  51.3 9.7 %all-gather.8.cloned.1.call-done = bf16[32,64,256]{2,1,0:T(8,128)(2,1)} async-done(((bf16[4,64,256]{2,1,0:T(8,128)(2,1)}), bf16[32,64,256]{2,1,0:T(8,128)(2,1)}) %all-gather.8.cloned.1.call-update) | async-done | bytes 1048592 | tf_op jit(solution)/shard_map/all_gather | solution.py:118
  61.0 1.3 reshape.261
  62.4 9.2 %fusion.3 = f32[256,2,4]{0,2,1:T(4,128)S(1)} fusion(f32[2,2048,256,4]{2,1,3,0:T(8,128)} %get-tuple-element.65, f32[256,2,4]{0,2,1:T(4,128)S(1)} %broadcast_maximum_fusion, pred[256,2048]{0,1:T(8,128)(4,1)S(1)} %compare_and_fusion), kind=kLoop, calls=%fused_computation.7 | loop fusion | flops 16775168 | bytes 17317888 | tf_op jit(solution)/shard_map/reduce_sum | solution.py:128
  71.5 7.8 %divide_convert_fusion = bf16[256,2,4,128]{0,3,2,1:T(8,128)(2,1)S(1)} fusion(f32[2,2048,256,4]{2,1,3,0:T(8,128)} %get-tuple-element.65, f32[256,2,4]{0,2,1:T(4,128)S(1)} %broadcast_maximum_fusion, pred[256,2048]{0,1:T(8,128)(4,1)S(1)} %compare_and_fusion, bf16[2048,2,128,1]{2,1,0,3:T(2,128)(2,1)S(1)} %bitcast.102, f32[256,2,4]{0,2,1:T(4,128)S(1)} %fusion.3), kind=kOutput, calls=%fused_computation.28 | convolution fusion | flops 1091043328 | bytes 18890752 | tf_op jit(solution)/shard_map/tgjs,sgd->tgjd/dot_general | solution.py:130
  79.3 8.0 %fusion.33 = f32[256,4096]{1,0:T(8,128)} fusion(bf16[256,1024]{0,1:T(8,128)(2,1)S(1)} %bitcast.105, bf16[1024,4096]{1,0:T(8,128)(2,1)} %param.24), kind=kOutput, calls=%fused_computation.57 | convolution fusion | flops 2147483648 | bytes 13107200 | tf_op jit(solution)/shard_map/dot_general | solution.py:166
  87.4 3.4 %all-gather.10.cloned.1.call-done = bf16[64,128,128]{2,1,0:T(8,128)(2,1)} async-done(((bf16[8,128,128]{2,1,0:T(8,128)(2,1)}), bf16[64,128,128]{2,1,0:T(8,128)(2,1)}) %all-gather.10.cloned.1.call-update) | async-done | bytes 2097168 | tf_op jit(solution)/shard_map/all_gather | solution.py:14
  90.9 0.2 while.12
  91.2 0.7 fusion.15
  91.9 8.9 %convolution_add_fusion = f32[256,4096]{1,0:T(8,128)} fusion(f32[256,4096]{1,0:T(8,128)} %fusion.33, bf16[256,1024]{0,1:T(8,128)(2,1)S(1)} %bitcast.101, bf16[1024,4096]{1,0:T(8,128)(2,1)} %param.25), kind=kOutput, calls=%fused_computation.11 | convolution fusion | flops 2148532224 | bytes 17301504 | tf_op jit(solution)/shard_map/dot_general | solution.py:167
  100.9 84.8 %reduce-scatter.2.cloned.1.call-done = f32[64,4096]{1,0:T(8,128)} async-done(((f32[256,4096]{1,0:T(8,128)}), f32[64,4096]{1,0:T(8,128)}) %reduce-scatter.2.cloned.1.call-update) | async-done | bytes 1048592 | tf_op jit(solution)/shard_map/reduce_scatter | solution.py:165
  185.7 2.1 %convert_element_type.103 = bf16[64,4096]{1,0:T(8,128)(2,1)} convert(f32[64,4096]{1,0:T(8,128)} %reduce-scatter.2.cloned.1.call-done) | non-fusion elementwise | flops 262144 | bytes 1572864 | tf_op jit(solution)/shard_map/convert_element_type | solution.py:172
  (35 shorter events, 1.8 us)
Async XLA Ops:
  6.5 11.0 %copy-start = (bf16[256,256]{1,0:T(8,128)(2,1)S(1)}, bf16[256,256]{1,0:T(8,128)(2,1)}, u32[]{:S(2)}) copy-start(bf16[256,256]{1,0:T(8,128)(2,1)} %param.19) | copy-start | bytes 393220
  6.5 18.1 %copy-start.2 = (u32[32]{0:T(128)S(1)}, u32[32]{0:T(128)}, u32[]{:S(2)}) copy-start(u32[32]{0:T(128)} %constant.53) | copy-start | bytes 388
  6.5 35.1 %all-gather.6.cloned.1.call-start = ((), (), s32[]{:S(2)}) async-start(), calls=%async_computation.1 | async-start | bytes 1179648 | tf_op jit(solution)/shard_map/all_gather | solution.py:110
  7.3 53.7 %all-gather.8.cloned.1.call-start = ((), (), s32[]{:S(2)}) async-start(), calls=%async_computation.2 | async-start | bytes 1179648 | tf_op jit(solution)/shard_map/all_gather | solution.py:118
  8.0 82.8 %all-gather.10.cloned.1.call-start = ((), (), s32[]{:S(2)}) async-start(), calls=%async_computation.4 | async-start | bytes 2359296 | tf_op jit(solution)/shard_map/all_gather | solution.py:14
  16.8 169.0 %reduce-scatter.2.cloned.1.call-start = ((), (), s32[]{:S(2)}) async-start(), calls=%async_computation.3 | async-start | bytes 5242880 | tf_op jit(solution)/shard_map/reduce_scatter | solution.py:165
  79.3 11.8 %copy-start.1 = (f32[8]{0:T(128)S(1)}, f32[8]{0:T(128)}, u32[]{:S(2)}) copy-start(f32[8]{0:T(128)} %param.21) | copy-start | bytes 100
Sparse Core Ops, SparseCore 0:
  9.2 26.3 all-gather.5
  37.5 23.4 all-gather.7
  62.9 27.8 all-gather.9
  101.0 84.6 reduce-scatter.1
where the time goes:
time: 195 us; the launch traced here: 194 us
  waiting for transfers between devices  99.4 us (51%)
  matrix products  36.4 us (19%)
  other arithmetic  18.2 us (9%)
  blocking collectives  15.3 us (8%)
  between operations  15.3 us (8%)
  local copies, waits for them, and re-layouts  9.32 us (5%)
    reduce_scatter x1, waiting for transfers between devices, shards(): lax.psum_scatter(jnp.dot(attention_out, attention_weight, preferred_eleme...  84.8 us
    unnamed x1, blocking collectives  15.3 us
    all_gather x1, waiting for transfers between devices, shards(): lax.all_gather(value_pages, 'ctx', axis=0, tiled=True)  9.7 us
    reduce_sum x1, other arithmetic, shards(): new_sum = jnp.sum(weights, axis=3)  9.17 us
    dot_general x1, matrix products, shards(): jnp.dot(mixer_out, mixer_weight, preferred_element_type=jnp.float32)  8.91 us
    dot_general x1, matrix products, shards(): jnp.einsum('tgjd,sgd->tgjs', query_heads, flat_keys, preferred_element_ty...  8.3 us
    dot_general x1, matrix products, shards(): jnp.dot(attention_out, attention_weight, preferred_element_type=jnp.float32)  8.04 us
    dot_general x1, matrix products, shards(): jnp.einsum('tgjs,sgd->tgjd', probabilities, flat_values, preferred_elemen...  7.79 us
  transfers between devices with their start and end apart: 4, of which 3 were waited for; matrix products, arithmetic and copies ran while one was open for 27% of the time, Pallas kernels for 0%

commit v1 on v0

v1 whole, which is shorter than its diff:
```python
import functools

import jax
import jax.numpy as jnp
from jax import lax
from jax.experimental import pallas as pl
from jax.experimental.pallas import tpu as pltpu
from jax.sharding import PartitionSpec as P

HEAD_DIM = 128
SSM_HEAD_DIM = 128
STATE = 128
LOG2E = 1.4426950408889634
LOW = -1e30
F32 = jnp.float32
BF16 = jnp.bfloat16

VMEM_SPEC = pl.BlockSpec(memory_space=pltpu.VMEM)
SMEM_SPEC = pl.BlockSpec(memory_space=pltpu.SMEM)


def doc_ends_of(len_ref):
    ends, total = [], 0
    for i in range(len_ref.shape[0]):
        total = total + len_ref[i]
        ends.append(total)
    return ends


def doc_start(pos, ends):
    start = jnp.zeros_like(pos)
    for end in ends:
        start = jnp.where(pos >= end, end, start)
    return start


def row_slot(part, z):
    d = part ^ z
    return jnp.where(d == 1, 0, jnp.where(d == 3, 1, jnp.where(d == 0, 2, 3)))


def nt(a, b):
    return lax.dot_general(a, b, (((1,), (1,)), ((), ())), preferred_element_type=F32)


def nn(a, b):
    return lax.dot_general(a, b, (((1,), (0,)), ((), ())), preferred_element_type=F32)


def mixer_kernel(len_ref, skip_ref, x_ref, w_ref, r_ref, ld_ref, base_ref, st_ref, eg_ref):
    me = lax.axis_index("ctx")
    heads, rows = ld_ref.shape
    groups = w_ref.shape[1] // STATE
    per_group = heads // groups
    half = heads // 2
    first = me * rows
    ends = doc_ends_of(len_ref)
    ds = ld_ref[...]
    lane = lax.broadcasted_iota(jnp.int32, ds.shape, 1)
    shift = 1
    while shift < rows:
        ds = ds + jnp.where(lane >= shift, pltpu.roll(ds, shift, 1), 0.0)
        shift *= 2
    col = ds.T
    t_pos = first + lax.broadcasted_iota(jnp.int32, (rows, 1), 0)
    t_start = doc_start(t_pos, ends)
    s_pos = first + lax.broadcasted_iota(jnp.int32, (1, rows), 1)
    last = first + rows - 1
    last_start = doc_start(jnp.full((1, 1), last, jnp.int32), ends)
    visible = (s_pos <= t_pos) & (s_pos >= t_start)
    bias = jnp.where(visible, 0.0, LOW)
    eg_ref[...] = jnp.where(t_start < first, jnp.exp(col), 0.0)
    total = ds[:, rows - 1 : rows]
    end_weight = jnp.where(s_pos >= last_start, jnp.exp(total - ds), 0.0)
    gain = jnp.where(last_start < first, jnp.exp(total), 0.0)
    gain = jnp.broadcast_to(gain, (heads, SSM_HEAD_DIM)).astype(BF16)
    pad = jnp.zeros((st_ref.shape[1] - half * STATE - half, SSM_HEAD_DIM), BF16)
    for c in range(2):
        st_ref[c, half * STATE :, :] = jnp.concatenate(
            [gain[c * half : (c + 1) * half].astype(F32), pad.astype(F32)], axis=0
        ).astype(BF16)
    for g in range(groups):
        cols = slice(g * STATE, (g + 1) * STATE)
        write, read = w_ref[:, cols], r_ref[:, cols]
        inner = nt(read, write)
        write_t = write.astype(F32).T
        for h in range(g * per_group, (g + 1) * per_group):
            hc = slice(h * SSM_HEAD_DIM, (h + 1) * SSM_HEAD_DIM)
            x = x_ref[:, hc]
            decay = jnp.exp((col[:, h : h + 1] - ds[h : h + 1, :]) + bias)
            mixing = (decay * inner).astype(BF16)
            base_ref[:, hc] = nn(mixing, x) + skip_ref[h] * x.astype(F32)
            end_write = (write_t * end_weight[h : h + 1, :]).astype(BF16)
            c, i = divmod(h, half)
            st_ref[c, i * STATE : (i + 1) * STATE, :] = nn(end_write, x).astype(BF16)


def mixer_local(doc_lengths, skip_gain, x, w, r, ld):
    heads, rows = ld.shape
    half = heads // 2
    return pl.pallas_call(
        mixer_kernel,
        out_shape=(
            jax.ShapeDtypeStruct(x.shape, F32),
            jax.ShapeDtypeStruct((2, half * STATE + 16, SSM_HEAD_DIM), BF16),
            jax.ShapeDtypeStruct((rows, heads), F32),
        ),
        in_specs=[SMEM_SPEC, SMEM_SPEC] + [VMEM_SPEC] * 4,
        out_specs=(VMEM_SPEC,) * 3,
        compiler_params=pltpu.CompilerParams(vmem_limit_bytes=24 << 20),
        cost_estimate=pl.CostEstimate(
            flops=2 * heads * rows * rows * 128 * 2,
            bytes_accessed=4 << 20,
            transcendentals=heads * rows * rows,
        ),
        name="mixer_local",
    )(doc_lengths, skip_gain, x, w, r, ld)


def compose_kernel(mine_ref, other_ref, out_ref):
    core = lax.axis_index("ctx") & 1
    state_rows = out_ref.shape[0] - 16
    half = state_rows // STATE
    a, b = mine_ref[core].astype(F32), other_ref[core].astype(F32)
    first = jnp.where(core == 0, a, b)
    second = jnp.where(core == 0, b, a)
    for i in range(half):
        rows = slice(i * STATE, (i + 1) * STATE)
        gain = second[state_rows + i : state_rows + i + 1]
        out_ref[rows, :] = (gain * first[rows] + second[rows]).astype(BF16)
    out_ref[state_rows:, :] = (first[state_rows:] * second[state_rows:]).astype(BF16)


def compose(mine, other):
    return pl.pallas_call(
        compose_kernel,
        out_shape=jax.ShapeDtypeStruct(mine.shape[1:], BF16),
        in_specs=[VMEM_SPEC] * 2,
        out_specs=VMEM_SPEC,
        cost_estimate=pl.CostEstimate(flops=1 << 17, bytes_accessed=1 << 20, transcendentals=0),
        name="compose",
    )(mine, other)


def carry_kernel(*refs):
    *got, out_ref, held = refs
    chip = lax.axis_index("ctx") // 2
    for j, ref in enumerate(got, 1):
        held[chip ^ j] = ref[...]
    state_rows = out_ref.shape[0]
    half = state_rows // STATE
    out_ref[...] = jnp.zeros_like(out_ref)

    def one(k, carry):
        gains = held[k, state_rows:, :].astype(F32)
        new = []
        for i in range(half):
            term = held[k, i * STATE : (i + 1) * STATE, :].astype(F32)
            new.append(gains[i : i + 1] * carry[i] + term)
        return tuple(new)

    zero = tuple(jnp.zeros((STATE, SSM_HEAD_DIM), F32) for _ in range(half))
    carry = lax.fori_loop(0, chip, one, zero)
    for i in range(half):
        out_ref[i * STATE : (i + 1) * STATE, :] = carry[i].astype(BF16)


def carry_in(got):
    rows = got[0].shape[0]
    return pl.pallas_call(
        carry_kernel,
        out_shape=jax.ShapeDtypeStruct((rows - 16, SSM_HEAD_DIM), BF16),
        in_specs=[VMEM_SPEC] * len(got),
        out_specs=VMEM_SPEC,
        scratch_shapes=[pltpu.VMEM((len(got) + 1, rows, SSM_HEAD_DIM), BF16)],
        cost_estimate=pl.CostEstimate(flops=1 << 18, bytes_accessed=1 << 20, transcendentals=0),
        name="carry_in",
    )(*got)


def finish_kernel(base_ref, r_ref, eg_ref, mine_ref, other_ref, st_ref, out_ref):
    core = lax.axis_index("ctx") & 1
    z = lax.axis_index("tp")
    rows = base_ref.shape[0]
    part = rows // 4
    half = mine_ref.shape[0] // STATE
    groups = r_ref.shape[1] // STATE
    heads = 2 * half
    per_group = heads // groups
    state_rows = half * STATE
    for h in range(heads):
        c, i = divmod(h, half)
        g = h // per_group
        hs = slice(i * STATE, (i + 1) * STATE)
        a, b = mine_ref[hs, :].astype(F32), other_ref[hs, :].astype(F32)
        entering = jnp.where(core == c, a, b)
        prev = st_ref[c, hs, :].astype(F32)
        gain = st_ref[c, state_rows + i : state_rows + i + 1, :].astype(F32)
        carry = jnp.where(core == 1, gain * entering + prev, entering).astype(BF16)
        hc = slice(h * SSM_HEAD_DIM, (h + 1) * SSM_HEAD_DIM)
        inter = nn(r_ref[:, g * STATE : (g + 1) * STATE], carry)
        res = (base_ref[:, hc] + eg_ref[:, h : h + 1] * inter).astype(BF16)
        for q in range(4):
            at = pl.multiple_of(row_slot(q, z) * part, part)
            out_ref[pl.ds(at, part), hc] = res[q * part : (q + 1) * part]


def finish(base, r, eg, mine, other, st_other):
    return pl.pallas_call(
        finish_kernel,
        out_shape=jax.ShapeDtypeStruct(base.shape, BF16),
        in_specs=[VMEM_SPEC] * 6,
        out_specs=VMEM_SPEC,
        cost_estimate=pl.CostEstimate(
            flops=2 * base.size * STATE, bytes_accessed=2 << 20, transcendentals=0
        ),
        name="finish",
    )(base, r, eg, mine, other, st_other)


def attention_kernel(page_len, len_ref, table_ref, q_ref, *refs):
    *got, out_ref, inv, ks, vs, sc, mx, ls, acc = refs
    me = lax.axis_index("ctx")
    z = lax.axis_index("tp")
    rows = q_ref.shape[0]
    part = rows // 4
    heads = q_ref.shape[1] // HEAD_DIM
    kv_heads = ks.shape[1] // HEAD_DIM
    group = heads // kv_heads
    first = me * rows
    ends = doc_ends_of(len_ref)
    start0 = 0
    for end in ends:
        start0 = jnp.where(first >= end, end, start0)
    low_block = start0 // rows
    pages_block = rows // page_len

    def invert(l, _):
        inv[table_ref[l]] = l
        return 0

    lax.fori_loop(0, table_ref.shape[0], invert, 0)
    low_page, high_page = low_block * pages_block, (me + 1) * pages_block
    for j, ref in enumerate(got):
        for slot in range(ref.shape[1] // page_len):
            page = inv[(me ^ j) * (ref.shape[1] // page_len) + slot]

            @pl.when((page >= low_page) & (page < high_page))
            def _():
                at = pl.ds(pl.multiple_of(page * page_len, page_len), page_len)
                here = slice(slot * page_len, (slot + 1) * page_len)
                ks[at, :] = ref[0, here, :]
                vs[at, :] = ref[1, here, :]

    t_pos = first + lax.broadcasted_iota(jnp.int32, (rows, 1), 0)
    t_start = doc_start(t_pos, ends)
    scale = LOG2E * HEAD_DIM ** (-0.5)

    def scores(block, own):
        at = pl.ds(pl.multiple_of(block * rows, rows), rows)
        u_pos = block * rows + lax.broadcasted_iota(jnp.int32, (1, rows), 1)
        shown = u_pos >= t_start
        if own:
            shown = shown & (u_pos <= t_pos)
        for h in range(heads):
            g = h // group
            s = nt(
                q_ref[:, h * HEAD_DIM : (h + 1) * HEAD_DIM],
                ks[at, g * HEAD_DIM : (g + 1) * HEAD_DIM],
            )
            s = jnp.where(shown, s * scale, LOW)
            sc[block - low_block, h] = s
            top = s[:, :128]
            for k in range(128, rows, 128):
                top = jnp.maximum(top, s[:, k : k + 128])
            mx[h] = top if own else jnp.maximum(mx[h], top)

    scores(me, True)

    def earlier(block, _):
        scores(block, False)
        return 0

    lax.fori_loop(low_block, me, earlier, 0)
    for h in range(heads):
        mx[h] = jnp.broadcast_to(jnp.max(mx[h], axis=1, keepdims=True), (rows, 128))
    ls[...] = jnp.zeros_like(ls)
    acc[...] = jnp.zeros_like(acc)

    def weigh(block, _):
        at = pl.ds(pl.multiple_of(block * rows, rows), rows)
        for h in range(heads):
            g = h // group
            m = mx[h]
            total = ls[h]
            pieces = []
            for k in range(0, rows, 128):
                w = jnp.exp2(sc[block - low_block, h, :, k : k + 128] - m)
                total = total + w
                pieces.append(w.astype(BF16))
            ls[h] = total
            acc[h] += nn(
                jnp.concatenate(pieces, axis=1), vs[at, g * HEAD_DIM : (g + 1) * HEAD_DIM]
            )
        return 0

    lax.fori_loop(low_block, me + 1, weigh, 0)
    for h in range(heads):
        res = (acc[h] / jnp.sum(ls[h], axis=1, keepdims=True)).astype(BF16)
        for q in range(4):
            at = pl.multiple_of(row_slot(q, z) * part, part)
            out_ref[pl.ds(at, part), h * HEAD_DIM : (h + 1) * HEAD_DIM] = res[
                q * part : (q + 1) * part
            ]


def attention(page_len, doc_lengths, page_table, queries, got):
    rows = queries.shape[0]
    heads = queries.shape[1] // HEAD_DIM
    keys = len(got) * got[0].shape[1]
    width = got[0].shape[2]
    blocks = min(keys // rows, keys // 2 // rows + 1)
    return pl.pallas_call(
        functools.partial(attention_kernel, page_len),
        out_shape=jax.ShapeDtypeStruct(queries.shape, BF16),
        in_specs=[SMEM_SPEC, SMEM_SPEC, VMEM_SPEC] + [VMEM_SPEC] * len(got),
        out_specs=VMEM_SPEC,
        scratch_shapes=[
            pltpu.SMEM((page_table.shape[0],), jnp.int32),
            pltpu.VMEM((keys, width), BF16),
            pltpu.VMEM((keys, width), BF16),
            pltpu.VMEM((blocks, heads, rows, rows), F32),
            pltpu.VMEM((heads, rows, 128), F32),
            pltpu.VMEM((heads, rows, 128), F32),
            pltpu.VMEM((heads, rows, HEAD_DIM), F32),
        ],
        compiler_params=pltpu.CompilerParams(vmem_limit_bytes=60 << 20),
        cost_estimate=pl.CostEstimate(
            flops=4 * heads * rows * 1280 * 128,
            bytes_accessed=4 << 20,
            transcendentals=heads * rows * 1280,
        ),
        name="attention",
    )(doc_lengths, page_table, queries, *got)


def project_kernel(att_ref, mix_ref, wa_ref, wm_ref, send_ref, keep_ref):
    sent = send_ref.shape[0]
    total = nn(att_ref[...], wa_ref[...]) + nn(mix_ref[...], wm_ref[...])
    send_ref[...] = total[:sent].astype(BF16)
    keep_ref[...] = total[sent:]


def project(att, mix, wa, wm, start, width, tile):
    rows, depth = att.shape
    base = start // tile
    whole = pl.BlockSpec((rows, depth), lambda j: (0, 0))
    weight = pl.BlockSpec((depth, tile), lambda j: (0, base + j))
    out = pl.BlockSpec((rows // 2, tile), lambda j: (0, j))
    return pl.pallas_call(
        project_kernel,
        grid=(width // tile,),
        out_shape=(
            jax.ShapeDtypeStruct((rows // 2, width), BF16),
            jax.ShapeDtypeStruct((rows // 2, width), F32),
        ),
        in_specs=[whole, whole, weight, weight],
        out_specs=(out, out),
        compiler_params=pltpu.CompilerParams(vmem_limit_bytes=24 << 20),
        cost_estimate=pl.CostEstimate(
            flops=4 * rows * depth * width,
            bytes_accessed=4 * depth * width + 4 * rows * depth + 4 * rows * width,
            transcendentals=0,
        ),
        name="project",
    )(att, mix, wa, wm)


def shards(
    n_ctx,
    n_tp,
    queries,
    key_pages,
    value_pages,
    mixer_input,
    state_write,
    state_read,
    log_decay,
    skip_gain,
    doc_lengths,
    page_table,
    attention_weight,
    mixer_weight,
):
    tok_rows = queries.shape[0]
    page_len = key_pages.shape[1]
    chips = n_ctx // 2

    def between_chips(a, j):
        return lax.ppermute(a, "ctx", [(i, i ^ (2 * j)) for i in range(n_ctx)])

    def other_core(a):
        return lax.ppermute(a, "ctx", [(i, i ^ 1) for i in range(n_ctx)])

    width = key_pages.shape[2]
    kv = jnp.stack([key_pages.reshape(-1, width), value_pages.reshape(-1, width)])
    far = [kv] + [between_chips(kv, j) for j in range(1, chips)]

    base, st, eg = mixer_local(
        doc_lengths, skip_gain, mixer_input, state_write, state_read, log_decay
    )
    st_other = other_core(st)
    chip_state = compose(st, st_other)
    got_states = [between_chips(chip_state, j) for j in range(1, chips)]

    got = []
    for a in far:
        got += [a, other_core(a)]
    att = attention(page_len, doc_lengths, page_table, queries, got)

    entering = carry_in(got_states)
    mix = finish(base, state_read, eg, entering, other_core(entering), st_other)

    part = tok_rows // n_tp
    columns = attention_weight.shape[1]
    chunk = columns // 4
    pieces = []
    for start in range(0, columns, chunk):
        send, keep = project(att, mix, attention_weight, mixer_weight, start, chunk, 512)
        near = lax.ppermute(send, "tp", [(i, i ^ 1) for i in range(n_tp)])
        both = keep + near.astype(F32)
        last = lax.ppermute(both[part:].astype(BF16), "tp", [(i, i ^ 2) for i in range(n_tp)])
        pieces.append((both[:part] + last.astype(F32)).astype(BF16))
    return jnp.concatenate(pieces, axis=1)


def solution(mesh):
    placed = (
        P("ctx", "tp"),
        P("ctx", None, "tp"),
        P("ctx", None, "tp"),
        P("ctx", "tp"),
        P("ctx", "tp"),
        P("ctx", "tp"),
        P("tp", "ctx"),
        P("tp"),
        P(),
        P(),
        P("tp", None),
        P("tp", None),
    )
    return jax.shard_map(
        functools.partial(shards, mesh.shape["ctx"], mesh.shape["tp"]),
        mesh=mesh,
        in_specs=placed,
        out_specs=P(("ctx", "tp"), None),
        check_vma=False,
    )
```

time: 195 us -> 106 us (0.54)
  waiting for transfers between devices: 99.4 us -> 40.9 us
  matrix products: 36.4 us -> 0 us
  starting transfers between devices: 0.12 us -> 21.9 us
  Pallas kernels: 0 us -> 20.5 us
  other arithmetic: 18.2 us -> 2.19 us
  blocking collectives: 15.3 us -> 0 us
  between operations: 15.3 us -> 0.27 us
  local copies, waits for them, and re-layouts: 9.32 us -> 18.9 us
    reduce_scatter x1 -> x0, waiting for transfers between devices: 84.8 us -> none  [shards(): lax.psum_scatter(jnp.dot(attention_out, attention_weight, preferred_eleme...]
    ppermute x0 -> x20, waiting for transfers between devices: none -> 40.9 us  [the longest x4 15.4 us: shards(): near = lax.ppermute(send, 'tp', [(i, i ^ 1) for i in range(n_tp)])]
    dot_general x8 -> x0, matrix products: 36.4 us -> none  [the longest x1 8.91 us: shards(): jnp.dot(mixer_out, mixer_weight, preferred_element_type=jnp.float32)]
    ppermute x0 -> x20, starting transfers between devices: none -> 21.9 us  [the longest x6 9.15 us: between_chips(): return lax.ppermute(a, 'ctx', [(i, i ^ 2 * j) for i in range(n_ctx)])]
    pallas_call x0 -> x9, Pallas kernels: none -> 20.5 us  [the longest x4 7.33 us: project(): pl.pallas_call(project_kernel, grid=(width // tile,), out_shape=(jax.Shap...]
    unnamed x10 -> x52, local copies, waits for them, and re-layouts: 2.17 us -> 18.8 us
    unnamed x1 -> x0, blocking collectives: 15.3 us -> none
    all_gather x3 -> x0, waiting for transfers between devices: 13.1 us -> none  [the longest x1 9.7 us: shards(): lax.all_gather(value_pages, 'ctx', axis=0, tiled=True)]
  transfers between devices with their start and end apart: 4 -> 20, of which waited for: 3 -> 9; matrix products, arithmetic and copies ran while one was open for 27% -> 1% of each run, Pallas kernels for 0% -> 13%
where the time goes in v1:
time: 106 us; the launch traced here: 105 us
  waiting for transfers between devices  40.9 us (39%)
  starting transfers between devices  21.9 us (21%)
  Pallas kernels  20.5 us (19%)
  local copies, waits for them, and re-layouts  18.9 us (18%)
  other arithmetic  2.19 us (2%)
    unnamed x52, local copies, waits for them, and re-layouts  18.8 us
    ppermute x4, waiting for transfers between devices, shards(): near = lax.ppermute(send, 'tp', [(i, i ^ 1) for i in range(n_tp)])  15.4 us
    ppermute x6, waiting for transfers between devices, between_chips(): return lax.ppermute(a, 'ctx', [(i, i ^ 2 * j) for i in range(n_ctx)])  13.6 us
    ppermute x4, waiting for transfers between devices, shards(): lax.ppermute(both[part:].astype(BF16), 'tp', [(i, i ^ 2) for i in range(n...  11.9 us
    ppermute x6, starting transfers between devices, between_chips(): return lax.ppermute(a, 'ctx', [(i, i ^ 2 * j) for i in range(n_ctx)])  9.15 us
    ppermute x4, starting transfers between devices, shards(): lax.ppermute(both[part:].astype(BF16), 'tp', [(i, i ^ 2) for i in range(n...  7.5 us
    pallas_call x4, Pallas kernels, project(): pl.pallas_call(project_kernel, grid=(width // tile,), out_shape=(jax.Shap...  7.33 us
    pallas_call x1, Pallas kernels, attention(): pl.pallas_call(functools.partial(attention_kernel, page_len), out_shape=j...  4.82 us
  transfers between devices with their start and end apart: 20, of which 9 were waited for; matrix products, arithmetic and copies ran while one was open for 1% of the time, Pallas kernels for 13%

profile of v1, /device:TPU:0, one launch (start us, length us, event | category | flops | bytes accessed | tf_op | source)
XLA Modules:
  0.0 104.6 jit_solution(8225560239688669446)
XLA Ops:
  4.9 2.1 %mixer_local.1 = (f32[256,1024]{1,0:T(8,128)S(1)}, bf16[2,528,128]{2,1,0:T(8,128)(2,1)S(1)}, f32[256,8]{1,0:T(8,128)S(1)}) custom-call(s32[4]{0:T(128)S(1)} %copy-done.12, f32[8]{0:T(128)S(1)} %copy-done.11, bf16[256,1024]{1,0:T(8,128)(2,1)S(1)} %copy-done.8, bf16[256,256]{1,0:T(8,128)(2,1)S(1)} %copy-done.9, bf16[256,256]{1,0:T(8,128)(2,1)S(1)} %copy-done.6, ...), custom_call_target="tpu_custom_call" | custom-call | flops 268435456 | bytes 4194304 | tf_op jit(solution)/shard_map/mixer_local/pallas_call | solution.py:101
  10.1 2.7 %collective-permute-start.1 = (bf16[2,256,256]{2,1,0:T(8,128)(2,1)S(1)}, bf16[2,256,256]{2,1,0:T(8,128)(2,1)S(1)}, u32[]{:S(2)}, u32[]{:S(2)}) collective-permute-start(bf16[2,256,256]{2,1,0:T(8,128)(2,1)S(1)} %pad_maximum_fusion.1.refs_0_), channel_id=1, source_target_pairs={{0,8},{4,12},{8,0},{12,4},{16,24},{20,28},{24,16},{28,20},{1,9},{5... | collective-permute-start | bytes 786440 | tf_op jit(solution)/shard_map/ppermute | solution.py:400
  12.8 1.5 %collective-permute-start.3 = (bf16[2,256,256]{2,1,0:T(8,128)(2,1)S(1)}, bf16[2,256,256]{2,1,0:T(8,128)(2,1)S(1)}, u32[]{:S(2)}, u32[]{:S(2)}) collective-permute-start(bf16[2,256,256]{2,1,0:T(8,128)(2,1)S(1)} %pad_maximum_fusion.1.refs_0_), channel_id=1, source_target_pairs={{0,16},{4,20},{8,24},{12,28},{16,0},{20,4},{24,8},{28,12},{1,17},{... | collective-permute-start | bytes 786440 | tf_op jit(solution)/shard_map/ppermute | solution.py:400
  15.0 1.7 %compose.1 = bf16[528,128]{1,0:T(8,128)(2,1)} custom-call(bf16[2,528,128]{2,1,0:T(8,128)(2,1)} %copy-done.5, bf16[2,528,128]{2,1,0:T(8,128)(2,1)} %copy-done.13), custom_call_target="tpu_custom_call" | custom-call | flops 131072 | bytes 1048576 | tf_op jit(solution)/shard_map/compose/pallas_call | solution.py:135
  16.7 1.9 %collective-permute-start.8 = (bf16[528,128]{1,0:T(8,128)(2,1)}, bf16[528,128]{1,0:T(8,128)(2,1)S(1)}, u32[]{:S(2)}, u32[]{:S(2)}) collective-permute-start(bf16[528,128]{1,0:T(8,128)(2,1)} %compose.1), channel_id=1, source_target_pairs={{0,8},{4,12},{8,0},{12,4},{16,24},{20,28},{24,16},{28,20},{1,9},{5... | collective-permute-start | bytes 405512 | tf_op jit(solution)/shard_map/ppermute | solution.py:400
  18.7 1.5 %collective-permute-start.9 = (bf16[528,128]{1,0:T(8,128)(2,1)}, bf16[528,128]{1,0:T(8,128)(2,1)S(1)}, u32[]{:S(2)}, u32[]{:S(2)}) collective-permute-start(bf16[528,128]{1,0:T(8,128)(2,1)} %compose.1), channel_id=1, source_target_pairs={{0,16},{4,20},{8,24},{12,28},{16,0},{20,4},{24,8},{28,12},{1,17},{... | collective-permute-start | bytes 405512 | tf_op jit(solution)/shard_map/ppermute | solution.py:400
  20.2 7.0 %collective-permute-done.3.refs_4_ = bf16[2,256,256]{2,1,0:T(8,128)(2,1)S(1)} collective-permute-done((bf16[2,256,256]{2,1,0:T(8,128)(2,1)S(1)}, bf16[2,256,256]{2,1,0:T(8,128)(2,1)S(1)}, u32[]{:S(2)}, u32[]{:S(2)}) %collective-permute-start.3) | collective-permute-done | bytes 262176 | tf_op jit(solution)/shard_map/ppermute | solution.py:400
  28.2 1.4 %collective-permute-done.9.refs_1_ = bf16[528,128]{1,0:T(8,128)(2,1)S(1)} collective-permute-done((bf16[528,128]{1,0:T(8,128)(2,1)}, bf16[528,128]{1,0:T(8,128)(2,1)S(1)}, u32[]{:S(2)}, u32[]{:S(2)}) %collective-permute-start.9) | collective-permute-done | bytes 135200 | tf_op jit(solution)/shard_map/ppermute | solution.py:400
  29.6 1.5 %collective-permute-start.10 = (bf16[528,128]{1,0:T(8,128)(2,1)}, bf16[528,128]{1,0:T(8,128)(2,1)S(1)}, u32[]{:S(2)}, u32[]{:S(2)}) collective-permute-start(bf16[528,128]{1,0:T(8,128)(2,1)} %compose.1), channel_id=1, source_target_pairs={{0,24},{4,28},{8,16},{12,20},{16,8},{20,12},{24,0},{28,4},{1,25},{... | collective-permute-start | bytes 405512 | tf_op jit(solution)/shard_map/ppermute | solution.py:400
  31.1 4.8 %collective-permute-done.10.refs_2_ = bf16[528,128]{1,0:T(8,128)(2,1)S(1)} collective-permute-done((bf16[528,128]{1,0:T(8,128)(2,1)}, bf16[528,128]{1,0:T(8,128)(2,1)S(1)}, u32[]{:S(2)}, u32[]{:S(2)}) %collective-permute-start.10) | collective-permute-done | bytes 135200 | tf_op jit(solution)/shard_map/ppermute | solution.py:400
  36.5 1.8 %carry_in.1.mine_ref = bf16[512,128]{1,0:T(8,128)(2,1)} custom-call(bf16[528,128]{1,0:T(8,128)(2,1)} %copy-done.15, bf16[528,128]{1,0:T(8,128)(2,1)} %copy-done.16, bf16[528,128]{1,0:T(8,128)(2,1)} %copy-done.17), custom_call_target="tpu_custom_call" | custom-call | flops 262144 | bytes 1048576 | tf_op jit(solution)/shard_map/carry_in/pallas_call | solution.py:170
  39.9 4.8 %attention.1.att_ref = bf16[256,1024]{1,0:T(8,128)(2,1)} custom-call(s32[4]{0:T(128)} %len_ref.3, s32[32]{0:T(128)} %table_ref.1, bf16[256,1024]{1,0:T(8,128)(2,1)} %q_ref.1, bf16[2,256,256]{2,1,0:T(8,128)(2,1)} %copy-done.14, bf16[2,256,256]{2,1,0:T(8,128)(2,1)} %copy-done.22, bf16[2,256,256]{2,1,0:T(8,128)(2,1)} %copy-done.19, ...), custom_call_target="tpu_custom_call" | custom-call | flops 1342177280 | bytes 4194304 | tf_op jit(solution)/shard_map/attention/pallas_call | solution.py:323
  45.4 2.7 %finish.1.mix_ref = bf16[256,1024]{1,0:T(8,128)(2,1)} custom-call(f32[256,1024]{1,0:T(8,128)} %copy-done.4, bf16[256,256]{1,0:T(8,128)(2,1)} %r_ref.3, f32[256,8]{1,0:T(8,128)} %copy-done.7, bf16[512,128]{1,0:T(8,128)(2,1)} %carry_in.1.mine_ref, bf16[512,128]{1,0:T(8,128)(2,1)} %copy-done.18, bf16[2,528,128]{2,1,0:T(8,128)(2,1)} %copy-done.13), custom_call_target="tpu_custom_call" | custom-call | flops 67108864 | bytes 2097152 | tf_op jit(solution)/shard_map/finish/pallas_call | solution.py:209
  48.0 3.4 %copy-done = bf16[1024,4096]{1,0:T(8,128)(2,1)S(1)} copy-done((bf16[1024,4096]{1,0:T(8,128)(2,1)S(1)}, bf16[1024,4096]{1,0:T(8,128)(2,1)}, u32[]{:S(2)}) %copy-start) | copy-done | bytes 8388632
  51.4 3.4 %copy-done.1 = bf16[1024,4096]{1,0:T(8,128)(2,1)S(1)} copy-done((bf16[1024,4096]{1,0:T(8,128)(2,1)S(1)}, bf16[1024,4096]{1,0:T(8,128)(2,1)}, u32[]{:S(2)}) %copy-start.1) | copy-done | bytes 8388632
  54.8 1.0 copy-done.2
  55.9 1.0 copy-done.3
  56.9 1.8 %project.7 = (bf16[128,1024]{1,0:T(8,128)(2,1)S(1)}, f32[128,1024]{1,0:T(8,128)S(1)}) custom-call(bf16[256,1024]{1,0:T(8,128)(2,1)S(1)} %copy-done.3, bf16[256,1024]{1,0:T(8,128)(2,1)S(1)} %copy-done.2, bf16[1024,4096]{1,0:T(8,128)(2,1)S(1)} %copy-done, bf16[1024,4096]{1,0:T(8,128)(2,1)S(1)} %copy-done.1), custom_call_target="tpu_custom_call" | custom-call | flops 1073741824 | bytes 6291456 | tf_op jit(solution)/shard_map/project/pallas_call | solution.py:360
  58.7 1.6 %collective-permute-start.18 = (bf16[128,1024]{1,0:T(8,128)(2,1)S(1)}, bf16[128,1024]{1,0:T(8,128)(2,1)S(1)}, u32[]{:S(2)}, u32[]{:S(2)}) collective-permute-start(bf16[128,1024]{1,0:T(8,128)(2,1)S(1)} %get-tuple-element.26), channel_id=1, source_target_pairs={{0,1},{1,0},{2,3},{3,2},{4,5},{5,4},{6,7},{7,6},{8,9},{9,8},{10,11... | collective-permute-start | bytes 786440 | tf_op jit(solution)/shard_map/ppermute | solution.py:430
  60.4 1.8 %project.6 = (bf16[128,1024]{1,0:T(8,128)(2,1)S(1)}, f32[128,1024]{1,0:T(8,128)S(1)}) custom-call(bf16[256,1024]{1,0:T(8,128)(2,1)S(1)} %copy-done.3, bf16[256,1024]{1,0:T(8,128)(2,1)S(1)} %copy-done.2, bf16[1024,4096]{1,0:T(8,128)(2,1)S(1)} %copy-done, bf16[1024,4096]{1,0:T(8,128)(2,1)S(1)} %copy-done.1), custom_call_target="tpu_custom_call" | custom-call | flops 1073741824 | bytes 6291456 | tf_op jit(solution)/shard_map/project/pallas_call | solution.py:360
  62.7 1.8 %project.5 = (bf16[128,1024]{1,0:T(8,128)(2,1)S(1)}, f32[128,1024]{1,0:T(8,128)S(1)}) custom-call(bf16[256,1024]{1,0:T(8,128)(2,1)S(1)} %copy-done.3, bf16[256,1024]{1,0:T(8,128)(2,1)S(1)} %copy-done.2, bf16[1024,4096]{1,0:T(8,128)(2,1)S(1)} %copy-done, bf16[1024,4096]{1,0:T(8,128)(2,1)S(1)} %copy-done.1), custom_call_target="tpu_custom_call" | custom-call | flops 1073741824 | bytes 6291456 | tf_op jit(solution)/shard_map/project/pallas_call | solution.py:360
  64.6 1.8 %project.4 = (bf16[128,1024]{1,0:T(8,128)(2,1)S(1)}, f32[128,1024]{1,0:T(8,128)S(1)}) custom-call(bf16[256,1024]{1,0:T(8,128)(2,1)S(1)} %copy-done.3, bf16[256,1024]{1,0:T(8,128)(2,1)S(1)} %copy-done.2, bf16[1024,4096]{1,0:T(8,128)(2,1)S(1)} %copy-done, bf16[1024,4096]{1,0:T(8,128)(2,1)S(1)} %copy-done.1), custom_call_target="tpu_custom_call" | custom-call | flops 1073741824 | bytes 6291456 | tf_op jit(solution)/shard_map/project/pallas_call | solution.py:360
  66.4 1.6 %collective-permute-start.14 = (bf16[128,1024]{1,0:T(8,128)(2,1)S(1)}, bf16[128,1024]{1,0:T(8,128)(2,1)S(1)}, u32[]{:S(2)}, u32[]{:S(2)}) collective-permute-start(bf16[128,1024]{1,0:T(8,128)(2,1)S(1)} %get-tuple-element.22), channel_id=1, source_target_pairs={{0,1},{1,0},{2,3},{3,2},{4,5},{5,4},{6,7},{7,6},{8,9},{9,8},{10,11... | collective-permute-start | bytes 786440 | tf_op jit(solution)/shard_map/ppermute | solution.py:430
  68.6 2.7 %collective-permute-start.19 = (bf16[64,1024]{1,0:T(8,128)(2,1)S(1)}, bf16[64,1024]{1,0:T(8,128)(2,1)S(1)}, u32[]{:S(2)}, u32[]{:S(2)}) collective-permute-start(bf16[64,1024]{1,0:T(8,128)(2,1)S(1)} %slice.60), channel_id=1, source_target_pairs={{0,2},{1,3},{2,0},{3,1},{4,6},{5,7},{6,4},{7,5},{8,10},{9,11},{10,... | collective-permute-start | bytes 393224 | tf_op jit(solution)/shard_map/ppermute | solution.py:432
  71.3 4.7 %collective-permute-done.16 = bf16[128,1024]{1,0:T(8,128)(2,1)S(1)} collective-permute-done((bf16[128,1024]{1,0:T(8,128)(2,1)S(1)}, bf16[128,1024]{1,0:T(8,128)(2,1)S(1)}, u32[]{:S(2)}, u32[]{:S(2)}) %collective-permute-start.16) | collective-permute-done | bytes 262176 | tf_op jit(solution)/shard_map/ppermute | solution.py:430
  76.0 1.6 %collective-permute-start.17 = (bf16[64,1024]{1,0:T(8,128)(2,1)S(1)}, bf16[64,1024]{1,0:T(8,128)(2,1)S(1)}, u32[]{:S(2)}, u32[]{:S(2)}) collective-permute-start(bf16[64,1024]{1,0:T(8,128)(2,1)S(1)} %slice.61), channel_id=1, source_target_pairs={{0,2},{1,3},{2,0},{3,1},{4,6},{5,7},{6,4},{7,5},{8,10},{9,11},{10,... | collective-permute-start | bytes 393224 | tf_op jit(solution)/shard_map/ppermute | solution.py:432
  77.6 6.8 %collective-permute-done.14 = bf16[128,1024]{1,0:T(8,128)(2,1)S(1)} collective-permute-done((bf16[128,1024]{1,0:T(8,128)(2,1)S(1)}, bf16[128,1024]{1,0:T(8,128)(2,1)S(1)}, u32[]{:S(2)}, u32[]{:S(2)}) %collective-permute-start.14) | collective-permute-done | bytes 262176 | tf_op jit(solution)/shard_map/ppermute | solution.py:430
  84.5 1.7 %collective-permute-start.15 = (bf16[64,1024]{1,0:T(8,128)(2,1)S(1)}, bf16[64,1024]{1,0:T(8,128)(2,1)S(1)}, u32[]{:S(2)}, u32[]{:S(2)}) collective-permute-start(bf16[64,1024]{1,0:T(8,128)(2,1)S(1)} %slice.62), channel_id=1, source_target_pairs={{0,2},{1,3},{2,0},{3,1},{4,6},{5,7},{6,4},{7,5},{8,10},{9,11},{10,... | collective-permute-start | bytes 393224 | tf_op jit(solution)/shard_map/ppermute | solution.py:432
  86.2 3.9 %collective-permute-done.12 = bf16[128,1024]{1,0:T(8,128)(2,1)S(1)} collective-permute-done((bf16[128,1024]{1,0:T(8,128)(2,1)S(1)}, bf16[128,1024]{1,0:T(8,128)(2,1)S(1)}, u32[]{:S(2)}, u32[]{:S(2)}) %collective-permute-start.12) | collective-permute-done | bytes 262176 | tf_op jit(solution)/shard_map/ppermute | solution.py:430
  90.2 1.5 %collective-permute-start.13 = (bf16[64,1024]{1,0:T(8,128)(2,1)S(1)}, bf16[64,1024]{1,0:T(8,128)(2,1)S(1)}, u32[]{:S(2)}, u32[]{:S(2)}) collective-permute-start(bf16[64,1024]{1,0:T(8,128)(2,1)S(1)} %slice.63), channel_id=1, source_target_pairs={{0,2},{1,3},{2,0},{3,1},{4,6},{5,7},{6,4},{7,5},{8,10},{9,11},{10,... | collective-permute-start | bytes 393224 | tf_op jit(solution)/shard_map/ppermute | solution.py:432
  91.8 9.1 %collective-permute-done.15 = bf16[64,1024]{1,0:T(8,128)(2,1)S(1)} collective-permute-done((bf16[64,1024]{1,0:T(8,128)(2,1)S(1)}, bf16[64,1024]{1,0:T(8,128)(2,1)S(1)}, u32[]{:S(2)}, u32[]{:S(2)}) %collective-permute-start.15) | collective-permute-done | bytes 131104 | tf_op jit(solution)/shard_map/ppermute | solution.py:432
  101.0 2.8 %collective-permute-done.13 = bf16[64,1024]{1,0:T(8,128)(2,1)S(1)} collective-permute-done((bf16[64,1024]{1,0:T(8,128)(2,1)S(1)}, bf16[64,1024]{1,0:T(8,128)(2,1)S(1)}, u32[]{:S(2)}, u32[]{:S(2)}) %collective-permute-start.13) | collective-permute-done | bytes 131104 | tf_op jit(solution)/shard_map/ppermute | solution.py:432
  (83 shorter events, 14.7 us)
Async XLA Ops:
  0.9 1.0 copy-start.8
  8.6 5.7 %copy-start.5 = (bf16[2,528,128]{2,1,0:T(8,128)(2,1)}, bf16[2,528,128]{2,1,0:T(8,128)(2,1)S(1)}, u32[]{:S(2)}) copy-start(bf16[2,528,128]{2,1,0:T(8,128)(2,1)S(1)} %get-tuple-element.18.mine_ref) | copy-start | bytes 811012
  8.6 5.7 %collective-permute-start.7 = (bf16[2,528,128]{2,1,0:T(8,128)(2,1)S(1)}, bf16[2,528,128]{2,1,0:T(8,128)(2,1)S(1)}, u32[]{:S(2)}, u32[]{:S(2)}) collective-permute-start(bf16[2,528,128]{2,1,0:T(8,128)(2,1)S(1)} %get-tuple-element.18.mine_ref), channel_id=1, source_target_pairs={{0,4},{4,0},{8,12},{12,8},{16,20},{20,16},{24,28},{28,24},{1,5},{5... | collective-permute-start | bytes 811016 | tf_op jit(solution)/shard_map/ppermute | solution.py:403
  10.1 28.3 %copy-start.14 = (bf16[2,256,256]{2,1,0:T(8,128)(2,1)}, bf16[2,256,256]{2,1,0:T(8,128)(2,1)S(1)}, u32[]{:S(2)}) copy-start(bf16[2,256,256]{2,1,0:T(8,128)(2,1)S(1)} %pad_maximum_fusion.1.refs_0_) | copy-start | bytes 786436
  10.1 10.1 %collective-permute-start.1 = (bf16[2,256,256]{2,1,0:T(8,128)(2,1)S(1)}, bf16[2,256,256]{2,1,0:T(8,128)(2,1)S(1)}, u32[]{:S(2)}, u32[]{:S(2)}) collective-permute-start(bf16[2,256,256]{2,1,0:T(8,128)(2,1)S(1)} %pad_maximum_fusion.1.refs_0_), channel_id=1, source_target_pairs={{0,8},{4,12},{8,0},{12,4},{16,24},{20,28},{24,16},{28,20},{1,9},{5... | collective-permute-start | bytes 786440 | tf_op jit(solution)/shard_map/ppermute | solution.py:400
  12.8 14.4 %collective-permute-start.3 = (bf16[2,256,256]{2,1,0:T(8,128)(2,1)S(1)}, bf16[2,256,256]{2,1,0:T(8,128)(2,1)S(1)}, u32[]{:S(2)}, u32[]{:S(2)}) collective-permute-start(bf16[2,256,256]{2,1,0:T(8,128)(2,1)S(1)} %pad_maximum_fusion.1.refs_0_), channel_id=1, source_target_pairs={{0,16},{4,20},{8,24},{12,28},{16,0},{20,4},{24,8},{28,12},{1,17},{... | collective-permute-start | bytes 786440 | tf_op jit(solution)/shard_map/ppermute | solution.py:400
  14.3 12.9 %collective-permute-start.5 = (bf16[2,256,256]{2,1,0:T(8,128)(2,1)S(1)}, bf16[2,256,256]{2,1,0:T(8,128)(2,1)S(1)}, u32[]{:S(2)}, u32[]{:S(2)}) collective-permute-start(bf16[2,256,256]{2,1,0:T(8,128)(2,1)S(1)} %pad_maximum_fusion.1.refs_0_), channel_id=1, source_target_pairs={{0,24},{4,28},{8,16},{12,20},{16,8},{20,12},{24,0},{28,4},{1,25},{... | collective-permute-start | bytes 786440 | tf_op jit(solution)/shard_map/ppermute | solution.py:400
  16.7 11.4 %collective-permute-start.8 = (bf16[528,128]{1,0:T(8,128)(2,1)}, bf16[528,128]{1,0:T(8,128)(2,1)S(1)}, u32[]{:S(2)}, u32[]{:S(2)}) collective-permute-start(bf16[528,128]{1,0:T(8,128)(2,1)} %compose.1), channel_id=1, source_target_pairs={{0,8},{4,12},{8,0},{12,4},{16,24},{20,28},{24,16},{28,20},{1,9},{5... | collective-permute-start | bytes 405512 | tf_op jit(solution)/shard_map/ppermute | solution.py:400
  18.7 10.9 %collective-permute-start.9 = (bf16[528,128]{1,0:T(8,128)(2,1)}, bf16[528,128]{1,0:T(8,128)(2,1)S(1)}, u32[]{:S(2)}, u32[]{:S(2)}) collective-permute-start(bf16[528,128]{1,0:T(8,128)(2,1)} %compose.1), channel_id=1, source_target_pairs={{0,16},{4,20},{8,24},{12,28},{16,0},{20,4},{24,8},{28,12},{1,17},{... | collective-permute-start | bytes 405512 | tf_op jit(solution)/shard_map/ppermute | solution.py:400
  20.2 18.2 %copy-start.19 = (bf16[2,256,256]{2,1,0:T(8,128)(2,1)}, bf16[2,256,256]{2,1,0:T(8,128)(2,1)S(1)}, u32[]{:S(2)}) copy-start(bf16[2,256,256]{2,1,0:T(8,128)(2,1)S(1)} %collective-permute-done.1.refs_2_) | copy-start | bytes 786436
  20.2 18.1 %collective-permute-start = (bf16[2,256,256]{2,1,0:T(8,128)(2,1)S(1)}, bf16[2,256,256]{2,1,0:T(8,128)(2,1)S(1)}, u32[]{:S(2)}, u32[]{:S(2)}) collective-permute-start(bf16[2,256,256]{2,1,0:T(8,128)(2,1)S(1)} %pad_maximum_fusion.1.refs_0_), channel_id=1, source_target_pairs={{0,4},{4,0},{8,12},{12,8},{16,20},{20,16},{24,28},{28,24},{1,5},{5... | collective-permute-start | bytes 786440 | tf_op jit(solution)/shard_map/ppermute | solution.py:403
  27.2 11.2 %copy-start.20 = (bf16[2,256,256]{2,1,0:T(8,128)(2,1)}, bf16[2,256,256]{2,1,0:T(8,128)(2,1)S(1)}, u32[]{:S(2)}) copy-start(bf16[2,256,256]{2,1,0:T(8,128)(2,1)S(1)} %collective-permute-done.3.refs_4_) | copy-start | bytes 786436
  27.2 11.1 %collective-permute-start.2 = (bf16[2,256,256]{2,1,0:T(8,128)(2,1)S(1)}, bf16[2,256,256]{2,1,0:T(8,128)(2,1)S(1)}, u32[]{:S(2)}, u32[]{:S(2)}) collective-permute-start(bf16[2,256,256]{2,1,0:T(8,128)(2,1)S(1)} %collective-permute-done.1.refs_2_), channel_id=1, source_target_pairs={{0,4},{4,0},{8,12},{12,8},{16,20},{20,16},{24,28},{28,24},{1,5},{5... | collective-permute-start | bytes 786440 | tf_op jit(solution)/shard_map/ppermute | solution.py:403
  27.2 11.2 %copy-start.21 = (bf16[2,256,256]{2,1,0:T(8,128)(2,1)}, bf16[2,256,256]{2,1,0:T(8,128)(2,1)S(1)}, u32[]{:S(2)}) copy-start(bf16[2,256,256]{2,1,0:T(8,128)(2,1)S(1)} %collective-permute-done.5.refs_6_) | copy-start | bytes 786436
  27.2 11.1 %collective-permute-start.4 = (bf16[2,256,256]{2,1,0:T(8,128)(2,1)S(1)}, bf16[2,256,256]{2,1,0:T(8,128)(2,1)S(1)}, u32[]{:S(2)}, u32[]{:S(2)}) collective-permute-start(bf16[2,256,256]{2,1,0:T(8,128)(2,1)S(1)} %collective-permute-done.3.refs_4_), channel_id=1, source_target_pairs={{0,4},{4,0},{8,12},{12,8},{16,20},{20,16},{24,28},{28,24},{1,5},{5... | collective-permute-start | bytes 786440 | tf_op jit(solution)/shard_map/ppermute | solution.py:403
  28.2 7.7 %copy-start.15 = (bf16[528,128]{1,0:T(8,128)(2,1)}, bf16[528,128]{1,0:T(8,128)(2,1)S(1)}, u32[]{:S(2)}) copy-start(bf16[528,128]{1,0:T(8,128)(2,1)S(1)} %collective-permute-done.8.refs_0_) | copy-start | bytes 405508
  28.2 10.2 %collective-permute-start.6 = (bf16[2,256,256]{2,1,0:T(8,128)(2,1)S(1)}, bf16[2,256,256]{2,1,0:T(8,128)(2,1)S(1)}, u32[]{:S(2)}, u32[]{:S(2)}) collective-permute-start(bf16[2,256,256]{2,1,0:T(8,128)(2,1)S(1)} %collective-permute-done.5.refs_6_), channel_id=1, source_target_pairs={{0,4},{4,0},{8,12},{12,8},{16,20},{20,16},{24,28},{28,24},{1,5},{5... | collective-permute-start | bytes 786440 | tf_op jit(solution)/shard_map/ppermute | solution.py:403
  29.6 6.3 %copy-start.16 = (bf16[528,128]{1,0:T(8,128)(2,1)}, bf16[528,128]{1,0:T(8,128)(2,1)S(1)}, u32[]{:S(2)}) copy-start(bf16[528,128]{1,0:T(8,128)(2,1)S(1)} %collective-permute-done.9.refs_1_) | copy-start | bytes 405508
  29.6 6.3 %collective-permute-start.10 = (bf16[528,128]{1,0:T(8,128)(2,1)}, bf16[528,128]{1,0:T(8,128)(2,1)S(1)}, u32[]{:S(2)}, u32[]{:S(2)}) collective-permute-start(bf16[528,128]{1,0:T(8,128)(2,1)} %compose.1), channel_id=1, source_target_pairs={{0,24},{4,28},{8,16},{12,20},{16,8},{20,12},{24,0},{28,4},{1,25},{... | collective-permute-start | bytes 405512 | tf_op jit(solution)/shard_map/ppermute | solution.py:400
  38.3 6.4 %collective-permute-start.11 = (bf16[512,128]{1,0:T(8,128)(2,1)}, bf16[512,128]{1,0:T(8,128)(2,1)S(1)}, u32[]{:S(2)}, u32[]{:S(2)}) collective-permute-start(bf16[512,128]{1,0:T(8,128)(2,1)} %carry_in.1.mine_ref), channel_id=1, source_target_pairs={{0,4},{4,0},{8,12},{12,8},{16,20},{20,16},{24,28},{28,24},{1,5},{5... | collective-permute-start | bytes 393224 | tf_op jit(solution)/shard_map/ppermute | solution.py:403
  48.0 3.4 %copy-start = (bf16[1024,4096]{1,0:T(8,128)(2,1)S(1)}, bf16[1024,4096]{1,0:T(8,128)(2,1)}, u32[]{:S(2)}) copy-start(bf16[1024,4096]{1,0:T(8,128)(2,1)} %wa_ref.7) | copy-start | bytes 25165828
  51.4 3.4 %copy-start.1 = (bf16[1024,4096]{1,0:T(8,128)(2,1)S(1)}, bf16[1024,4096]{1,0:T(8,128)(2,1)}, u32[]{:S(2)}) copy-start(bf16[1024,4096]{1,0:T(8,128)(2,1)} %wm_ref.7) | copy-start | bytes 25165828
  54.8 1.0 copy-start.2
  55.9 1.0 copy-start.3
  58.7 9.8 %collective-permute-start.18 = (bf16[128,1024]{1,0:T(8,128)(2,1)S(1)}, bf16[128,1024]{1,0:T(8,128)(2,1)S(1)}, u32[]{:S(2)}, u32[]{:S(2)}) collective-permute-start(bf16[128,1024]{1,0:T(8,128)(2,1)S(1)} %get-tuple-element.26), channel_id=1, source_target_pairs={{0,1},{1,0},{2,3},{3,2},{4,5},{5,4},{6,7},{7,6},{8,9},{9,8},{10,11... | collective-permute-start | bytes 786440 | tf_op jit(solution)/shard_map/ppermute | solution.py:430
  62.2 13.7 %collective-permute-start.16 = (bf16[128,1024]{1,0:T(8,128)(2,1)S(1)}, bf16[128,1024]{1,0:T(8,128)(2,1)S(1)}, u32[]{:S(2)}, u32[]{:S(2)}) collective-permute-start(bf16[128,1024]{1,0:T(8,128)(2,1)S(1)} %get-tuple-element.24), channel_id=1, source_target_pairs={{0,1},{1,0},{2,3},{3,2},{4,5},{5,4},{6,7},{7,6},{8,9},{9,8},{10,11... | collective-permute-start | bytes 786440 | tf_op jit(solution)/shard_map/ppermute | solution.py:430
  66.4 18.0 %collective-permute-start.14 = (bf16[128,1024]{1,0:T(8,128)(2,1)S(1)}, bf16[128,1024]{1,0:T(8,128)(2,1)S(1)}, u32[]{:S(2)}, u32[]{:S(2)}) collective-permute-start(bf16[128,1024]{1,0:T(8,128)(2,1)S(1)} %get-tuple-element.22), channel_id=1, source_target_pairs={{0,1},{1,0},{2,3},{3,2},{4,5},{5,4},{6,7},{7,6},{8,9},{9,8},{10,11... | collective-permute-start | bytes 786440 | tf_op jit(solution)/shard_map/ppermute | solution.py:430
  68.1 22.0 %collective-permute-start.12 = (bf16[128,1024]{1,0:T(8,128)(2,1)S(1)}, bf16[128,1024]{1,0:T(8,128)(2,1)S(1)}, u32[]{:S(2)}, u32[]{:S(2)}) collective-permute-start(bf16[128,1024]{1,0:T(8,128)(2,1)S(1)} %get-tuple-element.20), channel_id=1, source_target_pairs={{0,1},{1,0},{2,3},{3,2},{4,5},{5,4},{6,7},{7,6},{8,9},{9,8},{10,11... | collective-permute-start | bytes 786440 | tf_op jit(solution)/shard_map/ppermute | solution.py:430
  68.6 23.1 %collective-permute-start.19 = (bf16[64,1024]{1,0:T(8,128)(2,1)S(1)}, bf16[64,1024]{1,0:T(8,128)(2,1)S(1)}, u32[]{:S(2)}, u32[]{:S(2)}) collective-permute-start(bf16[64,1024]{1,0:T(8,128)(2,1)S(1)} %slice.60), channel_id=1, source_target_pairs={{0,2},{1,3},{2,0},{3,1},{4,6},{5,7},{6,4},{7,5},{8,10},{9,11},{10,... | collective-permute-start | bytes 393224 | tf_op jit(solution)/shard_map/ppermute | solution.py:432
  76.0 15.7 %collective-permute-start.17 = (bf16[64,1024]{1,0:T(8,128)(2,1)S(1)}, bf16[64,1024]{1,0:T(8,128)(2,1)S(1)}, u32[]{:S(2)}, u32[]{:S(2)}) collective-permute-start(bf16[64,1024]{1,0:T(8,128)(2,1)S(1)} %slice.61), channel_id=1, source_target_pairs={{0,2},{1,3},{2,0},{3,1},{4,6},{5,7},{6,4},{7,5},{8,10},{9,11},{10,... | collective-permute-start | bytes 393224 | tf_op jit(solution)/shard_map/ppermute | solution.py:432
  84.5 16.4 %collective-permute-start.15 = (bf16[64,1024]{1,0:T(8,128)(2,1)S(1)}, bf16[64,1024]{1,0:T(8,128)(2,1)S(1)}, u32[]{:S(2)}, u32[]{:S(2)}) collective-permute-start(bf16[64,1024]{1,0:T(8,128)(2,1)S(1)} %slice.62), channel_id=1, source_target_pairs={{0,2},{1,3},{2,0},{3,1},{4,6},{5,7},{6,4},{7,5},{8,10},{9,11},{10,... | collective-permute-start | bytes 393224 | tf_op jit(solution)/shard_map/ppermute | solution.py:432
  90.2 13.5 %collective-permute-start.13 = (bf16[64,1024]{1,0:T(8,128)(2,1)S(1)}, bf16[64,1024]{1,0:T(8,128)(2,1)S(1)}, u32[]{:S(2)}, u32[]{:S(2)}) collective-permute-start(bf16[64,1024]{1,0:T(8,128)(2,1)S(1)} %slice.63), channel_id=1, source_target_pairs={{0,2},{1,3},{2,0},{3,1},{4,6},{5,7},{6,4},{7,5},{8,10},{9,11},{10,... | collective-permute-start | bytes 393224 | tf_op jit(solution)/shard_map/ppermute | solution.py:432
  (14 other events, 10.5 us)

commit v2 on v1

v2 whole, which is shorter than its diff:
```python
import functools

import jax
import jax.numpy as jnp
from jax import lax
from jax.experimental import pallas as pl
from jax.experimental.pallas import tpu as pltpu
from jax.sharding import PartitionSpec as P

HEAD_DIM = 128
SSM_HEAD_DIM = 128
STATE = 128
LOG2E = 1.4426950408889634
LOW = -1e30
SHARES = (2, 2, 2, 1, 1)
F32 = jnp.float32
BF16 = jnp.bfloat16

MIB = 1 << 20
VMEM_SPEC = pl.BlockSpec(memory_space=pltpu.VMEM)
ANY_SPEC = pl.BlockSpec(memory_space=pl.ANY)
HBM_SPEC = pl.BlockSpec(memory_space=pltpu.HBM)


def in_hbm(a):
    return pltpu.with_memory_space_constraint(a, pltpu.HBM)


class Far:
    def __init__(self, array, space=pltpu.VMEM, lanes=None):
        self.array, self.lanes = array, lanes
        shape = array.shape if lanes is None else (array.shape[0], lanes.stop - lanes.start)
        self.scratch = space(shape, array.dtype)


def one_step(kernel, name, out_shape, far, near, scratch=(), cost=(0, 0, 0), room=6 * MIB, specs=None):
    flops, moved, exps = cost

    def body(*refs):
        given, refs = refs[: len(far)], refs[len(far) :]
        rest, held, sem = refs[: -len(far) - 1], refs[-len(far) - 1 : -1], refs[-1]
        copies = []
        for i, (f, src, dst) in enumerate(zip(far, given, held)):
            src = src if f.lanes is None else src.at[:, f.lanes]
            copies.append(pltpu.make_async_copy(src, dst, sem.at[i]))
        for c in copies:
            c.start()
        for c in copies:
            c.wait()
        kernel(*held, *rest)

    return pl.pallas_call(
        body,
        out_shape=tuple(out_shape),
        in_specs=[HBM_SPEC] * len(far) + (specs or [VMEM_SPEC] * len(near)),
        out_specs=(VMEM_SPEC,) * len(out_shape),
        scratch_shapes=[
            *scratch,
            *(f.scratch for f in far),
            pltpu.SemaphoreType.DMA((len(far),)),
        ],
        compiler_params=pltpu.CompilerParams(vmem_limit_bytes=room),
        cost_estimate=pl.CostEstimate(flops=flops, bytes_accessed=moved, transcendentals=exps),
        name=name,
    )(*(in_hbm(f.array) for f in far), *near)


def doc_ends_of(len_ref):
    ends, total = [], 0
    for i in range(len_ref.shape[0]):
        total = total + len_ref[i]
        ends.append(total)
    return ends


def doc_start(pos, ends):
    start = jnp.zeros_like(pos)
    for end in ends:
        start = jnp.where(pos >= end, end, start)
    return start


def row_slot(part, z):
    d = part ^ z
    return jnp.where(d == 1, 0, jnp.where(d == 3, 1, jnp.where(d == 0, 2, 3)))


def nt(a, b):
    return lax.dot_general(a, b, (((1,), (1,)), ((), ())), preferred_element_type=F32)


def nn(a, b):
    return lax.dot_general(a, b, (((1,), (0,)), ((), ())), preferred_element_type=F32)


def mixer_kernel(len_ref, skip_ref, x_ref, w_ref, r_ref, ld_ref, base_ref, st_ref, eg_ref):
    me = lax.axis_index("ctx")
    heads, rows = ld_ref.shape
    groups = w_ref.shape[1] // STATE
    per_group = heads // groups
    half = heads // 2
    first = me * rows
    ends = doc_ends_of(len_ref)
    ds = ld_ref[...]
    lane = lax.broadcasted_iota(jnp.int32, ds.shape, 1)
    shift = 1
    while shift < rows:
        ds = ds + jnp.where(lane >= shift, pltpu.roll(ds, shift, 1), 0.0)
        shift *= 2
    col = ds.T
    t_pos = first + lax.broadcasted_iota(jnp.int32, (rows, 1), 0)
    t_start = doc_start(t_pos, ends)
    s_pos = first + lax.broadcasted_iota(jnp.int32, (1, rows), 1)
    last = first + rows - 1
    last_start = doc_start(jnp.full((1, 1), last, jnp.int32), ends)
    visible = (s_pos <= t_pos) & (s_pos >= t_start)
    bias = jnp.where(visible, 0.0, LOW)
    eg_ref[...] = jnp.where(t_start < first, jnp.exp(col), 0.0)
    total = ds[:, rows - 1 : rows]
    end_weight = jnp.where(s_pos >= last_start, jnp.exp(total - ds), 0.0)
    gain = jnp.where(last_start < first, jnp.exp(total), 0.0)
    gain = jnp.broadcast_to(gain, (heads, SSM_HEAD_DIM)).astype(BF16)
    pad = jnp.zeros((st_ref.shape[1] - half * STATE - half, SSM_HEAD_DIM), BF16)
    for c in range(2):
        st_ref[c, half * STATE :, :] = jnp.concatenate(
            [gain[c * half : (c + 1) * half].astype(F32), pad.astype(F32)], axis=0
        ).astype(BF16)
    for g in range(groups):
        cols = slice(g * STATE, (g + 1) * STATE)
        write, read = w_ref[:, cols], r_ref[:, cols]
        inner = nt(read, write)
        write_t = write.astype(F32).T
        for h in range(g * per_group, (g + 1) * per_group):
            hc = slice(h * SSM_HEAD_DIM, (h + 1) * SSM_HEAD_DIM)
            x = x_ref[:, hc]
            decay = jnp.exp((col[:, h : h + 1] - ds[h : h + 1, :]) + bias)
            mixing = (decay * inner).astype(BF16)
            base_ref[:, hc] = nn(mixing, x) + skip_ref[h] * x.astype(F32)
            end_write = (write_t * end_weight[h : h + 1, :]).astype(BF16)
            c, i = divmod(h, half)
            st_ref[c, i * STATE : (i + 1) * STATE, :] = nn(end_write, x).astype(BF16)


def mixer_local(doc_lengths, skip_gain, x, w, r, ld):
    heads, rows = ld.shape
    half = heads // 2
    return one_step(
        mixer_kernel,
        "mixer_local",
        (
            jax.ShapeDtypeStruct(x.shape, F32),
            jax.ShapeDtypeStruct((2, half * STATE + 16, SSM_HEAD_DIM), BF16),
            jax.ShapeDtypeStruct((rows, heads), F32),
        ),
        (Far(doc_lengths, pltpu.SMEM), Far(skip_gain, pltpu.SMEM), Far(x), Far(w), Far(r), Far(ld)),
        (),
    )


def compose_kernel(mine_ref, other_ref, out_ref):
    core = lax.axis_index("ctx") & 1
    state_rows = out_ref.shape[0] - 16
    half = state_rows // STATE
    a, b = mine_ref[core].astype(F32), other_ref[core].astype(F32)
    first = jnp.where(core == 0, a, b)
    second = jnp.where(core == 0, b, a)
    for i in range(half):
        rows = slice(i * STATE, (i + 1) * STATE)
        gain = second[state_rows + i : state_rows + i + 1]
        out_ref[rows, :] = (gain * first[rows] + second[rows]).astype(BF16)
    out_ref[state_rows:, :] = (first[state_rows:] * second[state_rows:]).astype(BF16)


def compose(mine, other):
    return pl.pallas_call(
        compose_kernel,
        out_shape=jax.ShapeDtypeStruct(mine.shape[1:], BF16),
        in_specs=[VMEM_SPEC] * 2,
        out_specs=VMEM_SPEC,
        compiler_params=pltpu.CompilerParams(vmem_limit_bytes=4 * MIB),
        cost_estimate=pl.CostEstimate(flops=0, bytes_accessed=0, transcendentals=0),
        name="compose",
    )(mine, other)


def finish_kernel(r_ref, base_ref, eg_ref, st_ref, *refs):
    *got, out_ref, held = refs
    me = lax.axis_index("ctx")
    core, chip = me & 1, me // 2
    z = lax.axis_index("tp")
    rows = base_ref.shape[0]
    part = rows // 4
    state_rows = st_ref.shape[1] - 16
    half = state_rows // STATE
    groups = r_ref.shape[1] // STATE
    heads = 2 * half
    per_group = heads // groups
    for j in range(1, held.shape[0]):
        held[chip ^ j, core] = got[2 * j - 2][...]
        held[chip ^ j, core ^ 1] = got[2 * j - 1][...]

    for h in range(heads):
        c, i = divmod(h, half)
        hs = slice(i * STATE, (i + 1) * STATE)
        gs = slice(state_rows + i, state_rows + i + 1)

        def one(k, carry):
            return held[k, c, gs, :].astype(F32) * carry + held[k, c, hs, :].astype(F32)

        entering = lax.fori_loop(0, chip, one, jnp.zeros((STATE, SSM_HEAD_DIM), F32))
        prev = st_ref[c, hs, :].astype(F32)
        gain = st_ref[c, gs, :].astype(F32)
        carry = jnp.where(core == 1, gain * entering + prev, entering).astype(BF16)
        hc = slice(h * SSM_HEAD_DIM, (h + 1) * SSM_HEAD_DIM)
        g = h // per_group
        inter = nn(r_ref[:, g * STATE : (g + 1) * STATE], carry)
        res = (base_ref[:, hc] + eg_ref[:, h : h + 1] * inter).astype(BF16)
        for q in range(4):
            at = pl.multiple_of(row_slot(q, z) * part, part)
            out_ref[pl.ds(at, part), hc] = res[q * part : (q + 1) * part]


def finish(base, r, eg, st_other, got):
    chips = len(got) // 2 + 1
    return one_step(
        finish_kernel,
        "finish",
        (jax.ShapeDtypeStruct(base.shape, BF16),),
        (Far(r),),
        (base, eg, st_other, *got),
        scratch=[pltpu.VMEM((chips, 2) + got[0].shape, BF16)],
        room=(4 + chips) * MIB,
    )[0]


def attention_kernel(page_len, kv_head, len_ref, table_ref, q_ref, *refs):
    *got, _, _, out_ref, inv, kv, sem, sc, mx, ls, acc = refs
    me = lax.axis_index("ctx")
    z = lax.axis_index("tp")
    rows = q_ref.shape[0]
    part = rows // 4
    heads = q_ref.shape[1] // HEAD_DIM
    lanes = slice(kv_head * HEAD_DIM, (kv_head + 1) * HEAD_DIM)
    first = me * rows
    ends = doc_ends_of(len_ref)
    start0 = 0
    for end in ends:
        start0 = jnp.where(first >= end, end, start0)
    low_block = start0 // rows
    pages_block = rows // page_len

    def invert(l, _):
        inv[table_ref[l]] = l
        return 0

    lax.fori_loop(0, table_ref.shape[0], invert, 0)
    low_page, high_page = low_block * pages_block, (me + 1) * pages_block

    def page_copy(ref, slot, page):
        here = pl.ds(slot * page_len, page_len)
        there = pl.ds(pl.multiple_of(page * page_len, page_len), page_len)
        return pltpu.make_async_copy(ref.at[:, here, lanes], kv.at[:, there, :], sem.at[page])

    for j, ref in enumerate(got):
        for slot in range(ref.shape[1] // page_len):
            page = inv[(me ^ j) * (ref.shape[1] // page_len) + slot]

            @pl.when((page >= low_page) & (page < high_page))
            def _():
                page_copy(ref, slot, page).start()

    t_pos = first + lax.broadcasted_iota(jnp.int32, (rows, 1), 0)
    t_start = doc_start(t_pos, ends)
    scale = LOG2E * HEAD_DIM ** (-0.5)

    def scores(block, own):
        for i in range(pages_block):
            page_copy(got[0], 0, block * pages_block + i).wait()
        at = pl.ds(pl.multiple_of(block * rows, rows), rows)
        u_pos = block * rows + lax.broadcasted_iota(jnp.int32, (1, rows), 1)
        shown = u_pos >= t_start
        if own:
            shown = shown & (u_pos <= t_pos)
        for h in range(heads):
            s = nt(
                q_ref[:, h * HEAD_DIM : (h + 1) * HEAD_DIM],
                kv[0, at, :],
            )
            s = jnp.where(shown, s * scale, LOW)
            sc[block - low_block, h] = s
            top = s[:, :128]
            for k in range(128, rows, 128):
                top = jnp.maximum(top, s[:, k : k + 128])
            mx[h] = top if own else jnp.maximum(mx[h], top)

    scores(me, True)

    def earlier(block, _):
        scores(block, False)
        return 0

    lax.fori_loop(low_block, me, earlier, 0)
    for h in range(heads):
        mx[h] = jnp.broadcast_to(jnp.max(mx[h], axis=1, keepdims=True), (rows, 128))
    ls[...] = jnp.zeros_like(ls)
    acc[...] = jnp.zeros_like(acc)

    def weigh(block, _):
        at = pl.ds(pl.multiple_of(block * rows, rows), rows)
        for h in range(heads):
            m = mx[h]
            total = ls[h]
            pieces = []
            for k in range(0, rows, 128):
                w = jnp.exp2(sc[block - low_block, h, :, k : k + 128] - m)
                total = total + w
                pieces.append(w.astype(BF16))
            ls[h] = total
            acc[h] += nn(
                jnp.concatenate(pieces, axis=1), kv[1, at, :]
            )
        return 0

    lax.fori_loop(low_block, me + 1, weigh, 0)
    for h in range(heads):
        res = (acc[h] / jnp.sum(ls[h], axis=1, keepdims=True)).astype(BF16)
        for q in range(4):
            at = pl.multiple_of(row_slot(q, z) * part, part)
            out_ref[pl.ds(at, part), h * HEAD_DIM : (h + 1) * HEAD_DIM] = res[
                q * part : (q + 1) * part
            ]


def attention(page_len, doc_lengths, page_table, queries, got, ready, kv_head, kv_heads):
    rows = queries.shape[0]
    width = queries.shape[1] // kv_heads
    heads = width // HEAD_DIM
    out = jax.ShapeDtypeStruct((rows, width), BF16)
    keys = len(got) * got[0].shape[1]
    blocks = min(keys // rows, keys // 2 // rows + 1)
    return one_step(
        functools.partial(attention_kernel, page_len, kv_head),
        "attention",
        (out,),
        (
            Far(doc_lengths, pltpu.SMEM),
            Far(page_table, pltpu.SMEM),
            Far(queries, lanes=slice(kv_head * width, (kv_head + 1) * width)),
        ),
        (*got, *ready),
        specs=[ANY_SPEC] * (len(got) + len(ready)),
        scratch=[
            pltpu.SMEM((page_table.shape[0],), jnp.int32),
            pltpu.VMEM((2, keys, HEAD_DIM), BF16),
            pltpu.SemaphoreType.DMA((page_table.shape[0],)),
            pltpu.VMEM((blocks, heads, rows, rows), F32),
            pltpu.VMEM((heads, rows, 128), F32),
            pltpu.VMEM((heads, rows, 128), F32),
            pltpu.VMEM((heads, rows, HEAD_DIM), F32),
        ],
        cost=(64 * heads * rows * 1280 * 128, 4 << 20, heads * rows * 1280),
        room=5 * MIB + 4 * heads * rows * rows * blocks + 4 * keys * HEAD_DIM,
    )[0]


def fetch_kernel(pieces, *refs):
    *given, sem = refs
    given = given[1:]
    count = len(given) // 2
    copies = []
    for k in range(count):
        depth = given[k].shape[0] // pieces
        for i in range(pieces):
            here = slice(i * depth, (i + 1) * depth)
            copies.append(
                pltpu.make_async_copy(
                    given[k].at[here], given[count + k].at[here], sem.at[k * pieces + i]
                )
            )
    for c in copies:
        c.start()
    for c in copies:
        c.wait()


def fetch(after, *weights):
    return pl.pallas_call(
        functools.partial(fetch_kernel, 4),
        out_shape=tuple(jax.ShapeDtypeStruct(w.shape, w.dtype) for w in weights),
        in_specs=[ANY_SPEC] + [HBM_SPEC] * len(weights),
        out_specs=(VMEM_SPEC,) * len(weights),
        scratch_shapes=[pltpu.SemaphoreType.DMA((4 * len(weights),))],
        compiler_params=pltpu.CompilerParams(vmem_limit_bytes=1 * MIB),
        cost_estimate=pl.CostEstimate(
            flops=0, bytes_accessed=2 * sum(w.size for w in weights), transcendentals=0
        ),
        name="fetch",
    )(after, *(in_hbm(w) for w in weights))


def project_kernel(start, tile, count, *refs):
    att, (mix_ref, wa_ref, wm_ref), out = refs[:count], refs[count : count + 3], refs[count + 3 :]
    for send_ref, keep_ref in zip(out[::2], out[1::2]):
        sent, width = send_ref.shape
        for j in range(0, width, tile):
            here, there = slice(j, j + tile), slice(start + j, start + j + tile)
            total = nn(mix_ref[...], wm_ref[:, there])
            row = 0
            for a in att:
                total += nn(a[...], wa_ref[row : row + a.shape[1], there])
                row += a.shape[1]
            send_ref[:, here] = total[:sent].astype(BF16)
            keep_ref[:, here] = total[sent:]
        start += width


def project(att, mix, wa, wm, start, widths, tile):
    rows, depth = mix.shape
    out_shape = []
    for width in widths:
        out_shape.append(jax.ShapeDtypeStruct((rows // 2, width), BF16))
        out_shape.append(jax.ShapeDtypeStruct((rows // 2, width), F32))
    out = pl.pallas_call(
        functools.partial(project_kernel, start, tile, len(att)),
        out_shape=tuple(out_shape),
        in_specs=[VMEM_SPEC] * (len(att) + 3),
        out_specs=(VMEM_SPEC,) * len(out_shape),
        compiler_params=pltpu.CompilerParams(vmem_limit_bytes=4 * MIB),
        cost_estimate=pl.CostEstimate(
            flops=4 * rows * depth * sum(widths),
            bytes_accessed=6 * rows * sum(widths),
            transcendentals=0,
        ),
        name="project",
    )(*att, mix, wa, wm)
    return list(zip(out[::2], out[1::2]))


def shards(
    n_ctx,
    n_tp,
    queries,
    key_pages,
    value_pages,
    mixer_input,
    state_write,
    state_read,
    log_decay,
    skip_gain,
    doc_lengths,
    page_table,
    attention_weight,
    mixer_weight,
):
    tok_rows = queries.shape[0]
    page_len = key_pages.shape[1]
    chips = n_ctx // 2

    def between_chips(a, j):
        return lax.ppermute(a, "ctx", [(i, i ^ (2 * j)) for i in range(n_ctx)])

    def other_core(a):
        return lax.ppermute(a, "ctx", [(i, i ^ 1) for i in range(n_ctx)])

    width = key_pages.shape[2]
    kv = jnp.stack([key_pages.reshape(-1, width), value_pages.reshape(-1, width)])
    kv, mixer_input = lax.optimization_barrier((kv, mixer_input))
    far = [kv] + [between_chips(kv, j) for j in range(1, chips)]

    base, st, eg = mixer_local(
        doc_lengths, skip_gain, mixer_input, state_write, state_read, log_decay
    )
    st_other = other_core(st)
    chip_state = compose(st, st_other)
    ready = fetch(st, attention_weight, mixer_weight)
    far_states = [between_chips(chip_state, j) for j in range(1, chips)]

    far[1:], ready = lax.optimization_barrier((far[1:], ready))
    got = []
    for a in far:
        got += [a, other_core(a)]
    kv_heads = width // HEAD_DIM
    att = [
        attention(page_len, doc_lengths, page_table, queries, got, ready, i, kv_heads)
        for i in range(kv_heads)
    ]
    *far_states, att[0] = lax.optimization_barrier((*far_states, att[0]))
    got_states = []
    for a in far_states:
        got_states += [a, other_core(a)]
    mix = finish(base, state_read, eg, st_other, got_states)

    part = tok_rows // n_tp
    columns = attention_weight.shape[1]
    widths = [share * columns // 8 for share in SHARES]
    sums = project(att, mix, *ready, 0, widths[:1], 256)
    sums += project(att, mix, *ready, widths[0], widths[1:], 256)
    kept = [
        (keep, lax.ppermute(send, "tp", [(i, i ^ 1) for i in range(n_tp)])) for send, keep in sums
    ]
    pieces = []
    order = None
    for keep, near in kept:
        if order is not None:
            near, order = lax.optimization_barrier((near, order))
        both = keep + near.astype(F32)
        order = both[part:].astype(BF16)
        last = lax.ppermute(order, "tp", [(i, i ^ 2) for i in range(n_tp)])
        pieces.append((both[:part] + last.astype(F32)).astype(BF16))
    return jnp.concatenate(pieces, axis=1)


def solution(mesh):
    placed = (
        P("ctx", "tp"),
        P("ctx", None, "tp"),
        P("ctx", None, "tp"),
        P("ctx", "tp"),
        P("ctx", "tp"),
        P("ctx", "tp"),
        P("tp", "ctx"),
        P("tp"),
        P(),
        P(),
        P("tp", None),
        P("tp", None),
    )
    return jax.shard_map(
        functools.partial(shards, mesh.shape["ctx"], mesh.shape["tp"]),
        mesh=mesh,
        in_specs=placed,
        out_specs=P(("ctx", "tp"), None),
        check_vma=False,
    )
```

time: 106 us -> 82.2 us (0.78); the launches traced: 105 us -> 81.9 us
  local copies, waits for them, and re-layouts: 18.9 us -> 0.19 us
  waiting for transfers between devices: 40.9 us -> 33.5 us
  starting transfers between devices: 21.9 us -> 24.8 us
    unnamed x52 -> x2, local copies, waits for them, and re-layouts: 18.8 us -> 0.12 us
    ppermute x6, waiting for transfers between devices: 13.6 us -> 5.85 us  [between_chips(): return lax.ppermute(a, 'ctx', [(i, i ^ 2 * j) for i in range(n_ctx)])]
    ppermute x8 -> x10, starting transfers between devices: 11.7 us -> 15 us  [the longest x5 9.25 us: shards(): last = lax.ppermute(order, 'tp', [(i, i ^ 2) for i in range(n_tp)])]
    pallas_call x8 -> x7, Pallas kernels: 18.7 us -> 21.2 us  [the longest x4 10.6 us: one_step(): pl.pallas_call(body, out_shape=tuple(out_shape), in_specs=[HBM_SPEC] * le...]
    pallas_call x1, Pallas kernels: 1.74 us -> 0.06 us  [compose(): pl.pallas_call(compose_kernel, out_shape=jax.ShapeDtypeStruct(mine.shape[...]
    ppermute x8 -> x10, waiting for transfers between devices: 27.2 us -> 27.6 us  [the longest x5 17.8 us: shards(): lax.ppermute(send, 'tp', [(i, i ^ 1) for i in range(n_tp)])]
  transfers between devices with their start and end apart: 20 -> 24, of which waited for: 9 -> 9; matrix products, arithmetic and copies ran while one was open for 1% -> 1% of each run, Pallas kernels for 13% -> 21%
where the time goes in v2:
time: 82.2 us; the launch traced here: 81.9 us
  waiting for transfers between devices  33.5 us (41%)
  starting transfers between devices  24.8 us (30%)
  Pallas kernels  21.3 us (26%)
  other arithmetic  2 us (2%)
    ppermute x5, waiting for transfers between devices, shards(): lax.ppermute(send, 'tp', [(i, i ^ 1) for i in range(n_tp)])  17.8 us
    pallas_call x4, Pallas kernels, one_step(): pl.pallas_call(body, out_shape=tuple(out_shape), in_specs=[HBM_SPEC] * le...  10.6 us
    ppermute x5, waiting for transfers between devices, shards(): last = lax.ppermute(order, 'tp', [(i, i ^ 2) for i in range(n_tp)])  9.81 us
    ppermute x5, starting transfers between devices, shards(): last = lax.ppermute(order, 'tp', [(i, i ^ 2) for i in range(n_tp)])  9.25 us
    ppermute x6, starting transfers between devices, between_chips(): return lax.ppermute(a, 'ctx', [(i, i ^ 2 * j) for i in range(n_ctx)])  8.16 us
    pallas_call x1, Pallas kernels, fetch(): pl.pallas_call(functools.partial(fetch_kernel, 4), out_shape=tuple((jax.S...  5.92 us
    ppermute x6, waiting for transfers between devices, between_chips(): return lax.ppermute(a, 'ctx', [(i, i ^ 2 * j) for i in range(n_ctx)])  5.85 us
    ppermute x5, starting transfers between devices, shards(): lax.ppermute(send, 'tp', [(i, i ^ 1) for i in range(n_tp)])  5.76 us
  transfers between devices with their start and end apart: 24, of which 9 were waited for; matrix products, arithmetic and copies ran while one was open for 1% of the time, Pallas kernels for 21%

profile of v2, /device:TPU:0, one launch (start us, length us, event | category | flops | bytes accessed | tf_op | source)
XLA Modules:
  0.0 81.9 jit_solution(11493659027625434929)
XLA Ops:
  0.0 1.0 %pad_maximum_fusion.refs_3_ = bf16[2,256,256]{2,1,0:T(8,128)(2,1)S(1)} fusion(bf16[1,256,256]{2,1,0:T(8,128)(2,1)} %bitcast.2, bf16[1,256,256]{2,1,0:T(8,128)(2,1)} %bitcast.3), kind=kLoop, calls=%fused_computation.12 | loop fusion | flops 131072 | bytes 524288 | tf_op jit(solution)/shard_map/stack | solution.py:466
  1.0 4.0 %collective-permute-start.7 = (bf16[2,256,256]{2,1,0:T(8,128)(2,1)S(1)}, bf16[2,256,256]{2,1,0:T(8,128)(2,1)S(1)}, u32[]{:S(2)}, u32[]{:S(2)}) collective-permute-start(bf16[2,256,256]{2,1,0:T(8,128)(2,1)S(1)} %pad_maximum_fusion.refs_3_), channel_id=1, source_target_pairs={{0,24},{4,28},{8,16},{12,20},{16,8},{20,12},{24,0},{28,4},{1,25},{... | collective-permute-start | bytes 786440 | tf_op jit(solution)/shard_map/ppermute | solution.py:460
  5.0 0.5 collective-permute-start.6
  5.6 2.8 %mixer_local.1 = (f32[256,1024]{1,0:T(8,128)S(1)}, bf16[2,528,128]{2,1,0:T(8,128)(2,1)S(1)}, f32[256,8]{1,0:T(8,128)S(1)}) custom-call(s32[4]{0:T(128)} %refs_0_.6, f32[8]{0:T(128)} %refs_1_.4, bf16[256,1024]{1,0:T(8,128)(2,1)} %refs_2_.3, bf16[256,256]{1,0:T(8,128)(2,1)} %refs_3_.1, bf16[256,256]{1,0:T(8,128)(2,1)} %refs_0_.7, f32[8,256]{1,0:T(8,128)} %refs_5_.1), custom_call_target="tpu_custom_call" | custom-call | tf_op jit(solution)/shard_map/mixer_local/pallas_call | solution.py:52
  8.9 5.9 %fetch.1 = (bf16[1024,4096]{1,0:T(8,128)(2,1)S(1)}, bf16[1024,4096]{1,0:T(8,128)(2,1)S(1)}) custom-call(bf16[2,528,128]{2,1,0:T(8,128)(2,1)S(1)} %get-tuple-element.36.mine_ref.refs_0_, bf16[1024,4096]{1,0:T(8,128)(2,1)} %refs_1_.5, bf16[1024,4096]{1,0:T(8,128)(2,1)} %refs_2_.4), custom_call_target="tpu_custom_call" | custom-call | bytes 16777216 | tf_op jit(solution)/shard_map/fetch/pallas_call | solution.py:387
  14.9 2.0 %collective-permute-done.6.refs_7_ = bf16[2,256,256]{2,1,0:T(8,128)(2,1)S(1)} collective-permute-done((bf16[2,256,256]{2,1,0:T(8,128)(2,1)S(1)}, bf16[2,256,256]{2,1,0:T(8,128)(2,1)S(1)}, u32[]{:S(2)}, u32[]{:S(2)}) %collective-permute-start.6) | collective-permute-done | bytes 262176 | tf_op jit(solution)/shard_map/ppermute | solution.py:460
  17.2 0.5 collective-permute-start.9
  17.8 1.6 %collective-permute-start.3 = (bf16[528,128]{1,0:T(8,128)(2,1)S(1)}, bf16[528,128]{1,0:T(8,128)(2,1)S(1)}, u32[]{:S(2)}, u32[]{:S(2)}) collective-permute-start(bf16[528,128]{1,0:T(8,128)(2,1)S(1)} %compose.1), channel_id=1, source_target_pairs={{0,24},{4,28},{8,16},{12,20},{16,8},{20,12},{24,0},{28,4},{1,25},{... | collective-permute-start | bytes 405512 | tf_op jit(solution)/shard_map/ppermute | solution.py:460
  19.4 1.4 %collective-permute-start.2 = (bf16[528,128]{1,0:T(8,128)(2,1)S(1)}, bf16[528,128]{1,0:T(8,128)(2,1)S(1)}, u32[]{:S(2)}, u32[]{:S(2)}) collective-permute-start(bf16[528,128]{1,0:T(8,128)(2,1)S(1)} %compose.1), channel_id=1, source_target_pairs={{0,16},{4,20},{8,24},{12,28},{16,0},{20,4},{24,8},{28,12},{1,17},{... | collective-permute-start | bytes 405512 | tf_op jit(solution)/shard_map/ppermute | solution.py:460
  20.8 0.5 collective-permute-start.1
  21.3 2.7 %attention.2.refs_0_ = bf16[256,512]{1,0:T(8,128)(2,1)S(1)} custom-call(s32[4]{0:T(128)} %refs_0_.6, s32[32]{0:T(128)} %refs_1_.7, bf16[256,1024]{1,0:T(8,128)(2,1)} %refs_2_.6, bf16[2,256,256]{2,1,0:T(8,128)(2,1)S(1)} %pad_maximum_fusion.refs_3_, bf16[2,256,256]{2,1,0:T(8,128)(2,1)S(1)} %collective-permute-done.4.refs_4_, ...), custom_call_target="tpu_custom_call" | custom-call | flops 10737418240 | bytes 4194304 | tf_op jit(solution)/shard_map/attention/pallas_call | solution.py:52
  24.1 1.1 %collective-permute-done.3.refs_8_ = bf16[528,128]{1,0:T(8,128)(2,1)S(1)} collective-permute-done((bf16[528,128]{1,0:T(8,128)(2,1)S(1)}, bf16[528,128]{1,0:T(8,128)(2,1)S(1)}, u32[]{:S(2)}, u32[]{:S(2)}) %collective-permute-start.3) | collective-permute-done | bytes 135200 | tf_op jit(solution)/shard_map/ppermute | solution.py:460
  25.1 2.5 %collective-permute-done.2.refs_6_ = bf16[528,128]{1,0:T(8,128)(2,1)S(1)} collective-permute-done((bf16[528,128]{1,0:T(8,128)(2,1)S(1)}, bf16[528,128]{1,0:T(8,128)(2,1)S(1)}, u32[]{:S(2)}, u32[]{:S(2)}) %collective-permute-start.2) | collective-permute-done | bytes 135200 | tf_op jit(solution)/shard_map/ppermute | solution.py:460
  28.2 2.7 %attention.3.refs_1_ = bf16[256,512]{1,0:T(8,128)(2,1)S(1)} custom-call(s32[4]{0:T(128)} %refs_0_.6, s32[32]{0:T(128)} %refs_1_.7, bf16[256,1024]{1,0:T(8,128)(2,1)} %refs_2_.6, bf16[2,256,256]{2,1,0:T(8,128)(2,1)S(1)} %pad_maximum_fusion.refs_3_, bf16[2,256,256]{2,1,0:T(8,128)(2,1)S(1)} %collective-permute-done.4.refs_4_, ...), custom_call_target="tpu_custom_call" | custom-call | flops 10737418240 | bytes 4194304 | tf_op jit(solution)/shard_map/attention/pallas_call | solution.py:52
  30.9 2.4 %finish.1.refs_2_ = bf16[256,1024]{1,0:T(8,128)(2,1)S(1)} custom-call(bf16[256,256]{1,0:T(8,128)(2,1)} %refs_0_.7, f32[256,1024]{1,0:T(8,128)S(1)} %get-tuple-element.46.refs_1_, f32[256,8]{1,0:T(8,128)S(1)} %get-tuple-element.47.refs_2_, bf16[2,528,128]{2,1,0:T(8,128)(2,1)S(1)} %collective-permute-done.other_ref.refs_3_, ...), custom_call_target="tpu_custom_call" | custom-call | tf_op jit(solution)/shard_map/finish/pallas_call | solution.py:52
  33.4 1.2 %project.2 = (bf16[128,1024]{1,0:T(8,128)(2,1)S(1)}, f32[128,1024]{1,0:T(8,128)S(1)}) custom-call(bf16[256,512]{1,0:T(8,128)(2,1)S(1)} %attention.2.refs_0_, bf16[256,512]{1,0:T(8,128)(2,1)S(1)} %attention.3.refs_1_, bf16[256,1024]{1,0:T(8,128)(2,1)S(1)} %finish.1.refs_2_, bf16[1024,4096]{1,0:T(8,128)(2,1)S(1)} %get-tuple-element.43.refs_11_.refs_3_, ...), custom_call_target="tpu_custom_call" | custom-call | flops 1073741824 | bytes 1572864 | tf_op jit(solution)/shard_map/project/pallas_call | solution.py:423
  34.6 1.6 %collective-permute-start.14 = (bf16[128,1024]{1,0:T(8,128)(2,1)S(1)}, bf16[128,1024]{1,0:T(8,128)(2,1)S(1)}, u32[]{:S(2)}, u32[]{:S(2)}) collective-permute-start(bf16[128,1024]{1,0:T(8,128)(2,1)S(1)} %get-tuple-element.52), channel_id=1, source_target_pairs={{0,1},{1,0},{2,3},{3,2},{4,5},{5,4},{6,7},{7,6},{8,9},{9,8},{10,11... | collective-permute-start | bytes 786440 | tf_op jit(solution)/shard_map/ppermute | solution.py:499
  36.3 3.4 %project.3 = (bf16[128,1024]{1,0:T(8,128)(2,1)S(1)}, f32[128,1024]{1,0:T(8,128)S(1)}, bf16[128,1024]{1,0:T(8,128)(2,1)S(1)}, f32[128,1024]{1,0:T(8,128)S(1)}, bf...) custom-call(bf16[256,512]{1,0:T(8,128)(2,1)S(1)} %attention.2.refs_0, ...), custom_call_target="tpu_custom_call" | custom-call | flops 3221225472 | bytes 4718592 | tf_op jit(solution)/shard_map/project/pallas_call | solution.py:423
  39.7 0.5 collective-permute-start.16
  40.2 1.6 %collective-permute-start.20 = (bf16[128,512]{1,0:T(8,128)(2,1)S(1)}, bf16[128,512]{1,0:T(8,128)(2,1)S(1)}, u32[]{:S(2)}, u32[]{:S(2)}) collective-permute-start(bf16[128,512]{1,0:T(8,128)(2,1)S(1)} %get-tuple-element.60), channel_id=1, source_target_pairs={{0,1},{1,0},{2,3},{3,2},{4,5},{5,4},{6,7},{7,6},{8,9},{9,8},{10,11... | collective-permute-start | bytes 393224 | tf_op jit(solution)/shard_map/ppermute | solution.py:499
  42.2 1.6 %collective-permute-start.18 = (bf16[128,1024]{1,0:T(8,128)(2,1)S(1)}, bf16[128,1024]{1,0:T(8,128)(2,1)S(1)}, u32[]{:S(2)}, u32[]{:S(2)}) collective-permute-start(bf16[128,1024]{1,0:T(8,128)(2,1)S(1)} %get-tuple-element.57), channel_id=1, source_target_pairs={{0,1},{1,0},{2,3},{3,2},{4,5},{5,4},{6,7},{7,6},{8,9},{9,8},{10,11... | collective-permute-start | bytes 786440 | tf_op jit(solution)/shard_map/ppermute | solution.py:499
  43.9 2.7 %collective-permute-start.15 = (bf16[64,1024]{1,0:T(8,128)(2,1)S(1)}, bf16[64,1024]{1,0:T(8,128)(2,1)S(1)}, u32[]{:S(2)}, u32[]{:S(2)}) collective-permute-start(bf16[64,1024]{1,0:T(8,128)(2,1)S(1)} %slice.87), channel_id=1, source_target_pairs={{0,2},{1,3},{2,0},{3,1},{4,6},{5,7},{6,4},{7,5},{8,10},{9,11},{10,... | collective-permute-start | bytes 393224 | tf_op jit(solution)/shard_map/ppermute | solution.py:508
  46.5 5.6 %collective-permute-done.16 = bf16[128,1024]{1,0:T(8,128)(2,1)S(1)} collective-permute-done((bf16[128,1024]{1,0:T(8,128)(2,1)S(1)}, bf16[128,1024]{1,0:T(8,128)(2,1)S(1)}, u32[]{:S(2)}, u32[]{:S(2)}) %collective-permute-start.16) | collective-permute-done | bytes 262176 | tf_op jit(solution)/shard_map/ppermute | solution.py:499
  52.2 1.8 %collective-permute-start.17 = (bf16[64,1024]{1,0:T(8,128)(2,1)S(1)}, bf16[64,1024]{1,0:T(8,128)(2,1)S(1)}, u32[]{:S(2)}, u32[]{:S(2)}) collective-permute-start(bf16[64,1024]{1,0:T(8,128)(2,1)S(1)} %slice.86), channel_id=1, source_target_pairs={{0,2},{1,3},{2,0},{3,1},{4,6},{5,7},{6,4},{7,5},{8,10},{9,11},{10,... | collective-permute-start | bytes 393224 | tf_op jit(solution)/shard_map/ppermute | solution.py:508
  54.0 12.2 %collective-permute-done.18 = bf16[128,1024]{1,0:T(8,128)(2,1)S(1)} collective-permute-done((bf16[128,1024]{1,0:T(8,128)(2,1)S(1)}, bf16[128,1024]{1,0:T(8,128)(2,1)S(1)}, u32[]{:S(2)}, u32[]{:S(2)}) %collective-permute-start.18) | collective-permute-done | bytes 262176 | tf_op jit(solution)/shard_map/ppermute | solution.py:499
  66.3 1.8 %collective-permute-start.19 = (bf16[64,1024]{1,0:T(8,128)(2,1)S(1)}, bf16[64,1024]{1,0:T(8,128)(2,1)S(1)}, u32[]{:S(2)}, u32[]{:S(2)}) collective-permute-start(bf16[64,1024]{1,0:T(8,128)(2,1)S(1)} %slice.85), channel_id=1, source_target_pairs={{0,2},{1,3},{2,0},{3,1},{4,6},{5,7},{6,4},{7,5},{8,10},{9,11},{10,... | collective-permute-start | bytes 393224 | tf_op jit(solution)/shard_map/ppermute | solution.py:508
  68.1 1.3 %collective-permute-start.21 = (bf16[64,512]{1,0:T(8,128)(2,1)S(1)}, bf16[64,512]{1,0:T(8,128)(2,1)S(1)}, u32[]{:S(2)}, u32[]{:S(2)}) collective-permute-start(bf16[64,512]{1,0:T(8,128)(2,1)S(1)} %slice.89), channel_id=1, source_target_pairs={{0,2},{1,3},{2,0},{3,1},{4,6},{5,7},{6,4},{7,5},{8,10},{9,11},{10,... | collective-permute-start | bytes 196616 | tf_op jit(solution)/shard_map/ppermute | solution.py:508
  69.5 1.8 %collective-permute-start.23 = (bf16[64,512]{1,0:T(8,128)(2,1)S(1)}, bf16[64,512]{1,0:T(8,128)(2,1)S(1)}, u32[]{:S(2)}, u32[]{:S(2)}) collective-permute-start(bf16[64,512]{1,0:T(8,128)(2,1)S(1)} %slice.88), channel_id=1, source_target_pairs={{0,2},{1,3},{2,0},{3,1},{4,6},{5,7},{6,4},{7,5},{8,10},{9,11},{10,... | collective-permute-start | bytes 196616 | tf_op jit(solution)/shard_map/ppermute | solution.py:508
  71.3 7.9 %collective-permute-done.19 = bf16[64,1024]{1,0:T(8,128)(2,1)S(1)} collective-permute-done((bf16[64,1024]{1,0:T(8,128)(2,1)S(1)}, bf16[64,1024]{1,0:T(8,128)(2,1)S(1)}, u32[]{:S(2)}, u32[]{:S(2)}) %collective-permute-start.19) | collective-permute-done | bytes 131104 | tf_op jit(solution)/shard_map/ppermute | solution.py:508
  79.2 1.2 %collective-permute-done.21 = bf16[64,512]{1,0:T(8,128)(2,1)S(1)} collective-permute-done((bf16[64,512]{1,0:T(8,128)(2,1)S(1)}, bf16[64,512]{1,0:T(8,128)(2,1)S(1)}, u32[]{:S(2)}, u32[]{:S(2)}) %collective-permute-start.21) | collective-permute-done | bytes 65568 | tf_op jit(solution)/shard_map/ppermute | solution.py:508
  80.5 0.7 collective-permute-done.23
  81.3 0.6 fusion.9
  (42 shorter events, 2.7 us)
Async XLA Ops:
  1.0 13.9 %collective-permute-start.7 = (bf16[2,256,256]{2,1,0:T(8,128)(2,1)S(1)}, bf16[2,256,256]{2,1,0:T(8,128)(2,1)S(1)}, u32[]{:S(2)}, u32[]{:S(2)}) collective-permute-start(bf16[2,256,256]{2,1,0:T(8,128)(2,1)S(1)} %pad_maximum_fusion.refs_3_), channel_id=1, source_target_pairs={{0,24},{4,28},{8,16},{12,20},{16,8},{20,12},{24,0},{28,4},{1,25},{... | collective-permute-start | bytes 786440 | tf_op jit(solution)/shard_map/ppermute | solution.py:460
  5.0 11.9 %collective-permute-start.6 = (bf16[2,256,256]{2,1,0:T(8,128)(2,1)S(1)}, bf16[2,256,256]{2,1,0:T(8,128)(2,1)S(1)}, u32[]{:S(2)}, u32[]{:S(2)}) collective-permute-start(bf16[2,256,256]{2,1,0:T(8,128)(2,1)S(1)} %pad_maximum_fusion.refs_3_), channel_id=1, source_target_pairs={{0,16},{4,20},{8,24},{12,28},{16,0},{20,4},{24,8},{28,12},{1,17},{... | collective-permute-start | bytes 786440 | tf_op jit(solution)/shard_map/ppermute | solution.py:460
  5.5 11.7 %collective-permute-start.5 = (bf16[2,256,256]{2,1,0:T(8,128)(2,1)S(1)}, bf16[2,256,256]{2,1,0:T(8,128)(2,1)S(1)}, u32[]{:S(2)}, u32[]{:S(2)}) collective-permute-start(bf16[2,256,256]{2,1,0:T(8,128)(2,1)S(1)} %pad_maximum_fusion.refs_3_), channel_id=1, source_target_pairs={{0,8},{4,12},{8,0},{12,4},{16,24},{20,28},{24,16},{28,20},{1,9},{5... | collective-permute-start | bytes 786440 | tf_op jit(solution)/shard_map/ppermute | solution.py:460
  8.4 9.3 %collective-permute-start = (bf16[2,528,128]{2,1,0:T(8,128)(2,1)S(1)}, bf16[2,528,128]{2,1,0:T(8,128)(2,1)S(1)}, u32[]{:S(2)}, u32[]{:S(2)}) collective-permute-start(bf16[2,528,128]{2,1,0:T(8,128)(2,1)S(1)} %get-tuple-element.36.mine_ref.refs_0_), channel_id=1, source_target_pairs={{0,4},{4,0},{8,12},{12,8},{16,20},{20,16},{24,28},{28,24},{1,5},{5... | collective-permute-start | bytes 811016 | tf_op jit(solution)/shard_map/ppermute | solution.py:463
  8.4 10.9 %collective-permute-start.4 = (bf16[2,256,256]{2,1,0:T(8,128)(2,1)S(1)}, bf16[2,256,256]{2,1,0:T(8,128)(2,1)S(1)}, u32[]{:S(2)}, u32[]{:S(2)}) collective-permute-start(bf16[2,256,256]{2,1,0:T(8,128)(2,1)S(1)} %pad_maximum_fusion.refs_3_), channel_id=1, source_target_pairs={{0,4},{4,0},{8,12},{12,8},{16,20},{20,16},{24,28},{28,24},{1,5},{5... | collective-permute-start | bytes 786440 | tf_op jit(solution)/shard_map/ppermute | solution.py:463
  17.2 3.6 %collective-permute-start.8 = (bf16[2,256,256]{2,1,0:T(8,128)(2,1)S(1)}, bf16[2,256,256]{2,1,0:T(8,128)(2,1)S(1)}, u32[]{:S(2)}, u32[]{:S(2)}) collective-permute-start(bf16[2,256,256]{2,1,0:T(8,128)(2,1)S(1)} %collective-permute-done.5.refs_5_), channel_id=1, source_target_pairs={{0,4},{4,0},{8,12},{12,8},{16,20},{20,16},{24,28},{28,24},{1,5},{5... | collective-permute-start | bytes 786440 | tf_op jit(solution)/shard_map/ppermute | solution.py:463
  17.2 4.1 %collective-permute-start.9 = (bf16[2,256,256]{2,1,0:T(8,128)(2,1)S(1)}, bf16[2,256,256]{2,1,0:T(8,128)(2,1)S(1)}, u32[]{:S(2)}, u32[]{:S(2)}) collective-permute-start(bf16[2,256,256]{2,1,0:T(8,128)(2,1)S(1)} %collective-permute-done.6.refs_7_), channel_id=1, source_target_pairs={{0,4},{4,0},{8,12},{12,8},{16,20},{20,16},{24,28},{28,24},{1,5},{5... | collective-permute-start | bytes 786440 | tf_op jit(solution)/shard_map/ppermute | solution.py:463
  17.7 3.6 %collective-permute-start.10 = (bf16[2,256,256]{2,1,0:T(8,128)(2,1)S(1)}, bf16[2,256,256]{2,1,0:T(8,128)(2,1)S(1)}, u32[]{:S(2)}, u32[]{:S(2)}) collective-permute-start(bf16[2,256,256]{2,1,0:T(8,128)(2,1)S(1)} %collective-permute-done.7.refs_9_), channel_id=1, source_target_pairs={{0,4},{4,0},{8,12},{12,8},{16,20},{20,16},{24,28},{28,24},{1,5},{5... | collective-permute-start | bytes 786440 | tf_op jit(solution)/shard_map/ppermute | solution.py:463
  17.8 7.4 %collective-permute-start.3 = (bf16[528,128]{1,0:T(8,128)(2,1)S(1)}, bf16[528,128]{1,0:T(8,128)(2,1)S(1)}, u32[]{:S(2)}, u32[]{:S(2)}) collective-permute-start(bf16[528,128]{1,0:T(8,128)(2,1)S(1)} %compose.1), channel_id=1, source_target_pairs={{0,24},{4,28},{8,16},{12,20},{16,8},{20,12},{24,0},{28,4},{1,25},{... | collective-permute-start | bytes 405512 | tf_op jit(solution)/shard_map/ppermute | solution.py:460
  19.4 8.3 %collective-permute-start.2 = (bf16[528,128]{1,0:T(8,128)(2,1)S(1)}, bf16[528,128]{1,0:T(8,128)(2,1)S(1)}, u32[]{:S(2)}, u32[]{:S(2)}) collective-permute-start(bf16[528,128]{1,0:T(8,128)(2,1)S(1)} %compose.1), channel_id=1, source_target_pairs={{0,16},{4,20},{8,24},{12,28},{16,0},{20,4},{24,8},{28,12},{1,17},{... | collective-permute-start | bytes 405512 | tf_op jit(solution)/shard_map/ppermute | solution.py:460
  20.8 6.8 %collective-permute-start.1 = (bf16[528,128]{1,0:T(8,128)(2,1)S(1)}, bf16[528,128]{1,0:T(8,128)(2,1)S(1)}, u32[]{:S(2)}, u32[]{:S(2)}) collective-permute-start(bf16[528,128]{1,0:T(8,128)(2,1)S(1)} %compose.1), channel_id=1, source_target_pairs={{0,8},{4,12},{8,0},{12,4},{16,24},{20,28},{24,16},{28,20},{1,9},{5... | collective-permute-start | bytes 405512 | tf_op jit(solution)/shard_map/ppermute | solution.py:460
  27.6 3.3 %collective-permute-start.11 = (bf16[528,128]{1,0:T(8,128)(2,1)S(1)}, bf16[528,128]{1,0:T(8,128)(2,1)S(1)}, u32[]{:S(2)}, u32[]{:S(2)}) collective-permute-start(bf16[528,128]{1,0:T(8,128)(2,1)S(1)} %collective-permute-done.1.refs_4_), channel_id=1, source_target_pairs={{0,4},{4,0},{8,12},{12,8},{16,20},{20,16},{24,28},{28,24},{1,5},{5... | collective-permute-start | bytes 405512 | tf_op jit(solution)/shard_map/ppermute | solution.py:463
  27.7 3.3 %collective-permute-start.12 = (bf16[528,128]{1,0:T(8,128)(2,1)S(1)}, bf16[528,128]{1,0:T(8,128)(2,1)S(1)}, u32[]{:S(2)}, u32[]{:S(2)}) collective-permute-start(bf16[528,128]{1,0:T(8,128)(2,1)S(1)} %collective-permute-done.2.refs_6_), channel_id=1, source_target_pairs={{0,4},{4,0},{8,12},{12,8},{16,20},{20,16},{24,28},{28,24},{1,5},{5... | collective-permute-start | bytes 405512 | tf_op jit(solution)/shard_map/ppermute | solution.py:463
  28.1 2.8 %collective-permute-start.13 = (bf16[528,128]{1,0:T(8,128)(2,1)S(1)}, bf16[528,128]{1,0:T(8,128)(2,1)S(1)}, u32[]{:S(2)}, u32[]{:S(2)}) collective-permute-start(bf16[528,128]{1,0:T(8,128)(2,1)S(1)} %collective-permute-done.3.refs_8_), channel_id=1, source_target_pairs={{0,4},{4,0},{8,12},{12,8},{16,20},{20,16},{24,28},{28,24},{1,5},{5... | collective-permute-start | bytes 405512 | tf_op jit(solution)/shard_map/ppermute | solution.py:463
  34.6 9.2 %collective-permute-start.14 = (bf16[128,1024]{1,0:T(8,128)(2,1)S(1)}, bf16[128,1024]{1,0:T(8,128)(2,1)S(1)}, u32[]{:S(2)}, u32[]{:S(2)}) collective-permute-start(bf16[128,1024]{1,0:T(8,128)(2,1)S(1)} %get-tuple-element.52), channel_id=1, source_target_pairs={{0,1},{1,0},{2,3},{3,2},{4,5},{5,4},{6,7},{7,6},{8,9},{9,8},{10,11... | collective-permute-start | bytes 786440 | tf_op jit(solution)/shard_map/ppermute | solution.py:499
  39.7 12.5 %collective-permute-start.16 = (bf16[128,1024]{1,0:T(8,128)(2,1)S(1)}, bf16[128,1024]{1,0:T(8,128)(2,1)S(1)}, u32[]{:S(2)}, u32[]{:S(2)}) collective-permute-start(bf16[128,1024]{1,0:T(8,128)(2,1)S(1)} %get-tuple-element.54), channel_id=1, source_target_pairs={{0,1},{1,0},{2,3},{3,2},{4,5},{5,4},{6,7},{7,6},{8,9},{9,8},{10,11... | collective-permute-start | bytes 786440 | tf_op jit(solution)/shard_map/ppermute | solution.py:499
  40.2 27.9 %collective-permute-start.20 = (bf16[128,512]{1,0:T(8,128)(2,1)S(1)}, bf16[128,512]{1,0:T(8,128)(2,1)S(1)}, u32[]{:S(2)}, u32[]{:S(2)}) collective-permute-start(bf16[128,512]{1,0:T(8,128)(2,1)S(1)} %get-tuple-element.60), channel_id=1, source_target_pairs={{0,1},{1,0},{2,3},{3,2},{4,5},{5,4},{6,7},{7,6},{8,9},{9,8},{10,11... | collective-permute-start | bytes 393224 | tf_op jit(solution)/shard_map/ppermute | solution.py:499
  41.8 27.6 %collective-permute-start.22 = (bf16[128,512]{1,0:T(8,128)(2,1)S(1)}, bf16[128,512]{1,0:T(8,128)(2,1)S(1)}, u32[]{:S(2)}, u32[]{:S(2)}) collective-permute-start(bf16[128,512]{1,0:T(8,128)(2,1)S(1)} %get-tuple-element.63), channel_id=1, source_target_pairs={{0,1},{1,0},{2,3},{3,2},{4,5},{5,4},{6,7},{7,6},{8,9},{9,8},{10,11... | collective-permute-start | bytes 393224 | tf_op jit(solution)/shard_map/ppermute | solution.py:499
  42.2 24.0 %collective-permute-start.18 = (bf16[128,1024]{1,0:T(8,128)(2,1)S(1)}, bf16[128,1024]{1,0:T(8,128)(2,1)S(1)}, u32[]{:S(2)}, u32[]{:S(2)}) collective-permute-start(bf16[128,1024]{1,0:T(8,128)(2,1)S(1)} %get-tuple-element.57), channel_id=1, source_target_pairs={{0,1},{1,0},{2,3},{3,2},{4,5},{5,4},{6,7},{7,6},{8,9},{9,8},{10,11... | collective-permute-start | bytes 786440 | tf_op jit(solution)/shard_map/ppermute | solution.py:499
  43.9 27.4 %collective-permute-start.15 = (bf16[64,1024]{1,0:T(8,128)(2,1)S(1)}, bf16[64,1024]{1,0:T(8,128)(2,1)S(1)}, u32[]{:S(2)}, u32[]{:S(2)}) collective-permute-start(bf16[64,1024]{1,0:T(8,128)(2,1)S(1)} %slice.87), channel_id=1, source_target_pairs={{0,2},{1,3},{2,0},{3,1},{4,6},{5,7},{6,4},{7,5},{8,10},{9,11},{10,... | collective-permute-start | bytes 393224 | tf_op jit(solution)/shard_map/ppermute | solution.py:508
  52.2 19.0 %collective-permute-start.17 = (bf16[64,1024]{1,0:T(8,128)(2,1)S(1)}, bf16[64,1024]{1,0:T(8,128)(2,1)S(1)}, u32[]{:S(2)}, u32[]{:S(2)}) collective-permute-start(bf16[64,1024]{1,0:T(8,128)(2,1)S(1)} %slice.86), channel_id=1, source_target_pairs={{0,2},{1,3},{2,0},{3,1},{4,6},{5,7},{6,4},{7,5},{8,10},{9,11},{10,... | collective-permute-start | bytes 393224 | tf_op jit(solution)/shard_map/ppermute | solution.py:508
  66.3 12.9 %collective-permute-start.19 = (bf16[64,1024]{1,0:T(8,128)(2,1)S(1)}, bf16[64,1024]{1,0:T(8,128)(2,1)S(1)}, u32[]{:S(2)}, u32[]{:S(2)}) collective-permute-start(bf16[64,1024]{1,0:T(8,128)(2,1)S(1)} %slice.85), channel_id=1, source_target_pairs={{0,2},{1,3},{2,0},{3,1},{4,6},{5,7},{6,4},{7,5},{8,10},{9,11},{10,... | collective-permute-start | bytes 393224 | tf_op jit(solution)/shard_map/ppermute | solution.py:508
  68.1 12.4 %collective-permute-start.21 = (bf16[64,512]{1,0:T(8,128)(2,1)S(1)}, bf16[64,512]{1,0:T(8,128)(2,1)S(1)}, u32[]{:S(2)}, u32[]{:S(2)}) collective-permute-start(bf16[64,512]{1,0:T(8,128)(2,1)S(1)} %slice.89), channel_id=1, source_target_pairs={{0,2},{1,3},{2,0},{3,1},{4,6},{5,7},{6,4},{7,5},{8,10},{9,11},{10,... | collective-permute-start | bytes 196616 | tf_op jit(solution)/shard_map/ppermute | solution.py:508
  69.5 11.7 %collective-permute-start.23 = (bf16[64,512]{1,0:T(8,128)(2,1)S(1)}, bf16[64,512]{1,0:T(8,128)(2,1)S(1)}, u32[]{:S(2)}, u32[]{:S(2)}) collective-permute-start(bf16[64,512]{1,0:T(8,128)(2,1)S(1)} %slice.88), channel_id=1, source_target_pairs={{0,2},{1,3},{2,0},{3,1},{4,6},{5,7},{6,4},{7,5},{8,10},{9,11},{10,... | collective-permute-start | bytes 196616 | tf_op jit(solution)/shard_map/ppermute | solution.py:508
  80.5 0.8 copy-start

commit v3 on v2

--- a/solution.py
+++ b/solution.py
@@ -12,7 +12,7 @@
 STATE = 128
 LOG2E = 1.4426950408889634
 LOW = -1e30
-SHARES = (2, 2, 2, 1, 1)
+SHARES = (2, 2, 2, 2)
 F32 = jnp.float32
 BF16 = jnp.bfloat16
 
@@ -57,7 +57,7 @@
         scratch_shapes=[
             *scratch,
             *(f.scratch for f in far),
-            pltpu.SemaphoreType.DMA((len(far),)),
+            pltpu.SemaphoreType.DMA((max(len(far), 1),)),
         ],
         compiler_params=pltpu.CompilerParams(vmem_limit_bytes=room),
         cost_estimate=pl.CostEstimate(flops=flops, bytes_accessed=moved, transcendentals=exps),
@@ -81,8 +81,7 @@
 
 
 def row_slot(part, z):
-    d = part ^ z
-    return jnp.where(d == 1, 0, jnp.where(d == 3, 1, jnp.where(d == 0, 2, 3)))
+    return 3 - (part ^ z)
 
 
 def nt(a, b):
@@ -184,7 +183,7 @@
 
 
 def finish_kernel(r_ref, base_ref, eg_ref, st_ref, *refs):
-    *got, out_ref, held = refs
+    *got, out_ref, held, carry = refs
     me = lax.axis_index("ctx")
     core, chip = me & 1, me // 2
     z = lax.axis_index("tp")
@@ -198,22 +197,30 @@
     for j in range(1, held.shape[0]):
         held[chip ^ j, core] = got[2 * j - 2][...]
         held[chip ^ j, core ^ 1] = got[2 * j - 1][...]
+    carry[...] = jnp.zeros_like(carry)
+
+    def where(h):
+        c, i = divmod(h, half)
+        return c, slice(i * STATE, (i + 1) * STATE), slice(state_rows + i, state_rows + i + 1)
+
+    def one(k, _):
+        for h in range(heads):
+            c, hs, gs = where(h)
+            carry[h] = held[k, c, gs, :].astype(F32) * carry[h] + held[k, c, hs, :].astype(F32)
+        return 0
+
+    lax.fori_loop(0, chip, one, 0)
+
+    @pl.when(core == 1)
+    def _():
+        for h in range(heads):
+            c, hs, gs = where(h)
+            carry[h] = st_ref[c, gs, :].astype(F32) * carry[h] + st_ref[c, hs, :].astype(F32)
 
     for h in range(heads):
-        c, i = divmod(h, half)
-        hs = slice(i * STATE, (i + 1) * STATE)
-        gs = slice(state_rows + i, state_rows + i + 1)
-
-        def one(k, carry):
-            return held[k, c, gs, :].astype(F32) * carry + held[k, c, hs, :].astype(F32)
-
-        entering = lax.fori_loop(0, chip, one, jnp.zeros((STATE, SSM_HEAD_DIM), F32))
-        prev = st_ref[c, hs, :].astype(F32)
-        gain = st_ref[c, gs, :].astype(F32)
-        carry = jnp.where(core == 1, gain * entering + prev, entering).astype(BF16)
         hc = slice(h * SSM_HEAD_DIM, (h + 1) * SSM_HEAD_DIM)
         g = h // per_group
-        inter = nn(r_ref[:, g * STATE : (g + 1) * STATE], carry)
+        inter = nn(r_ref[:, g * STATE : (g + 1) * STATE], carry[h].astype(BF16))
         res = (base_ref[:, hc] + eg_ref[:, h : h + 1] * inter).astype(BF16)
         for q in range(4):
             at = pl.multiple_of(row_slot(q, z) * part, part)
@@ -222,145 +229,160 @@
 
 def finish(base, r, eg, st_other, got):
     chips = len(got) // 2 + 1
+    heads = base.shape[1] // SSM_HEAD_DIM
     return one_step(
         finish_kernel,
         "finish",
         (jax.ShapeDtypeStruct(base.shape, BF16),),
-        (Far(r),),
-        (base, eg, st_other, *got),
-        scratch=[pltpu.VMEM((chips, 2) + got[0].shape, BF16)],
+        (),
+        (r, base, eg, st_other, *got),
+        scratch=[
+            pltpu.VMEM((chips, 2) + got[0].shape, BF16),
+            pltpu.VMEM((heads, STATE, SSM_HEAD_DIM), F32),
+        ],
         room=(4 + chips) * MIB,
     )[0]
 
 
-def attention_kernel(page_len, kv_head, len_ref, table_ref, q_ref, *refs):
-    *got, _, _, out_ref, inv, kv, sem, sc, mx, ls, acc = refs
+def attention_kernel(page_len, together, len_ref, table_ref, q_ref, *refs):
+    *got, weight_ref, out_ref, ready_ref, inv, kv, sc, mx, ls, acc, weight_sem = refs
+    pieces = weight_sem.shape[0]
+    depth = weight_ref.shape[0] // pieces
+    fetches = []
+    for i in range(pieces):
+        here = slice(i * depth, (i + 1) * depth)
+        fetches.append(
+            pltpu.make_async_copy(weight_ref.at[here], ready_ref.at[here], weight_sem.at[i])
+        )
+    for f in fetches:
+        f.start()
     me = lax.axis_index("ctx")
     z = lax.axis_index("tp")
     rows = q_ref.shape[0]
     part = rows // 4
     heads = q_ref.shape[1] // HEAD_DIM
-    lanes = slice(kv_head * HEAD_DIM, (kv_head + 1) * HEAD_DIM)
+    group = heads // (kv.shape[2] // HEAD_DIM)
     first = me * rows
     ends = doc_ends_of(len_ref)
     start0 = 0
     for end in ends:
         start0 = jnp.where(first >= end, end, start0)
     low_block = start0 // rows
-    pages_block = rows // page_len
 
     def invert(l, _):
         inv[table_ref[l]] = l
         return 0
 
-    lax.fori_loop(0, table_ref.shape[0], invert, 0)
-    low_page, high_page = low_block * pages_block, (me + 1) * pages_block
-
-    def page_copy(ref, slot, page):
-        here = pl.ds(slot * page_len, page_len)
-        there = pl.ds(pl.multiple_of(page * page_len, page_len), page_len)
-        return pltpu.make_async_copy(ref.at[:, here, lanes], kv.at[:, there, :], sem.at[page])
-
+    lax.fori_loop(0, table_ref.shape[0], invert, 0, unroll=8)
     for j, ref in enumerate(got):
-        for slot in range(ref.shape[1] // page_len):
-            page = inv[(me ^ j) * (ref.shape[1] // page_len) + slot]
-
-            @pl.when((page >= low_page) & (page < high_page))
-            def _():
-                page_copy(ref, slot, page).start()
+        pages = ref.shape[1] // page_len
+        for slot in range(pages):
+            page = inv[(me ^ j) * pages + slot]
+            there = pl.ds(pl.multiple_of(page * page_len, page_len), page_len)
+            here = slice(slot * page_len, (slot + 1) * page_len)
+            for i in range(2):
+                kv[i, there, :] = ref[i, here, :]
 
     t_pos = first + lax.broadcasted_iota(jnp.int32, (rows, 1), 0)
     t_start = doc_start(t_pos, ends)
     scale = LOG2E * HEAD_DIM ** (-0.5)
 
-    def scores(block, own):
-        for i in range(pages_block):
-            page_copy(got[0], 0, block * pages_block + i).wait()
-        at = pl.ds(pl.multiple_of(block * rows, rows), rows)
-        u_pos = block * rows + lax.broadcasted_iota(jnp.int32, (1, rows), 1)
-        shown = u_pos >= t_start
-        if own:
-            shown = shown & (u_pos <= t_pos)
-        for h in range(heads):
-            s = nt(
-                q_ref[:, h * HEAD_DIM : (h + 1) * HEAD_DIM],
-                kv[0, at, :],
-            )
-            s = jnp.where(shown, s * scale, LOW)
-            sc[block - low_block, h] = s
-            top = s[:, :128]
-            for k in range(128, rows, 128):
-                top = jnp.maximum(top, s[:, k : k + 128])
-            mx[h] = top if own else jnp.maximum(mx[h], top)
-
-    scores(me, True)
-
-    def earlier(block, _):
-        scores(block, False)
-        return 0
-
-    lax.fori_loop(low_block, me, earlier, 0)
-    for h in range(heads):
-        mx[h] = jnp.broadcast_to(jnp.max(mx[h], axis=1, keepdims=True), (rows, 128))
-    ls[...] = jnp.zeros_like(ls)
-    acc[...] = jnp.zeros_like(acc)
-
-    def weigh(block, _):
-        at = pl.ds(pl.multiple_of(block * rows, rows), rows)
-        for h in range(heads):
-            m = mx[h]
-            total = ls[h]
-            pieces = []
-            for k in range(0, rows, 128):
-                w = jnp.exp2(sc[block - low_block, h, :, k : k + 128] - m)
-                total = total + w
-                pieces.append(w.astype(BF16))
-            ls[h] = total
-            acc[h] += nn(
-                jnp.concatenate(pieces, axis=1), kv[1, at, :]
-            )
-        return 0
-
-    lax.fori_loop(low_block, me + 1, weigh, 0)
-    for h in range(heads):
-        res = (acc[h] / jnp.sum(ls[h], axis=1, keepdims=True)).astype(BF16)
-        for q in range(4):
-            at = pl.multiple_of(row_slot(q, z) * part, part)
-            out_ref[pl.ds(at, part), h * HEAD_DIM : (h + 1) * HEAD_DIM] = res[
-                q * part : (q + 1) * part
-            ]
-
-
-def attention(page_len, doc_lengths, page_table, queries, got, ready, kv_head, kv_heads):
+    def lanes(h):
+        return slice(h // group * HEAD_DIM, (h // group + 1) * HEAD_DIM)
+
+    for h0 in range(0, heads, together):
+        some = range(h0, h0 + together)
+
+        def scores(block, own):
+            at = pl.ds(pl.multiple_of(block * rows, rows), rows)
+            u_pos = block * rows + lax.broadcasted_iota(jnp.int32, (1, rows), 1)
+            shown = u_pos >= t_start
+            if own:
+                shown = shown & (u_pos <= t_pos)
+            for h in some:
+                s = nt(q_ref[:, h * HEAD_DIM : (h + 1) * HEAD_DIM], kv[0, at, lanes(h)])
+                s = jnp.where(shown, s * scale, LOW)
+                sc[block - low_block, h - h0] = s
+                top = s[:, :128]
+                for k in range(128, rows, 128):
+                    top = jnp.maximum(top, s[:, k : k + 128])
+                mx[h - h0] = top if own else jnp.maximum(mx[h - h0], top)
+
+        scores(me, True)
+
+        def earlier(block, _):
+            scores(block, False)
+            return 0
+
+        lax.fori_loop(low_block, me, earlier, 0)
+        for i in range(together):
+            mx[i] = jnp.broadcast_to(jnp.max(mx[i], axis=1, keepdims=True), (rows, 128))
+
+        def weigh(block, own):
+            at = pl.ds(pl.multiple_of(block * rows, rows), rows)
+            for h in some:
+                i = h - h0
+                m = mx[i]
+                total, pieces = None, []
+                for k in range(0, rows, 128):
+                    w = jnp.exp2(sc[block - low_block, i, :, k : k + 128] - m)
+                    total = w if total is None else total + w
+                    pieces.append(w.astype(BF16))
+                term = nn(jnp.concatenate(pieces, axis=1), kv[1, at, lanes(h)])
+                ls[i] = total if own else ls[i] + total
+                acc[i] = term if own else acc[i] + term
+
+        weigh(me, True)
+
+        def weigh_earlier(block, _):
+            weigh(block, False)
+            return 0
+
+        lax.fori_loop(low_block, me, weigh_earlier, 0)
+        for h in some:
+            inverse = 1.0 / jnp.sum(ls[h - h0], axis=1, keepdims=True)
+            res = (acc[h - h0] * inverse).astype(BF16)
+            for q in range(4):
+                at = pl.multiple_of(row_slot(q, z) * part, part)
+                out_ref[pl.ds(at, part), h * HEAD_DIM : (h + 1) * HEAD_DIM] = res[
+                    q * part : (q + 1) * part
+                ]
+    for f in fetches:
+        f.wait()
+
+
+def attention(page_len, doc_lengths, page_table, queries, got, weight):
     rows = queries.shape[0]
-    width = queries.shape[1] // kv_heads
-    heads = width // HEAD_DIM
-    out = jax.ShapeDtypeStruct((rows, width), BF16)
+    heads = queries.shape[1] // HEAD_DIM
     keys = len(got) * got[0].shape[1]
+    width = got[0].shape[2]
     blocks = min(keys // rows, keys // 2 // rows + 1)
+    block_bytes = 4 * rows * rows * blocks
+    together = heads
+    while together > 1 and together * block_bytes > 12 * MIB:
+        together //= 2
     return one_step(
-        functools.partial(attention_kernel, page_len, kv_head),
+        functools.partial(attention_kernel, page_len, together),
         "attention",
-        (out,),
         (
-            Far(doc_lengths, pltpu.SMEM),
-            Far(page_table, pltpu.SMEM),
-            Far(queries, lanes=slice(kv_head * width, (kv_head + 1) * width)),
+            jax.ShapeDtypeStruct(queries.shape, BF16),
+            jax.ShapeDtypeStruct(weight.shape, weight.dtype),
         ),
-        (*got, *ready),
-        specs=[ANY_SPEC] * (len(got) + len(ready)),
+        (Far(doc_lengths, pltpu.SMEM), Far(page_table, pltpu.SMEM)),
+        (queries, *got, in_hbm(weight)),
+        specs=[VMEM_SPEC] * (1 + len(got)) + [HBM_SPEC],
         scratch=[
             pltpu.SMEM((page_table.shape[0],), jnp.int32),
-            pltpu.VMEM((2, keys, HEAD_DIM), BF16),
-            pltpu.SemaphoreType.DMA((page_table.shape[0],)),
-            pltpu.VMEM((blocks, heads, rows, rows), F32),
-            pltpu.VMEM((heads, rows, 128), F32),
-            pltpu.VMEM((heads, rows, 128), F32),
-            pltpu.VMEM((heads, rows, HEAD_DIM), F32),
+            pltpu.VMEM((2, keys, width), BF16),
+            pltpu.VMEM((blocks, together, rows, rows), F32),
+            pltpu.VMEM((together, rows, 128), F32),
+            pltpu.VMEM((together, rows, 128), F32),
+            pltpu.VMEM((together, rows, HEAD_DIM), F32),
+            pltpu.SemaphoreType.DMA((4,)),
         ],
-        cost=(64 * heads * rows * 1280 * 128, 4 << 20, heads * rows * 1280),
-        room=5 * MIB + 4 * heads * rows * rows * blocks + 4 * keys * HEAD_DIM,
-    )[0]
+        cost=(128 * heads * rows * 1280 * 128, 4 << 20, heads * rows * 1280),
+        room=6 * MIB + together * block_bytes + 4 * keys * width,
+    )
 
 
 def fetch_kernel(pieces, *refs):
@@ -398,42 +420,48 @@
     )(after, *(in_hbm(w) for w in weights))
 
 
-def project_kernel(start, tile, count, *refs):
-    att, (mix_ref, wa_ref, wm_ref), out = refs[:count], refs[count : count + 3], refs[count + 3 :]
-    for send_ref, keep_ref in zip(out[::2], out[1::2]):
-        sent, width = send_ref.shape
-        for j in range(0, width, tile):
-            here, there = slice(j, j + tile), slice(start + j, start + j + tile)
-            total = nn(mix_ref[...], wm_ref[:, there])
-            row = 0
-            for a in att:
-                total += nn(a[...], wa_ref[row : row + a.shape[1], there])
-                row += a.shape[1]
-            send_ref[:, here] = total[:sent].astype(BF16)
-            keep_ref[:, here] = total[sent:]
-        start += width
-
-
-def project(att, mix, wa, wm, start, widths, tile):
+def project_kernel(start, tile, joined, att_ref, mix_ref, wa_ref, wm_ref, *out):
+    *other, send_ref, keep_ref = out
+    part = keep_ref.shape[0]
+    at = 0
+    for keep_other in other[-1:] if joined else other[1::2]:
+        for j in range(0, keep_other.shape[1], tile):
+            here, there = slice(j, j + tile), slice(start + at, start + at + tile)
+            own = slice(at, at + tile)
+            total = nn(att_ref[...], wa_ref[:, there]) + nn(mix_ref[...], wm_ref[:, there])
+            through = total[:part].astype(BF16)
+            if joined:
+                send_ref[:part, own] = through
+                send_ref[part:, own] = total[2 * part : 3 * part].astype(BF16)
+            else:
+                other[2 * [o is keep_other for o in other[1::2]].index(True)][:, here] = through
+                send_ref[:, own] = total[2 * part : 3 * part].astype(BF16)
+            keep_other[:, here] = total[part : 2 * part]
+            keep_ref[:, own] = total[3 * part :]
+            at += tile
+
+
+def project(att, mix, wa, wm, start, widths, tile, joined):
     rows, depth = mix.shape
+    part, width = rows // 4, sum(widths)
     out_shape = []
-    for width in widths:
-        out_shape.append(jax.ShapeDtypeStruct((rows // 2, width), BF16))
-        out_shape.append(jax.ShapeDtypeStruct((rows // 2, width), F32))
-    out = pl.pallas_call(
-        functools.partial(project_kernel, start, tile, len(att)),
+    for w in widths:
+        if not joined:
+            out_shape.append(jax.ShapeDtypeStruct((part, w), BF16))
+        out_shape.append(jax.ShapeDtypeStruct((part, w), F32))
+    out_shape.append(jax.ShapeDtypeStruct((2 * part if joined else part, width), BF16))
+    out_shape.append(jax.ShapeDtypeStruct((part, width), F32))
+    return pl.pallas_call(
+        functools.partial(project_kernel, start, tile, joined),
         out_shape=tuple(out_shape),
-        in_specs=[VMEM_SPEC] * (len(att) + 3),
+        in_specs=[VMEM_SPEC] * 4,
         out_specs=(VMEM_SPEC,) * len(out_shape),
         compiler_params=pltpu.CompilerParams(vmem_limit_bytes=4 * MIB),
         cost_estimate=pl.CostEstimate(
-            flops=4 * rows * depth * sum(widths),
-            bytes_accessed=6 * rows * sum(widths),
-            transcendentals=0,
+            flops=4 * rows * depth * width, bytes_accessed=6 * rows * width, transcendentals=0
         ),
         name="project",
-    )(*att, mix, wa, wm)
-    return list(zip(out[::2], out[1::2]))
+    )(att, mix, wa, wm)
 
 
 def shards(
@@ -472,41 +500,64 @@
     )
     st_other = other_core(st)
     chip_state = compose(st, st_other)
-    ready = fetch(st, attention_weight, mixer_weight)
+    near_weight, near_queries, near_read = fetch(
+        st, attention_weight, queries, state_read
+    )
     far_states = [between_chips(chip_state, j) for j in range(1, chips)]
 
-    far[1:], ready = lax.optimization_barrier((far[1:], ready))
+    far[1:], near_queries = lax.optimization_barrier((far[1:], near_queries))
     got = []
     for a in far:
         got += [a, other_core(a)]
-    kv_heads = width // HEAD_DIM
-    att = [
-        attention(page_len, doc_lengths, page_table, queries, got, ready, i, kv_heads)
-        for i in range(kv_heads)
-    ]
-    *far_states, att[0] = lax.optimization_barrier((*far_states, att[0]))
+    att, far_weight = attention(
+        page_len, doc_lengths, page_table, near_queries, got, mixer_weight
+    )
+    *far_states, att = lax.optimization_barrier((*far_states, att))
     got_states = []
     for a in far_states:
         got_states += [a, other_core(a)]
-    mix = finish(base, state_read, eg, st_other, got_states)
+    mix = finish(base, near_read, eg, st_other, got_states)
 
     part = tok_rows // n_tp
     columns = attention_weight.shape[1]
     widths = [share * columns // 8 for share in SHARES]
-    sums = project(att, mix, *ready, 0, widths[:1], 256)
-    sums += project(att, mix, *ready, widths[0], widths[1:], 256)
-    kept = [
-        (keep, lax.ppermute(send, "tp", [(i, i ^ 1) for i in range(n_tp)])) for send, keep in sums
-    ]
-    pieces = []
-    order = None
-    for keep, near in kept:
+    weights = (near_weight, far_weight)
+
+    def neighbour(a):
+        return lax.ppermute(a, "tp", [(i, i ^ 1) for i in range(n_tp)])
+
+    def across(a):
+        return lax.ppermute(a, "tp", [(i, i ^ 2) for i in range(n_tp)])
+
+    keep_other, send, keep = project(att, mix, *weights, 0, widths[:1], 256, True)
+    send, mix = lax.optimization_barrier((send, mix))
+    *other, send_rest, keep_rest = project(
+        att, mix, *weights, widths[0], widths[1:], 256, False
+    )
+    near = neighbour(send)
+    near_other = [near[:part]] + [neighbour(a) for a in other[::2]]
+    keep_other = [keep_other] + other[1::2]
+    last, order = [], None
+    for k in range(len(widths)):
         if order is not None:
-            near, order = lax.optimization_barrier((near, order))
-        both = keep + near.astype(F32)
-        order = both[part:].astype(BF16)
-        last = lax.ppermute(order, "tp", [(i, i ^ 2) for i in range(n_tp)])
-        pieces.append((both[:part] + last.astype(F32)).astype(BF16))
+            near_other[k], order = lax.optimization_barrier((near_other[k], order))
+        both = keep_other[k] + near_other[k].astype(F32)
+
+        order = both.astype(BF16)
+        last.append(across(order))
+        if k == 99:
+            send_rest, order = lax.optimization_barrier((send_rest, order))
+    near_rest = neighbour(send_rest)
+    parts = [(keep, near[part:], last[0])]
+    at = 0
+    for a, width in zip(last[1:], widths[1:]):
+        parts.append((keep_rest[:, at : at + width], near_rest[:, at : at + width], a))
+        at += width
+    pieces, done = [], None
+    for a, b, c in parts:
+
+        done = (a + b.astype(F32) + c.astype(F32)).astype(BF16)
+        pieces.append(done)
     return jnp.concatenate(pieces, axis=1)
 
 

time: 82.2 us -> 73.6 us (0.90)
  Pallas kernels: 21.3 us -> 15.8 us
  starting transfers between devices: 24.8 us -> 23.2 us
  waiting for transfers between devices: 33.5 us -> 32.2 us
    ppermute x10 -> x9, waiting for transfers between devices: 27.6 us -> 23.8 us  [the longest x4 14.4 us: across(): return lax.ppermute(a, 'tp', [(i, i ^ 2) for i in range(n_tp)])]
    pallas_call x4 -> x3, Pallas kernels: 10.6 us -> 7.48 us  [one_step(): pl.pallas_call(body, out_shape=tuple(out_shape), in_specs=[HBM_SPEC] * le...]
    pallas_call x1, Pallas kernels: 5.92 us -> 3.59 us  [fetch(): pl.pallas_call(functools.partial(fetch_kernel, 4), out_shape=tuple((jax.S...]
    ppermute x10 -> x9, starting transfers between devices: 15 us -> 13.5 us  [the longest x4 7.74 us: across(): return lax.ppermute(a, 'tp', [(i, i ^ 2) for i in range(n_tp)])]
    ppermute x8, waiting for transfers between devices: 0.02 us -> 1.36 us  [other_core(): return lax.ppermute(a, 'ctx', [(i, i ^ 1) for i in range(n_ctx)])]
    ppermute x6, waiting for transfers between devices: 5.85 us -> 7.04 us  [between_chips(): return lax.ppermute(a, 'ctx', [(i, i ^ 2 * j) for i in range(n_ctx)])]
  transfers between devices with their start and end apart: 24 -> 23, of which waited for: 9 -> 11; matrix products, arithmetic and copies ran while one was open for 1% -> 0% of each run, Pallas kernels for 21% -> 19%
where the time goes in v3:
time: 73.6 us; the launch traced here: 73.5 us
  waiting for transfers between devices  32.2 us (44%)
  starting transfers between devices  23.2 us (32%)
  Pallas kernels  15.8 us (21%)
  other arithmetic  2.15 us (3%)
    ppermute x4, waiting for transfers between devices, across(): return lax.ppermute(a, 'tp', [(i, i ^ 2) for i in range(n_tp)])  14.4 us
    ppermute x5, waiting for transfers between devices, neighbour(): return lax.ppermute(a, 'tp', [(i, i ^ 1) for i in range(n_tp)])  9.39 us
    ppermute x6, starting transfers between devices, between_chips(): return lax.ppermute(a, 'ctx', [(i, i ^ 2 * j) for i in range(n_ctx)])  8.1 us
    ppermute x4, starting transfers between devices, across(): return lax.ppermute(a, 'tp', [(i, i ^ 2) for i in range(n_tp)])  7.74 us
    pallas_call x3, Pallas kernels, one_step(): pl.pallas_call(body, out_shape=tuple(out_shape), in_specs=[HBM_SPEC] * le...  7.48 us
    ppermute x6, waiting for transfers between devices, between_chips(): return lax.ppermute(a, 'ctx', [(i, i ^ 2 * j) for i in range(n_ctx)])  7.04 us
    ppermute x5, starting transfers between devices, neighbour(): return lax.ppermute(a, 'tp', [(i, i ^ 1) for i in range(n_tp)])  5.76 us
    pallas_call x2, Pallas kernels, project(): pl.pallas_call(functools.partial(project_kernel, start, tile, joined), ou...  4.65 us
  transfers between devices with their start and end apart: 23, of which 11 were waited for; matrix products, arithmetic and copies ran while one was open for 0% of the time, Pallas kernels for 19%

profile of v3, /device:TPU:0, one launch (start us, length us, event | category | flops | bytes accessed | tf_op | source)
XLA Modules:
  0.0 73.5 jit_solution(3097447780574026528)
XLA Ops:
  0.0 1.0 %pad_maximum_fusion.1.refs_3_ = bf16[2,256,256]{2,1,0:T(8,128)(2,1)S(1)} fusion(bf16[1,256,256]{2,1,0:T(8,128)(2,1)} %bitcast.2, bf16[1,256,256]{2,1,0:T(8,128)(2,1)} %bitcast.3), kind=kLoop, calls=%fused_computation.1 | loop fusion | flops 131072 | bytes 524288 | tf_op jit(solution)/shard_map/stack | solution.py:494
  1.0 3.0 %collective-permute-start.4 = (bf16[2,256,256]{2,1,0:T(8,128)(2,1)S(1)}, bf16[2,256,256]{2,1,0:T(8,128)(2,1)S(1)}, u32[]{:S(2)}, u32[]{:S(2)}) collective-permute-start(bf16[2,256,256]{2,1,0:T(8,128)(2,1)S(1)} %pad_maximum_fusion.1.refs_3_), channel_id=1, source_target_pairs={{0,8},{4,12},{8,0},{12,4},{16,24},{20,28},{24,16},{28,20},{1,9},{5... | collective-permute-start | bytes 786440 | tf_op jit(solution)/shard_map/ppermute | solution.py:488
  4.0 1.5 %collective-permute-start.5 = (bf16[2,256,256]{2,1,0:T(8,128)(2,1)S(1)}, bf16[2,256,256]{2,1,0:T(8,128)(2,1)S(1)}, u32[]{:S(2)}, u32[]{:S(2)}) collective-permute-start(bf16[2,256,256]{2,1,0:T(8,128)(2,1)S(1)} %pad_maximum_fusion.1.refs_3_), channel_id=1, source_target_pairs={{0,16},{4,20},{8,24},{12,28},{16,0},{20,4},{24,8},{28,12},{1,17},{... | collective-permute-start | bytes 786440 | tf_op jit(solution)/shard_map/ppermute | solution.py:488
  5.5 2.8 %mixer_local.1 = (f32[256,1024]{1,0:T(8,128)S(1)}, bf16[2,528,128]{2,1,0:T(8,128)(2,1)S(1)}, f32[256,8]{1,0:T(8,128)S(1)}) custom-call(s32[4]{0:T(128)} %refs_0_.3, f32[8]{0:T(128)} %refs_1_.3, bf16[256,1024]{1,0:T(8,128)(2,1)} %refs_2_.1, bf16[256,256]{1,0:T(8,128)(2,1)} %refs_3_.2, bf16[256,256]{1,0:T(8,128)(2,1)} %refs_3_.3, f32[8,256]{1,0:T(8,128)} %refs_5_.1), custom_call_target="tpu_custom_call" | custom-call | tf_op jit(solution)/shard_map/mixer_local/pallas_call | solution.py:52
  8.9 3.6 %fetch.1 = (bf16[1024,4096]{1,0:T(8,128)(2,1)S(1)}, bf16[256,1024]{1,0:T(8,128)(2,1)S(1)}, bf16[256,256]{1,0:T(8,128)(2,1)S(1)}) custom-call(bf16[2,528,128]{2,1,0:T(8,128)(2,1)S(1)} %get-tuple-element.40.mine_ref.refs_0_, bf16[1024,4096]{1,0:T(8,128)(2,1)} %refs_1_.4, bf16[256,1024]{1,0:T(8,128)(2,1)} %refs_2_.2, bf16[256,256]{1,0:T(8,128)(2,1)} %refs_3_.3), custom_call_target="tpu_custom_call" | custom-call | bytes 9043968 | tf_op jit(solution)/shard_map/fetch/pallas_call | solution.py:409
  12.5 4.9 %collective-permute-done.5.refs_7_ = bf16[2,256,256]{2,1,0:T(8,128)(2,1)S(1)} collective-permute-done((bf16[2,256,256]{2,1,0:T(8,128)(2,1)S(1)}, bf16[2,256,256]{2,1,0:T(8,128)(2,1)S(1)}, u32[]{:S(2)}, u32[]{:S(2)}) %collective-permute-start.5) | collective-permute-done | bytes 262176 | tf_op jit(solution)/shard_map/ppermute | solution.py:488
  17.4 0.5 collective-permute-start.8
  18.0 1.3 %collective-permute-start.1 = (bf16[528,128]{1,0:T(8,128)(2,1)S(1)}, bf16[528,128]{1,0:T(8,128)(2,1)S(1)}, u32[]{:S(2)}, u32[]{:S(2)}) collective-permute-start(bf16[528,128]{1,0:T(8,128)(2,1)S(1)} %compose.1), channel_id=1, source_target_pairs={{0,8},{4,12},{8,0},{12,4},{16,24},{20,28},{24,16},{28,20},{1,9},{5... | collective-permute-start | bytes 405512 | tf_op jit(solution)/shard_map/ppermute | solution.py:488
  19.3 0.8 %collective-permute-start.2 = (bf16[528,128]{1,0:T(8,128)(2,1)S(1)}, bf16[528,128]{1,0:T(8,128)(2,1)S(1)}, u32[]{:S(2)}, u32[]{:S(2)}) collective-permute-start(bf16[528,128]{1,0:T(8,128)(2,1)S(1)} %compose.1), channel_id=1, source_target_pairs={{0,16},{4,20},{8,24},{12,28},{16,0},{20,4},{24,8},{28,12},{1,17},{... | collective-permute-start | bytes 405512 | tf_op jit(solution)/shard_map/ppermute | solution.py:488
  20.1 1.4 %collective-permute-start.3 = (bf16[528,128]{1,0:T(8,128)(2,1)S(1)}, bf16[528,128]{1,0:T(8,128)(2,1)S(1)}, u32[]{:S(2)}, u32[]{:S(2)}) collective-permute-start(bf16[528,128]{1,0:T(8,128)(2,1)S(1)} %compose.1), channel_id=1, source_target_pairs={{0,24},{4,28},{8,16},{12,20},{16,8},{20,12},{24,0},{28,4},{1,25},{... | collective-permute-start | bytes 405512 | tf_op jit(solution)/shard_map/ppermute | solution.py:488
  21.5 4.2 %attention.1 = (bf16[256,1024]{1,0:T(8,128)(2,1)S(1)}, bf16[1024,4096]{1,0:T(8,128)(2,1)S(1)}) custom-call(s32[4]{0:T(128)} %refs_0_.3, s32[32]{0:T(128)} %refs_1_.5, bf16[256,1024]{1,0:T(8,128)(2,1)S(1)} %get-tuple-element.43.refs_2_, bf16[2,256,256]{2,1,0:T(8,128)(2,1)S(1)} %pad_maximum_fusion.1.refs_3_, ...), custom_call_target="tpu_custom_call" | custom-call | flops 42949672960 | bytes 4194304 | tf_op jit(solution)/shard_map/attention/pallas_call | solution.py:52
  25.7 0.5 collective-permute-done.2.refs_6_
  26.3 1.6 %collective-permute-done.3.refs_8_ = bf16[528,128]{1,0:T(8,128)(2,1)S(1)} collective-permute-done((bf16[528,128]{1,0:T(8,128)(2,1)S(1)}, bf16[528,128]{1,0:T(8,128)(2,1)S(1)}, u32[]{:S(2)}, u32[]{:S(2)}) %collective-permute-start.3) | collective-permute-done | bytes 135200 | tf_op jit(solution)/shard_map/ppermute | solution.py:488
  27.9 0.5 collective-permute-start.12
  28.4 0.8 %collective-permute-done.11.refs_5_ = bf16[528,128]{1,0:T(8,128)(2,1)S(1)} collective-permute-done((bf16[528,128]{1,0:T(8,128)(2,1)S(1)}, bf16[528,128]{1,0:T(8,128)(2,1)S(1)}, u32[]{:S(2)}, u32[]{:S(2)}) %collective-permute-start.11) | collective-permute-done | bytes 135200 | tf_op jit(solution)/shard_map/ppermute | solution.py:491
  29.8 0.5 finish.1.mix_ref
  30.3 1.2 %project.2 = (f32[64,1024]{1,0:T(8,128)S(1)}, bf16[128,1024]{1,0:T(8,128)(2,1)S(1)}, f32[64,1024]{1,0:T(8,128)S(1)}) custom-call(bf16[256,1024]{1,0:T(8,128)(2,1)S(1)} %get-tuple-element.48.att_ref, bf16[256,1024]{1,0:T(8,128)(2,1)S(1)} %finish.1.mix_ref, bf16[1024,4096]{1,0:T(8,128)(2,1)S(1)} %get-tuple-element.55.wa_ref, ...), custom_call_target="tpu_custom_call" | custom-call | flops 1073741824 | bytes 1572864 | tf_op jit(solution)/shard_map/project/pallas_call | solution.py:454
  31.6 1.6 %collective-permute-start.14 = (bf16[128,1024]{1,0:T(8,128)(2,1)S(1)}, bf16[128,1024]{1,0:T(8,128)(2,1)S(1)}, u32[]{:S(2)}, u32[]{:S(2)}) collective-permute-start(bf16[128,1024]{1,0:T(8,128)(2,1)S(1)} %get-tuple-element.59), channel_id=1, source_target_pairs={{0,1},{1,0},{2,3},{3,2},{4,5},{5,4},{6,7},{7,6},{8,9},{9,8},{10,11... | collective-permute-start | bytes 786440 | tf_op jit(solution)/shard_map/ppermute | solution.py:527
  33.2 3.4 %project.3 = (bf16[64,1024]{1,0:T(8,128)(2,1)S(1)}, f32[64,1024]{1,0:T(8,128)S(1)}, bf16[64,1024]{1,0:T(8,128)(2,1)S(1)}, f32[64,1024]{1,0:T(8,128)S(1)}, bf16[6...) custom-call(bf16[256,1024]{1,0:T(8,128)(2,1)S(1)} %get-tuple-element.48., ...), custom_call_target="tpu_custom_call" | custom-call | flops 3221225472 | bytes 4718592 | tf_op jit(solution)/shard_map/project/pallas_call | solution.py:454
  36.6 0.5 collective-permute-start.17
  37.1 1.6 %collective-permute-start.19 = (bf16[64,1024]{1,0:T(8,128)(2,1)S(1)}, bf16[64,1024]{1,0:T(8,128)(2,1)S(1)}, u32[]{:S(2)}, u32[]{:S(2)}) collective-permute-start(bf16[64,1024]{1,0:T(8,128)(2,1)S(1)} %get-tuple-element.68), channel_id=1, source_target_pairs={{0,1},{1,0},{2,3},{3,2},{4,5},{5,4},{6,7},{7,6},{8,9},{9,8},{10,11... | collective-permute-start | bytes 393224 | tf_op jit(solution)/shard_map/ppermute | solution.py:527
  39.1 1.6 %collective-permute-start.16 = (bf16[64,3072]{1,0:T(8,128)(2,1)S(1)}, bf16[64,3072]{1,0:T(8,128)(2,1)S(1)}, u32[]{:S(2)}, u32[]{:S(2)}) collective-permute-start(bf16[64,3072]{1,0:T(8,128)(2,1)S(1)} %get-tuple-element.63), channel_id=1, source_target_pairs={{0,1},{1,0},{2,3},{3,2},{4,5},{5,4},{6,7},{7,6},{8,9},{9,8},{10,11... | collective-permute-start | bytes 1179656 | tf_op jit(solution)/shard_map/ppermute | solution.py:527
  40.8 2.7 %collective-permute-start.15 = (bf16[64,1024]{1,0:T(8,128)(2,1)S(1)}, bf16[64,1024]{1,0:T(8,128)(2,1)S(1)}, u32[]{:S(2)}, u32[]{:S(2)}) collective-permute-start(bf16[64,1024]{1,0:T(8,128)(2,1)S(1)} %add_convert_fusion.7), channel_id=1, source_target_pairs={{0,2},{1,3},{2,0},{3,1},{4,6},{5,7},{6,4},{7,5},{8,10},{9,11},{10,... | collective-permute-start | bytes 393224 | tf_op jit(solution)/shard_map/ppermute | solution.py:530
  43.4 1.5 %collective-permute-done.17 = bf16[64,1024]{1,0:T(8,128)(2,1)S(1)} collective-permute-done((bf16[64,1024]{1,0:T(8,128)(2,1)S(1)}, bf16[64,1024]{1,0:T(8,128)(2,1)S(1)}, u32[]{:S(2)}, u32[]{:S(2)}) %collective-permute-start.17) | collective-permute-done | bytes 131104 | tf_op jit(solution)/shard_map/ppermute | solution.py:527
  45.0 1.6 %collective-permute-start.18 = (bf16[64,1024]{1,0:T(8,128)(2,1)S(1)}, bf16[64,1024]{1,0:T(8,128)(2,1)S(1)}, u32[]{:S(2)}, u32[]{:S(2)}) collective-permute-start(bf16[64,1024]{1,0:T(8,128)(2,1)S(1)} %add_convert_fusion.5), channel_id=1, source_target_pairs={{0,2},{1,3},{2,0},{3,1},{4,6},{5,7},{6,4},{7,5},{8,10},{9,11},{10,... | collective-permute-start | bytes 393224 | tf_op jit(solution)/shard_map/ppermute | solution.py:530
  46.6 5.4 %collective-permute-done.19 = bf16[64,1024]{1,0:T(8,128)(2,1)S(1)} collective-permute-done((bf16[64,1024]{1,0:T(8,128)(2,1)S(1)}, bf16[64,1024]{1,0:T(8,128)(2,1)S(1)}, u32[]{:S(2)}, u32[]{:S(2)}) %collective-permute-start.19) | collective-permute-done | bytes 131104 | tf_op jit(solution)/shard_map/ppermute | solution.py:527
  52.0 1.7 %collective-permute-start.20 = (bf16[64,1024]{1,0:T(8,128)(2,1)S(1)}, bf16[64,1024]{1,0:T(8,128)(2,1)S(1)}, u32[]{:S(2)}, u32[]{:S(2)}) collective-permute-start(bf16[64,1024]{1,0:T(8,128)(2,1)S(1)} %add_convert_fusion.3), channel_id=1, source_target_pairs={{0,2},{1,3},{2,0},{3,1},{4,6},{5,7},{6,4},{7,5},{8,10},{9,11},{10,... | collective-permute-start | bytes 393224 | tf_op jit(solution)/shard_map/ppermute | solution.py:530
  53.8 2.4 %collective-permute-done.21 = bf16[64,1024]{1,0:T(8,128)(2,1)S(1)} collective-permute-done((bf16[64,1024]{1,0:T(8,128)(2,1)S(1)}, bf16[64,1024]{1,0:T(8,128)(2,1)S(1)}, u32[]{:S(2)}, u32[]{:S(2)}) %collective-permute-start.21) | collective-permute-done | bytes 131104 | tf_op jit(solution)/shard_map/ppermute | solution.py:527
  56.2 1.7 %collective-permute-start.22 = (bf16[64,1024]{1,0:T(8,128)(2,1)S(1)}, bf16[64,1024]{1,0:T(8,128)(2,1)S(1)}, u32[]{:S(2)}, u32[]{:S(2)}) collective-permute-start(bf16[64,1024]{1,0:T(8,128)(2,1)S(1)} %add_convert_fusion.1), channel_id=1, source_target_pairs={{0,2},{1,3},{2,0},{3,1},{4,6},{5,7},{6,4},{7,5},{8,10},{9,11},{10,... | collective-permute-start | bytes 393224 | tf_op jit(solution)/shard_map/ppermute | solution.py:530
  58.0 1.6 %collective-permute-done.15 = bf16[64,1024]{1,0:T(8,128)(2,1)S(1)} collective-permute-done((bf16[64,1024]{1,0:T(8,128)(2,1)S(1)}, bf16[64,1024]{1,0:T(8,128)(2,1)S(1)}, u32[]{:S(2)}, u32[]{:S(2)}) %collective-permute-start.15) | collective-permute-done | bytes 131104 | tf_op jit(solution)/shard_map/ppermute | solution.py:530
  59.6 12.9 %collective-permute-done.22 = bf16[64,1024]{1,0:T(8,128)(2,1)S(1)} collective-permute-done((bf16[64,1024]{1,0:T(8,128)(2,1)S(1)}, bf16[64,1024]{1,0:T(8,128)(2,1)S(1)}, u32[]{:S(2)}, u32[]{:S(2)}) %collective-permute-start.22) | collective-permute-done | bytes 131104 | tf_op jit(solution)/shard_map/ppermute | solution.py:530
  72.6 0.8 %pad_maximum_fusion = bf16[64,4096]{1,0:T(8,128)(2,1)} fusion(bf16[64,1024]{1,0:T(8,128)(2,1)S(1)} %get-tuple-element.74, bf16[64,1024]{1,0:T(8,128)(2,1)S(1)} %get-tuple-element.75, bf16[64,1024]{1,0:T(8,128)(2,1)S(1)} %get-tuple-element.73, bf16[64,1024]{1,0:T(8,128)(2,1)S(1)} %add_convert_fusion.6), kind=kLoop, calls=%fused_computation | loop fusion | flops 2097152 | bytes 1048576 | tf_op jit(solution)/shard_map/concatenate | solution.py:561
  (29 shorter events, 2.0 us)
Async XLA Ops:
  1.0 11.5 %collective-permute-start.4 = (bf16[2,256,256]{2,1,0:T(8,128)(2,1)S(1)}, bf16[2,256,256]{2,1,0:T(8,128)(2,1)S(1)}, u32[]{:S(2)}, u32[]{:S(2)}) collective-permute-start(bf16[2,256,256]{2,1,0:T(8,128)(2,1)S(1)} %pad_maximum_fusion.1.refs_3_), channel_id=1, source_target_pairs={{0,8},{4,12},{8,0},{12,4},{16,24},{20,28},{24,16},{28,20},{1,9},{5... | collective-permute-start | bytes 786440 | tf_op jit(solution)/shard_map/ppermute | solution.py:488
  4.0 13.4 %collective-permute-start.5 = (bf16[2,256,256]{2,1,0:T(8,128)(2,1)S(1)}, bf16[2,256,256]{2,1,0:T(8,128)(2,1)S(1)}, u32[]{:S(2)}, u32[]{:S(2)}) collective-permute-start(bf16[2,256,256]{2,1,0:T(8,128)(2,1)S(1)} %pad_maximum_fusion.1.refs_3_), channel_id=1, source_target_pairs={{0,16},{4,20},{8,24},{12,28},{16,0},{20,4},{24,8},{28,12},{1,17},{... | collective-permute-start | bytes 786440 | tf_op jit(solution)/shard_map/ppermute | solution.py:488
  5.5 11.9 %collective-permute-start.6 = (bf16[2,256,256]{2,1,0:T(8,128)(2,1)S(1)}, bf16[2,256,256]{2,1,0:T(8,128)(2,1)S(1)}, u32[]{:S(2)}, u32[]{:S(2)}) collective-permute-start(bf16[2,256,256]{2,1,0:T(8,128)(2,1)S(1)} %pad_maximum_fusion.1.refs_3_), channel_id=1, source_target_pairs={{0,24},{4,28},{8,16},{12,20},{16,8},{20,12},{24,0},{28,4},{1,25},{... | collective-permute-start | bytes 786440 | tf_op jit(solution)/shard_map/ppermute | solution.py:488
  8.3 9.6 %collective-permute-start = (bf16[2,528,128]{2,1,0:T(8,128)(2,1)S(1)}, bf16[2,528,128]{2,1,0:T(8,128)(2,1)S(1)}, u32[]{:S(2)}, u32[]{:S(2)}) collective-permute-start(bf16[2,528,128]{2,1,0:T(8,128)(2,1)S(1)} %get-tuple-element.40.mine_ref.refs_0_), channel_id=1, source_target_pairs={{0,4},{4,0},{8,12},{12,8},{16,20},{20,16},{24,28},{28,24},{1,5},{5... | collective-permute-start | bytes 811016 | tf_op jit(solution)/shard_map/ppermute | solution.py:491
  8.4 10.9 %collective-permute-start.7 = (bf16[2,256,256]{2,1,0:T(8,128)(2,1)S(1)}, bf16[2,256,256]{2,1,0:T(8,128)(2,1)S(1)}, u32[]{:S(2)}, u32[]{:S(2)}) collective-permute-start(bf16[2,256,256]{2,1,0:T(8,128)(2,1)S(1)} %pad_maximum_fusion.1.refs_3_), channel_id=1, source_target_pairs={{0,4},{4,0},{8,12},{12,8},{16,20},{20,16},{24,28},{28,24},{1,5},{5... | collective-permute-start | bytes 786440 | tf_op jit(solution)/shard_map/ppermute | solution.py:491
  17.4 2.7 %collective-permute-start.10 = (bf16[2,256,256]{2,1,0:T(8,128)(2,1)S(1)}, bf16[2,256,256]{2,1,0:T(8,128)(2,1)S(1)}, u32[]{:S(2)}, u32[]{:S(2)}) collective-permute-start(bf16[2,256,256]{2,1,0:T(8,128)(2,1)S(1)} %collective-permute-done.6.refs_9_), channel_id=1, source_target_pairs={{0,4},{4,0},{8,12},{12,8},{16,20},{20,16},{24,28},{28,24},{1,5},{5... | collective-permute-start | bytes 786440 | tf_op jit(solution)/shard_map/ppermute | solution.py:491
  17.4 4.1 %collective-permute-start.8 = (bf16[2,256,256]{2,1,0:T(8,128)(2,1)S(1)}, bf16[2,256,256]{2,1,0:T(8,128)(2,1)S(1)}, u32[]{:S(2)}, u32[]{:S(2)}) collective-permute-start(bf16[2,256,256]{2,1,0:T(8,128)(2,1)S(1)} %collective-permute-done.4.refs_5_), channel_id=1, source_target_pairs={{0,4},{4,0},{8,12},{12,8},{16,20},{20,16},{24,28},{28,24},{1,5},{5... | collective-permute-start | bytes 786440 | tf_op jit(solution)/shard_map/ppermute | solution.py:491
  17.9 3.6 %collective-permute-start.9 = (bf16[2,256,256]{2,1,0:T(8,128)(2,1)S(1)}, bf16[2,256,256]{2,1,0:T(8,128)(2,1)S(1)}, u32[]{:S(2)}, u32[]{:S(2)}) collective-permute-start(bf16[2,256,256]{2,1,0:T(8,128)(2,1)S(1)} %collective-permute-done.5.refs_7_), channel_id=1, source_target_pairs={{0,4},{4,0},{8,12},{12,8},{16,20},{20,16},{24,28},{28,24},{1,5},{5... | collective-permute-start | bytes 786440 | tf_op jit(solution)/shard_map/ppermute | solution.py:491
  18.0 7.8 %collective-permute-start.1 = (bf16[528,128]{1,0:T(8,128)(2,1)S(1)}, bf16[528,128]{1,0:T(8,128)(2,1)S(1)}, u32[]{:S(2)}, u32[]{:S(2)}) collective-permute-start(bf16[528,128]{1,0:T(8,128)(2,1)S(1)} %compose.1), channel_id=1, source_target_pairs={{0,8},{4,12},{8,0},{12,4},{16,24},{20,28},{24,16},{28,20},{1,9},{5... | collective-permute-start | bytes 405512 | tf_op jit(solution)/shard_map/ppermute | solution.py:488
  19.3 7.0 %collective-permute-start.2 = (bf16[528,128]{1,0:T(8,128)(2,1)S(1)}, bf16[528,128]{1,0:T(8,128)(2,1)S(1)}, u32[]{:S(2)}, u32[]{:S(2)}) collective-permute-start(bf16[528,128]{1,0:T(8,128)(2,1)S(1)} %compose.1), channel_id=1, source_target_pairs={{0,16},{4,20},{8,24},{12,28},{16,0},{20,4},{24,8},{28,12},{1,17},{... | collective-permute-start | bytes 405512 | tf_op jit(solution)/shard_map/ppermute | solution.py:488
  20.1 7.8 %collective-permute-start.3 = (bf16[528,128]{1,0:T(8,128)(2,1)S(1)}, bf16[528,128]{1,0:T(8,128)(2,1)S(1)}, u32[]{:S(2)}, u32[]{:S(2)}) collective-permute-start(bf16[528,128]{1,0:T(8,128)(2,1)S(1)} %compose.1), channel_id=1, source_target_pairs={{0,24},{4,28},{8,16},{12,20},{16,8},{20,12},{24,0},{28,4},{1,25},{... | collective-permute-start | bytes 405512 | tf_op jit(solution)/shard_map/ppermute | solution.py:488
  27.9 1.4 %collective-permute-start.11 = (bf16[528,128]{1,0:T(8,128)(2,1)S(1)}, bf16[528,128]{1,0:T(8,128)(2,1)S(1)}, u32[]{:S(2)}, u32[]{:S(2)}) collective-permute-start(bf16[528,128]{1,0:T(8,128)(2,1)S(1)} %collective-permute-done.1.refs_4_), channel_id=1, source_target_pairs={{0,4},{4,0},{8,12},{12,8},{16,20},{20,16},{24,28},{28,24},{1,5},{5... | collective-permute-start | bytes 405512 | tf_op jit(solution)/shard_map/ppermute | solution.py:491
  27.9 1.5 %collective-permute-start.12 = (bf16[528,128]{1,0:T(8,128)(2,1)S(1)}, bf16[528,128]{1,0:T(8,128)(2,1)S(1)}, u32[]{:S(2)}, u32[]{:S(2)}) collective-permute-start(bf16[528,128]{1,0:T(8,128)(2,1)S(1)} %collective-permute-done.2.refs_6_), channel_id=1, source_target_pairs={{0,4},{4,0},{8,12},{12,8},{16,20},{20,16},{24,28},{28,24},{1,5},{5... | collective-permute-start | bytes 405512 | tf_op jit(solution)/shard_map/ppermute | solution.py:491
  28.4 1.4 %collective-permute-start.13 = (bf16[528,128]{1,0:T(8,128)(2,1)S(1)}, bf16[528,128]{1,0:T(8,128)(2,1)S(1)}, u32[]{:S(2)}, u32[]{:S(2)}) collective-permute-start(bf16[528,128]{1,0:T(8,128)(2,1)S(1)} %collective-permute-done.3.refs_8_), channel_id=1, source_target_pairs={{0,4},{4,0},{8,12},{12,8},{16,20},{20,16},{24,28},{28,24},{1,5},{5... | collective-permute-start | bytes 405512 | tf_op jit(solution)/shard_map/ppermute | solution.py:491
  31.6 9.2 %collective-permute-start.14 = (bf16[128,1024]{1,0:T(8,128)(2,1)S(1)}, bf16[128,1024]{1,0:T(8,128)(2,1)S(1)}, u32[]{:S(2)}, u32[]{:S(2)}) collective-permute-start(bf16[128,1024]{1,0:T(8,128)(2,1)S(1)} %get-tuple-element.59), channel_id=1, source_target_pairs={{0,1},{1,0},{2,3},{3,2},{4,5},{5,4},{6,7},{7,6},{8,9},{9,8},{10,11... | collective-permute-start | bytes 786440 | tf_op jit(solution)/shard_map/ppermute | solution.py:527
  36.6 8.4 %collective-permute-start.17 = (bf16[64,1024]{1,0:T(8,128)(2,1)S(1)}, bf16[64,1024]{1,0:T(8,128)(2,1)S(1)}, u32[]{:S(2)}, u32[]{:S(2)}) collective-permute-start(bf16[64,1024]{1,0:T(8,128)(2,1)S(1)} %get-tuple-element.65), channel_id=1, source_target_pairs={{0,1},{1,0},{2,3},{3,2},{4,5},{5,4},{6,7},{7,6},{8,9},{9,8},{10,11... | collective-permute-start | bytes 393224 | tf_op jit(solution)/shard_map/ppermute | solution.py:527
  37.1 14.9 %collective-permute-start.19 = (bf16[64,1024]{1,0:T(8,128)(2,1)S(1)}, bf16[64,1024]{1,0:T(8,128)(2,1)S(1)}, u32[]{:S(2)}, u32[]{:S(2)}) collective-permute-start(bf16[64,1024]{1,0:T(8,128)(2,1)S(1)} %get-tuple-element.68), channel_id=1, source_target_pairs={{0,1},{1,0},{2,3},{3,2},{4,5},{5,4},{6,7},{7,6},{8,9},{9,8},{10,11... | collective-permute-start | bytes 393224 | tf_op jit(solution)/shard_map/ppermute | solution.py:527
  38.7 17.5 %collective-permute-start.21 = (bf16[64,1024]{1,0:T(8,128)(2,1)S(1)}, bf16[64,1024]{1,0:T(8,128)(2,1)S(1)}, u32[]{:S(2)}, u32[]{:S(2)}) collective-permute-start(bf16[64,1024]{1,0:T(8,128)(2,1)S(1)} %get-tuple-element.71), channel_id=1, source_target_pairs={{0,1},{1,0},{2,3},{3,2},{4,5},{5,4},{6,7},{7,6},{8,9},{9,8},{10,11... | collective-permute-start | bytes 393224 | tf_op jit(solution)/shard_map/ppermute | solution.py:527
  39.1 33.3 %collective-permute-start.16 = (bf16[64,3072]{1,0:T(8,128)(2,1)S(1)}, bf16[64,3072]{1,0:T(8,128)(2,1)S(1)}, u32[]{:S(2)}, u32[]{:S(2)}) collective-permute-start(bf16[64,3072]{1,0:T(8,128)(2,1)S(1)} %get-tuple-element.63), channel_id=1, source_target_pairs={{0,1},{1,0},{2,3},{3,2},{4,5},{5,4},{6,7},{7,6},{8,9},{9,8},{10,11... | collective-permute-start | bytes 1179656 | tf_op jit(solution)/shard_map/ppermute | solution.py:527
  40.8 18.8 %collective-permute-start.15 = (bf16[64,1024]{1,0:T(8,128)(2,1)S(1)}, bf16[64,1024]{1,0:T(8,128)(2,1)S(1)}, u32[]{:S(2)}, u32[]{:S(2)}) collective-permute-start(bf16[64,1024]{1,0:T(8,128)(2,1)S(1)} %add_convert_fusion.7), channel_id=1, source_target_pairs={{0,2},{1,3},{2,0},{3,1},{4,6},{5,7},{6,4},{7,5},{8,10},{9,11},{10,... | collective-permute-start | bytes 393224 | tf_op jit(solution)/shard_map/ppermute | solution.py:530
  45.0 27.5 %collective-permute-start.18 = (bf16[64,1024]{1,0:T(8,128)(2,1)S(1)}, bf16[64,1024]{1,0:T(8,128)(2,1)S(1)}, u32[]{:S(2)}, u32[]{:S(2)}) collective-permute-start(bf16[64,1024]{1,0:T(8,128)(2,1)S(1)} %add_convert_fusion.5), channel_id=1, source_target_pairs={{0,2},{1,3},{2,0},{3,1},{4,6},{5,7},{6,4},{7,5},{8,10},{9,11},{10,... | collective-permute-start | bytes 393224 | tf_op jit(solution)/shard_map/ppermute | solution.py:530
  52.0 20.4 %collective-permute-start.20 = (bf16[64,1024]{1,0:T(8,128)(2,1)S(1)}, bf16[64,1024]{1,0:T(8,128)(2,1)S(1)}, u32[]{:S(2)}, u32[]{:S(2)}) collective-permute-start(bf16[64,1024]{1,0:T(8,128)(2,1)S(1)} %add_convert_fusion.3), channel_id=1, source_target_pairs={{0,2},{1,3},{2,0},{3,1},{4,6},{5,7},{6,4},{7,5},{8,10},{9,11},{10,... | collective-permute-start | bytes 393224 | tf_op jit(solution)/shard_map/ppermute | solution.py:530
  56.2 16.2 %collective-permute-start.22 = (bf16[64,1024]{1,0:T(8,128)(2,1)S(1)}, bf16[64,1024]{1,0:T(8,128)(2,1)S(1)}, u32[]{:S(2)}, u32[]{:S(2)}) collective-permute-start(bf16[64,1024]{1,0:T(8,128)(2,1)S(1)} %add_convert_fusion.1), channel_id=1, source_target_pairs={{0,2},{1,3},{2,0},{3,1},{4,6},{5,7},{6,4},{7,5},{8,10},{9,11},{10,... | collective-permute-start | bytes 393224 | tf_op jit(solution)/shard_map/ppermute | solution.py:530

commit v4 on v3

--- a/solution.py
+++ b/solution.py
@@ -12,7 +12,7 @@
 STATE = 128
 LOG2E = 1.4426950408889634
 LOW = -1e30
-SHARES = (2, 2, 2, 2)
+SHARES = (2, 2, 4)
 F32 = jnp.float32
 BF16 = jnp.bfloat16
 
@@ -244,144 +244,159 @@
     )[0]
 
 
-def attention_kernel(page_len, together, len_ref, table_ref, q_ref, *refs):
-    *got, weight_ref, out_ref, ready_ref, inv, kv, sc, mx, ls, acc, weight_sem = refs
-    pieces = weight_sem.shape[0]
-    depth = weight_ref.shape[0] // pieces
-    fetches = []
-    for i in range(pieces):
-        here = slice(i * depth, (i + 1) * depth)
-        fetches.append(
-            pltpu.make_async_copy(weight_ref.at[here], ready_ref.at[here], weight_sem.at[i])
-        )
-    for f in fetches:
-        f.start()
+def attention_kernel(page_len, later, len_ref, table_ref, q_ref, *refs):
+    if later:
+        kv, out_ref, qs, sc, mx, ls, acc = refs
+    else:
+        *got, weight_ref, out_ref, kv, ready_ref, inv, qs, sc, mx, ls, acc, weight_sem = refs
+        pieces = weight_sem.shape[0]
+        depth = weight_ref.shape[0] // pieces
+        fetches = []
+        for i in range(pieces):
+            here = slice(i * depth, (i + 1) * depth)
+            fetches.append(
+                pltpu.make_async_copy(weight_ref.at[here], ready_ref.at[here], weight_sem.at[i])
+            )
+        for f in fetches:
+            f.start()
     me = lax.axis_index("ctx")
     z = lax.axis_index("tp")
-    rows = q_ref.shape[0]
-    part = rows // 4
-    heads = q_ref.shape[1] // HEAD_DIM
-    group = heads // (kv.shape[2] // HEAD_DIM)
-    first = me * rows
+    keys = q_ref.shape[0]
+    rows = keys // 2
+    part = rows // 2
+    kv_heads = kv.shape[2] // HEAD_DIM
+    group = q_ref.shape[1] // HEAD_DIM // kv_heads
+    stacked = group * rows
     ends = doc_ends_of(len_ref)
     start0 = 0
     for end in ends:
-        start0 = jnp.where(first >= end, end, start0)
-    low_block = start0 // rows
-
-    def invert(l, _):
-        inv[table_ref[l]] = l
-        return 0
-
-    lax.fori_loop(0, table_ref.shape[0], invert, 0, unroll=8)
-    for j, ref in enumerate(got):
-        pages = ref.shape[1] // page_len
-        for slot in range(pages):
-            page = inv[(me ^ j) * pages + slot]
-            there = pl.ds(pl.multiple_of(page * page_len, page_len), page_len)
-            here = slice(slot * page_len, (slot + 1) * page_len)
-            for i in range(2):
-                kv[i, there, :] = ref[i, here, :]
-
-    t_pos = first + lax.broadcasted_iota(jnp.int32, (rows, 1), 0)
+        start0 = jnp.where(me * keys >= end, end, start0)
+    low_block = start0 // keys
+    side = z // 2 if later else 1 - z // 2
+
+    if not later:
+
+        def invert(l, _):
+            inv[table_ref[l]] = l
+            return 0
+
+        lax.fori_loop(0, table_ref.shape[0], invert, 0, unroll=8)
+        for j, ref in enumerate(got):
+            pages = ref.shape[1] // page_len
+            for slot in range(pages):
+                page = inv[(me ^ j) * pages + slot]
+                there = pl.ds(pl.multiple_of(page * page_len, page_len), page_len)
+                here = slice(slot * page_len, (slot + 1) * page_len)
+                for i in range(2):
+                    kv[i, there, :] = ref[i, here, :]
+
+    here = pl.ds(pl.multiple_of(side * rows, rows), rows)
+    for h in range(kv_heads * group):
+        g, i = divmod(h, group)
+        qs[g, i * rows : (i + 1) * rows, :] = q_ref[here, h * HEAD_DIM : (h + 1) * HEAD_DIM]
+    row = lax.rem(lax.broadcasted_iota(jnp.int32, (stacked, 1), 0), rows)
+    t_pos = me * keys + side * rows + row
     t_start = doc_start(t_pos, ends)
     scale = LOG2E * HEAD_DIM ** (-0.5)
 
-    def lanes(h):
-        return slice(h // group * HEAD_DIM, (h // group + 1) * HEAD_DIM)
-
-    for h0 in range(0, heads, together):
-        some = range(h0, h0 + together)
-
-        def scores(block, own):
-            at = pl.ds(pl.multiple_of(block * rows, rows), rows)
-            u_pos = block * rows + lax.broadcasted_iota(jnp.int32, (1, rows), 1)
-            shown = u_pos >= t_start
-            if own:
-                shown = shown & (u_pos <= t_pos)
-            for h in some:
-                s = nt(q_ref[:, h * HEAD_DIM : (h + 1) * HEAD_DIM], kv[0, at, lanes(h)])
-                s = jnp.where(shown, s * scale, LOW)
-                sc[block - low_block, h - h0] = s
-                top = s[:, :128]
-                for k in range(128, rows, 128):
-                    top = jnp.maximum(top, s[:, k : k + 128])
-                mx[h - h0] = top if own else jnp.maximum(mx[h - h0], top)
-
-        scores(me, True)
-
-        def earlier(block, _):
-            scores(block, False)
-            return 0
-
-        lax.fori_loop(low_block, me, earlier, 0)
-        for i in range(together):
-            mx[i] = jnp.broadcast_to(jnp.max(mx[i], axis=1, keepdims=True), (rows, 128))
-
-        def weigh(block, own):
-            at = pl.ds(pl.multiple_of(block * rows, rows), rows)
-            for h in some:
-                i = h - h0
-                m = mx[i]
-                total, pieces = None, []
-                for k in range(0, rows, 128):
-                    w = jnp.exp2(sc[block - low_block, i, :, k : k + 128] - m)
-                    total = w if total is None else total + w
-                    pieces.append(w.astype(BF16))
-                term = nn(jnp.concatenate(pieces, axis=1), kv[1, at, lanes(h)])
-                ls[i] = total if own else ls[i] + total
-                acc[i] = term if own else acc[i] + term
-
-        weigh(me, True)
-
-        def weigh_earlier(block, _):
-            weigh(block, False)
-            return 0
-
-        lax.fori_loop(low_block, me, weigh_earlier, 0)
-        for h in some:
-            inverse = 1.0 / jnp.sum(ls[h - h0], axis=1, keepdims=True)
-            res = (acc[h - h0] * inverse).astype(BF16)
-            for q in range(4):
-                at = pl.multiple_of(row_slot(q, z) * part, part)
-                out_ref[pl.ds(at, part), h * HEAD_DIM : (h + 1) * HEAD_DIM] = res[
-                    q * part : (q + 1) * part
-                ]
-    for f in fetches:
-        f.wait()
-
-
-def attention(page_len, doc_lengths, page_table, queries, got, weight):
-    rows = queries.shape[0]
-    heads = queries.shape[1] // HEAD_DIM
-    keys = len(got) * got[0].shape[1]
-    width = got[0].shape[2]
-    blocks = min(keys // rows, keys // 2 // rows + 1)
-    block_bytes = 4 * rows * rows * blocks
-    together = heads
-    while together > 1 and together * block_bytes > 12 * MIB:
-        together //= 2
+    def lanes(g):
+        return slice(g * HEAD_DIM, (g + 1) * HEAD_DIM)
+
+    def scores(block, own):
+        at = pl.ds(pl.multiple_of(block * keys, keys), keys)
+        u_pos = block * keys + lax.broadcasted_iota(jnp.int32, (1, keys), 1)
+        shown = u_pos >= t_start
+        if own:
+            shown = shown & (u_pos <= t_pos)
+        for g in range(kv_heads):
+            s = nt(qs[g], kv[0, at, lanes(g)])
+            s = jnp.where(shown, s * scale, LOW)
+            sc[block - low_block, g] = s
+            top = s[:, :128]
+            for k in range(128, keys, 128):
+                top = jnp.maximum(top, s[:, k : k + 128])
+            mx[g] = top if own else jnp.maximum(mx[g], top)
+
+    scores(me, True)
+
+    def earlier(block, _):
+        scores(block, False)
+        return 0
+
+    lax.fori_loop(low_block, me, earlier, 0)
+    for g in range(kv_heads):
+        mx[g] = jnp.broadcast_to(jnp.max(mx[g], axis=1, keepdims=True), (stacked, 128))
+
+    def weigh(block, own):
+        at = pl.ds(pl.multiple_of(block * keys, keys), keys)
+        for g in range(kv_heads):
+            m = mx[g]
+            total, pieces = None, []
+            for k in range(0, keys, 128):
+                w = jnp.exp2(sc[block - low_block, g, :, k : k + 128] - m)
+                total = w if total is None else total + w
+                pieces.append(w.astype(BF16))
+            term = nn(jnp.concatenate(pieces, axis=1), kv[1, at, lanes(g)])
+            ls[g] = total if own else ls[g] + total
+            acc[g] = term if own else acc[g] + term
+
+    weigh(me, True)
+
+    def weigh_earlier(block, _):
+        weigh(block, False)
+        return 0
+
+    lax.fori_loop(low_block, me, weigh_earlier, 0)
+    for g in range(kv_heads):
+        inverse = 1.0 / jnp.sum(ls[g], axis=1, keepdims=True)
+        res = (acc[g] * inverse).astype(BF16)
+        for i in range(group):
+            h = g * group + i
+            for q in range(2):
+                slot = row_slot(2 * side + q, z) - (2 if later else 0)
+                at = pl.multiple_of(slot * part, part)
+                src = i * rows + q * part
+                out_ref[pl.ds(at, part), h * HEAD_DIM : (h + 1) * HEAD_DIM] = res[src : src + part]
+    if not later:
+        for f in fetches:
+            f.wait()
+
+
+def attention(page_len, doc_lengths, page_table, queries, kv_heads, got=(), weight=None, kv=None):
+    later = kv is not None
+    keys = queries.shape[0]
+    rows = keys // 2
+    group = queries.shape[1] // HEAD_DIM // kv_heads
+    total = kv.shape[1] if later else len(got) * keys
+    width = kv_heads * HEAD_DIM
+    blocks = min(total // keys, total // 2 // keys + 1)
+    out = [jax.ShapeDtypeStruct((rows, queries.shape[1]), BF16)]
+    stat = pltpu.VMEM((kv_heads, group * rows, 128), F32)
+    scratch = [
+        pltpu.VMEM((kv_heads, group * rows, HEAD_DIM), BF16),
+        pltpu.VMEM((blocks, kv_heads, group * rows, keys), F32),
+        stat,
+        stat,
+        stat,
+    ]
+    near, specs = (queries, kv), None
+    if not later:
+        out.append(jax.ShapeDtypeStruct((2, total, width), BF16))
+        out.append(jax.ShapeDtypeStruct(weight.shape, weight.dtype))
+        scratch.insert(0, pltpu.SMEM((page_table.shape[0],), jnp.int32))
+        scratch.append(pltpu.SemaphoreType.DMA((4,)))
+        near = (queries, *got, in_hbm(weight))
+        specs = [VMEM_SPEC] * (1 + len(got)) + [HBM_SPEC]
     return one_step(
-        functools.partial(attention_kernel, page_len, together),
+        functools.partial(attention_kernel, page_len, later),
         "attention",
-        (
-            jax.ShapeDtypeStruct(queries.shape, BF16),
-            jax.ShapeDtypeStruct(weight.shape, weight.dtype),
-        ),
+        out,
         (Far(doc_lengths, pltpu.SMEM), Far(page_table, pltpu.SMEM)),
-        (queries, *got, in_hbm(weight)),
-        specs=[VMEM_SPEC] * (1 + len(got)) + [HBM_SPEC],
-        scratch=[
-            pltpu.SMEM((page_table.shape[0],), jnp.int32),
-            pltpu.VMEM((2, keys, width), BF16),
-            pltpu.VMEM((blocks, together, rows, rows), F32),
-            pltpu.VMEM((together, rows, 128), F32),
-            pltpu.VMEM((together, rows, 128), F32),
-            pltpu.VMEM((together, rows, HEAD_DIM), F32),
-            pltpu.SemaphoreType.DMA((4,)),
-        ],
-        cost=(128 * heads * rows * 1280 * 128, 4 << 20, heads * rows * 1280),
-        room=6 * MIB + together * block_bytes + 4 * keys * width,
+        near,
+        specs=specs,
+        scratch=scratch,
+        cost=((0 if later else 1280) * 1280 * group * rows * 128, 0 if later else 4 << 20, 0),
+        room=5 * MIB + 4 * kv_heads * group * rows * keys * blocks,
     )
 
 
@@ -420,45 +435,36 @@
     )(after, *(in_hbm(w) for w in weights))
 
 
-def project_kernel(start, tile, joined, att_ref, mix_ref, wa_ref, wm_ref, *out):
-    *other, send_ref, keep_ref = out
-    part = keep_ref.shape[0]
-    at = 0
-    for keep_other in other[-1:] if joined else other[1::2]:
-        for j in range(0, keep_other.shape[1], tile):
-            here, there = slice(j, j + tile), slice(start + at, start + at + tile)
-            own = slice(at, at + tile)
-            total = nn(att_ref[...], wa_ref[:, there]) + nn(mix_ref[...], wm_ref[:, there])
-            through = total[:part].astype(BF16)
-            if joined:
-                send_ref[:part, own] = through
-                send_ref[part:, own] = total[2 * part : 3 * part].astype(BF16)
-            else:
-                other[2 * [o is keep_other for o in other[1::2]].index(True)][:, here] = through
-                send_ref[:, own] = total[2 * part : 3 * part].astype(BF16)
-            keep_other[:, here] = total[part : 2 * part]
-            keep_ref[:, own] = total[3 * part :]
-            at += tile
-
-
-def project(att, mix, wa, wm, start, widths, tile, joined):
-    rows, depth = mix.shape
-    part, width = rows // 4, sum(widths)
+def project_kernel(start, tile, side, att_ref, mix_ref, wa_ref, wm_ref, *out):
+    part = out[0].shape[0]
+    mix = mix_ref[2 * part * side : 2 * part * (side + 1), :]
+    for send_ref, keep_ref in zip(out[::2], out[1::2]):
+        width = send_ref.shape[1]
+        for j in range(0, width, tile):
+            here, there = slice(j, j + tile), slice(start + j, start + j + tile)
+            total = nn(att_ref[...], wa_ref[:, there]) + nn(mix, wm_ref[:, there])
+            send_ref[:, here] = total[:part].astype(BF16)
+            keep_ref[:, here] = total[part:]
+        start += width
+
+
+def project(side, att, mix, wa, wm, start, widths, tile):
+    rows, depth = att.shape
+    width = sum(widths)
     out_shape = []
     for w in widths:
-        if not joined:
-            out_shape.append(jax.ShapeDtypeStruct((part, w), BF16))
-        out_shape.append(jax.ShapeDtypeStruct((part, w), F32))
-    out_shape.append(jax.ShapeDtypeStruct((2 * part if joined else part, width), BF16))
-    out_shape.append(jax.ShapeDtypeStruct((part, width), F32))
+        out_shape.append(jax.ShapeDtypeStruct((rows // 2, w), BF16))
+        out_shape.append(jax.ShapeDtypeStruct((rows // 2, w), F32))
     return pl.pallas_call(
-        functools.partial(project_kernel, start, tile, joined),
+        functools.partial(project_kernel, start, tile, side),
         out_shape=tuple(out_shape),
         in_specs=[VMEM_SPEC] * 4,
         out_specs=(VMEM_SPEC,) * len(out_shape),
         compiler_params=pltpu.CompilerParams(vmem_limit_bytes=4 * MIB),
         cost_estimate=pl.CostEstimate(
-            flops=4 * rows * depth * width, bytes_accessed=6 * rows * width, transcendentals=0
+            flops=(1 - side) * 4 * rows * depth * width,
+            bytes_accessed=(1 - side) * 6 * rows * width,
+            transcendentals=0,
         ),
         name="project",
     )(att, mix, wa, wm)
@@ -509,9 +515,8 @@
     got = []
     for a in far:
         got += [a, other_core(a)]
-    att, far_weight = attention(
-        page_len, doc_lengths, page_table, near_queries, got, mixer_weight
-    )
+    place = (page_len, doc_lengths, page_table, near_queries, width // HEAD_DIM)
+    att, kv, far_weight = attention(*place, got, mixer_weight)
     *far_states, att = lax.optimization_barrier((*far_states, att))
     got_states = []
     for a in far_states:
@@ -529,35 +534,33 @@
     def across(a):
         return lax.ppermute(a, "tp", [(i, i ^ 2) for i in range(n_tp)])
 
-    keep_other, send, keep = project(att, mix, *weights, 0, widths[:1], 256, True)
-    send, mix = lax.optimization_barrier((send, mix))
-    *other, send_rest, keep_rest = project(
-        att, mix, *weights, widths[0], widths[1:], 256, False
-    )
-    near = neighbour(send)
-    near_other = [near[:part]] + [neighbour(a) for a in other[::2]]
-    keep_other = [keep_other] + other[1::2]
+    sums = list(project(0, att, mix, *weights, 0, widths[:1], 256))
+    att, sums[0] = lax.optimization_barrier((att, sums[0]))
+    sums += project(0, att, mix, *weights, widths[0], widths[1:], 256)
+    kv, sums[2] = lax.optimization_barrier((kv, sums[2]))
+    near_other = [neighbour(a) for a in sums[::2]]
     last, order = [], None
-    for k in range(len(widths)):
+    for k, keep in enumerate(sums[1::2]):
         if order is not None:
             near_other[k], order = lax.optimization_barrier((near_other[k], order))
-        both = keep_other[k] + near_other[k].astype(F32)
-
-        order = both.astype(BF16)
+        if k == 2:
+            near_other[k], last[1] = lax.optimization_barrier((near_other[k], last[1]))
+        order = (keep + near_other[k].astype(F32)).astype(BF16)
+        if k == 0:
+            kv, order = lax.optimization_barrier((kv, order))
         last.append(across(order))
-        if k == 99:
-            send_rest, order = lax.optimization_barrier((send_rest, order))
-    near_rest = neighbour(send_rest)
-    parts = [(keep, near[part:], last[0])]
-    at = 0
-    for a, width in zip(last[1:], widths[1:]):
-        parts.append((keep_rest[:, at : at + width], near_rest[:, at : at + width], a))
-        at += width
-    pieces, done = [], None
-    for a, b, c in parts:
-
-        done = (a + b.astype(F32) + c.astype(F32)).astype(BF16)
-        pieces.append(done)
+    (later,) = attention(*place, kv=kv)
+    own_widths = (columns // 1,) * 1
+    sums = project(1, later, mix, *weights, 0, own_widths, 256)
+    near_own = [neighbour(a) for a in sums[::2]]
+    near_own = near_own[0] if 1 == 1 else jnp.concatenate(near_own, axis=1)
+    keep_own = sums[1] if 1 == 1 else jnp.concatenate(sums[1::2], axis=1)
+    pieces, at = [], 0
+    for a in last:
+        here = slice(at, at + a.shape[1])
+        own = keep_own[:, here] + near_own[:, here].astype(F32) + a.astype(F32)
+        pieces.append(own.astype(BF16))
+        at += a.shape[1]
     return jnp.concatenate(pieces, axis=1)
 
 

time: 73.6 us -> 69.7 us (0.947)
  starting transfers between devices: 23.2 us -> 20 us
  waiting for transfers between devices: 32.2 us -> 29.6 us
  Pallas kernels: 15.8 us -> 17.6 us
    ppermute x5 -> x4, waiting for transfers between devices: 9.39 us -> 6.7 us  [neighbour(): return lax.ppermute(a, 'tp', [(i, i ^ 1) for i in range(n_tp)])]
    ppermute x4 -> x3, starting transfers between devices: 7.74 us -> 5.65 us  [across(): return lax.ppermute(a, 'tp', [(i, i ^ 2) for i in range(n_tp)])]
    pallas_call x3 -> x4, Pallas kernels: 7.48 us -> 9.1 us  [one_step(): pl.pallas_call(body, out_shape=tuple(out_shape), in_specs=[HBM_SPEC] * le...]
    ppermute x5 -> x4, starting transfers between devices: 5.76 us -> 4.7 us  [neighbour(): return lax.ppermute(a, 'tp', [(i, i ^ 1) for i in range(n_tp)])]
    pallas_call x2 -> x3, Pallas kernels: 4.65 us -> 4.86 us  [project(): pl.pallas_call(functools.partial(project_kernel, start, tile, side), out_...]
    ppermute x4 -> x3, waiting for transfers between devices: 14.4 us -> 14.4 us  [across(): return lax.ppermute(a, 'tp', [(i, i ^ 2) for i in range(n_tp)])]
  transfers between devices with their start and end apart: 23 -> 21, of which waited for: 11 -> 9; matrix products, arithmetic and copies ran while one was open for 0% -> 0% of each run, Pallas kernels for 19% -> 24%
where the time goes in v4:
time: 69.7 us; the launch traced here: 69.5 us
  waiting for transfers between devices  29.6 us (42%)
  starting transfers between devices  20 us (29%)
  Pallas kernels  17.6 us (25%)
  other arithmetic  2.12 us (3%)
    ppermute x3, waiting for transfers between devices, across(): return lax.ppermute(a, 'tp', [(i, i ^ 2) for i in range(n_tp)])  14.4 us
    pallas_call x4, Pallas kernels, one_step(): pl.pallas_call(body, out_shape=tuple(out_shape), in_specs=[HBM_SPEC] * le...  9.1 us
    ppermute x6, starting transfers between devices, between_chips(): return lax.ppermute(a, 'ctx', [(i, i ^ 2 * j) for i in range(n_ctx)])  8.1 us
    ppermute x6, waiting for transfers between devices, between_chips(): return lax.ppermute(a, 'ctx', [(i, i ^ 2 * j) for i in range(n_ctx)])  7.09 us
    ppermute x4, waiting for transfers between devices, neighbour(): return lax.ppermute(a, 'tp', [(i, i ^ 1) for i in range(n_tp)])  6.7 us
    ppermute x3, starting transfers between devices, across(): return lax.ppermute(a, 'tp', [(i, i ^ 2) for i in range(n_tp)])  5.65 us
    pallas_call x3, Pallas kernels, project(): pl.pallas_call(functools.partial(project_kernel, start, tile, side), out_...  4.86 us
    ppermute x4, starting transfers between devices, neighbour(): return lax.ppermute(a, 'tp', [(i, i ^ 1) for i in range(n_tp)])  4.7 us
  transfers between devices with their start and end apart: 21, of which 9 were waited for; matrix products, arithmetic and copies ran while one was open for 0% of the time, Pallas kernels for 24%

profile of v4, /device:TPU:0, one launch (start us, length us, event | category | flops | bytes accessed | tf_op | source)
XLA Modules:
  0.0 69.5 jit_solution(6686921459505189786)
XLA Ops:
  0.0 1.0 %pad_maximum_fusion.1.refs_3_ = bf16[2,256,256]{2,1,0:T(8,128)(2,1)S(1)} fusion(bf16[1,256,256]{2,1,0:T(8,128)(2,1)} %bitcast.2, bf16[1,256,256]{2,1,0:T(8,128)(2,1)} %bitcast.3), kind=kLoop, calls=%fused_computation.3 | loop fusion | flops 131072 | bytes 524288 | tf_op jit(solution)/shard_map/stack | solution.py:500
  1.0 3.0 %collective-permute-start = (bf16[2,256,256]{2,1,0:T(8,128)(2,1)S(1)}, bf16[2,256,256]{2,1,0:T(8,128)(2,1)S(1)}, u32[]{:S(2)}, u32[]{:S(2)}) collective-permute-start(bf16[2,256,256]{2,1,0:T(8,128)(2,1)S(1)} %pad_maximum_fusion.1.refs_3_), channel_id=1, source_target_pairs={{0,8},{4,12},{8,0},{12,4},{16,24},{20,28},{24,16},{28,20},{1,9},{5... | collective-permute-start | bytes 786440 | tf_op jit(solution)/shard_map/ppermute | solution.py:494
  4.0 1.5 %collective-permute-start.1 = (bf16[2,256,256]{2,1,0:T(8,128)(2,1)S(1)}, bf16[2,256,256]{2,1,0:T(8,128)(2,1)S(1)}, u32[]{:S(2)}, u32[]{:S(2)}) collective-permute-start(bf16[2,256,256]{2,1,0:T(8,128)(2,1)S(1)} %pad_maximum_fusion.1.refs_3_), channel_id=1, source_target_pairs={{0,16},{4,20},{8,24},{12,28},{16,0},{20,4},{24,8},{28,12},{1,17},{... | collective-permute-start | bytes 786440 | tf_op jit(solution)/shard_map/ppermute | solution.py:494
  5.5 2.8 %mixer_local.1 = (f32[256,1024]{1,0:T(8,128)S(1)}, bf16[2,528,128]{2,1,0:T(8,128)(2,1)S(1)}, f32[256,8]{1,0:T(8,128)S(1)}) custom-call(s32[4]{0:T(128)} %refs_0_.5, f32[8]{0:T(128)} %refs_1_.4, bf16[256,1024]{1,0:T(8,128)(2,1)} %refs_2_.1, bf16[256,256]{1,0:T(8,128)(2,1)} %refs_3_.2, bf16[256,256]{1,0:T(8,128)(2,1)} %refs_3_.3, f32[8,256]{1,0:T(8,128)} %refs_5_.1), custom_call_target="tpu_custom_call" | custom-call | tf_op jit(solution)/shard_map/mixer_local/pallas_call | solution.py:52
  8.4 0.5 collective-permute-start.3
  8.9 3.6 %fetch.1 = (bf16[1024,4096]{1,0:T(8,128)(2,1)S(1)}, bf16[256,1024]{1,0:T(8,128)(2,1)S(1)}, bf16[256,256]{1,0:T(8,128)(2,1)S(1)}) custom-call(bf16[2,528,128]{2,1,0:T(8,128)(2,1)S(1)} %get-tuple-element.44.refs_0_.mine_ref, bf16[1024,4096]{1,0:T(8,128)(2,1)} %refs_1_.5, bf16[256,1024]{1,0:T(8,128)(2,1)} %refs_2_.2, bf16[256,256]{1,0:T(8,128)(2,1)} %refs_3_.3), custom_call_target="tpu_custom_call" | custom-call | bytes 9043968 | tf_op jit(solution)/shard_map/fetch/pallas_call | solution.py:424
  12.5 4.9 %collective-permute-done.1.refs_7_ = bf16[2,256,256]{2,1,0:T(8,128)(2,1)S(1)} collective-permute-done((bf16[2,256,256]{2,1,0:T(8,128)(2,1)S(1)}, bf16[2,256,256]{2,1,0:T(8,128)(2,1)S(1)}, u32[]{:S(2)}, u32[]{:S(2)}) %collective-permute-start.1) | collective-permute-done | bytes 262176 | tf_op jit(solution)/shard_map/ppermute | solution.py:494
  17.4 0.5 collective-permute-start.5
  18.0 1.6 %collective-permute-start.10 = (bf16[528,128]{1,0:T(8,128)(2,1)S(1)}, bf16[528,128]{1,0:T(8,128)(2,1)S(1)}, u32[]{:S(2)}, u32[]{:S(2)}) collective-permute-start(bf16[528,128]{1,0:T(8,128)(2,1)S(1)} %compose.1), channel_id=1, source_target_pairs={{0,24},{4,28},{8,16},{12,20},{16,8},{20,12},{24,0},{28,4},{1,25},{... | collective-permute-start | bytes 405512 | tf_op jit(solution)/shard_map/ppermute | solution.py:494
  19.5 1.5 %collective-permute-start.8 = (bf16[528,128]{1,0:T(8,128)(2,1)S(1)}, bf16[528,128]{1,0:T(8,128)(2,1)S(1)}, u32[]{:S(2)}, u32[]{:S(2)}) collective-permute-start(bf16[528,128]{1,0:T(8,128)(2,1)S(1)} %compose.1), channel_id=1, source_target_pairs={{0,8},{4,12},{8,0},{12,4},{16,24},{20,28},{24,16},{28,20},{1,9},{5... | collective-permute-start | bytes 405512 | tf_op jit(solution)/shard_map/ppermute | solution.py:494
  21.0 0.5 collective-permute-start.9
  21.5 4.2 %attention.2 = (bf16[128,1024]{1,0:T(8,128)(2,1)S(1)}, bf16[2,2048,256]{2,1,0:T(8,128)(2,1)S(1)}, bf16[1024,4096]{1,0:T(8,128)(2,1)S(1)}) custom-call(s32[4]{0:T(128)} %refs_0_.5, s32[32]{0:T(128)} %refs_1_.7, bf16[256,1024]{1,0:T(8,128)(2,1)S(1)} %get-tuple-element.46.refs_2_, bf16[2,256,256]{2,1,0:T(8,128)(2,1)S(1)} %pad_maximum_fusion.1.refs_3_, ...), custom_call_target="tpu_custom_call" | custom-call | flops 107374182400 | bytes 4194304 | tf_op jit(solution)/shard_map/attention/pallas_call | solution.py:52
  25.7 2.2 %collective-permute-done.8.refs_4_ = bf16[528,128]{1,0:T(8,128)(2,1)S(1)} collective-permute-done((bf16[528,128]{1,0:T(8,128)(2,1)S(1)}, bf16[528,128]{1,0:T(8,128)(2,1)S(1)}, u32[]{:S(2)}, u32[]{:S(2)}) %collective-permute-start.8) | collective-permute-done | bytes 135200 | tf_op jit(solution)/shard_map/ppermute | solution.py:494
  27.9 0.5 collective-permute-start.12
  28.4 0.8 %collective-permute-done.11.refs_5_ = bf16[528,128]{1,0:T(8,128)(2,1)S(1)} collective-permute-done((bf16[528,128]{1,0:T(8,128)(2,1)S(1)}, bf16[528,128]{1,0:T(8,128)(2,1)S(1)}, u32[]{:S(2)}, u32[]{:S(2)}) %collective-permute-start.11) | collective-permute-done | bytes 135200 | tf_op jit(solution)/shard_map/ppermute | solution.py:497
  29.5 0.3 collective-permute-done.13.refs_9_
  29.8 0.5 finish.1.mix_ref
  30.3 0.7 %project.3 = (bf16[64,1024]{1,0:T(8,128)(2,1)S(1)}, f32[64,1024]{1,0:T(8,128)S(1)}) custom-call(bf16[128,1024]{1,0:T(8,128)(2,1)S(1)} %get-tuple-element.62.att_ref, bf16[256,1024]{1,0:T(8,128)(2,1)S(1)} %finish.1.mix_ref, bf16[1024,4096]{1,0:T(8,128)(2,1)S(1)} %get-tuple-element.59.wa_ref, bf16[1024,4096]{1,0:T(8,128)(2,1)S(1)} %get-tuple-element.60.wm_ref), custom_call_target="tpu_custom_call" | custom-call | flops 536870912 | bytes 786432 | tf_op jit(solution)/shard_map/project/pallas_call | solution.py:458
  31.1 1.6 %collective-permute-start.14 = (bf16[64,1024]{1,0:T(8,128)(2,1)S(1)}, bf16[64,1024]{1,0:T(8,128)(2,1)S(1)}, u32[]{:S(2)}, u32[]{:S(2)}) collective-permute-start(bf16[64,1024]{1,0:T(8,128)(2,1)S(1)} %get-tuple-element.66), channel_id=1, source_target_pairs={{0,1},{1,0},{2,3},{3,2},{4,5},{5,4},{6,7},{7,6},{8,9},{9,8},{10,11... | collective-permute-start | bytes 393224 | tf_op jit(solution)/shard_map/ppermute | solution.py:532
  32.7 1.8 %project.4 = (bf16[64,1024]{1,0:T(8,128)(2,1)S(1)}, f32[64,1024]{1,0:T(8,128)S(1)}, bf16[64,2048]{1,0:T(8,128)(2,1)S(1)}, f32[64,2048]{1,0:T(8,128)S(1)}) custom-call(bf16[128,1024]{1,0:T(8,128)(2,1)S(1)} %get-tuple-element.62.att_ref, bf16[256,1024]{1,0:T(8,128)(2,1)S(1)} %finish.1.mix_ref, bf16[1024,4096]{1,0:T(8,128)(2,1)S(1)} %get-tuple-element.59.wa_ref, ...), custom_call_target="tpu_custom_call" | custom-call | flops 1610612736 | bytes 2359296 | tf_op jit(solution)/shard_map/project/pallas_call | solution.py:458
  34.5 0.5 collective-permute-start.18
  35.0 1.6 %collective-permute-start.17 = (bf16[64,2048]{1,0:T(8,128)(2,1)S(1)}, bf16[64,2048]{1,0:T(8,128)(2,1)S(1)}, u32[]{:S(2)}, u32[]{:S(2)}) collective-permute-start(bf16[64,2048]{1,0:T(8,128)(2,1)S(1)} %get-tuple-element.71), channel_id=1, source_target_pairs={{0,1},{1,0},{2,3},{3,2},{4,5},{5,4},{6,7},{7,6},{8,9},{9,8},{10,11... | collective-permute-start | bytes 786440 | tf_op jit(solution)/shard_map/ppermute | solution.py:532
  36.8 4.1 %collective-permute-done.18 = bf16[64,1024]{1,0:T(8,128)(2,1)S(1)} collective-permute-done((bf16[64,1024]{1,0:T(8,128)(2,1)S(1)}, bf16[64,1024]{1,0:T(8,128)(2,1)S(1)}, u32[]{:S(2)}, u32[]{:S(2)}) %collective-permute-start.18) | collective-permute-done | bytes 131104 | tf_op jit(solution)/shard_map/ppermute | solution.py:532
  41.0 2.7 %collective-permute-start.19 = (bf16[64,1024]{1,0:T(8,128)(2,1)S(1)}, bf16[64,1024]{1,0:T(8,128)(2,1)S(1)}, u32[]{:S(2)}, u32[]{:S(2)}) collective-permute-start(bf16[64,1024]{1,0:T(8,128)(2,1)S(1)} %add_convert_fusion.3), channel_id=1, source_target_pairs={{0,2},{1,3},{2,0},{3,1},{4,6},{5,7},{6,4},{7,5},{8,10},{9,11},{10,... | collective-permute-start | bytes 393224 | tf_op jit(solution)/shard_map/ppermute | solution.py:535
  43.6 1.6 %attention.3.att_ref = bf16[128,1024]{1,0:T(8,128)(2,1)S(1)} custom-call(s32[4]{0:T(128)} %refs_0_.5, s32[32]{0:T(128)} %refs_1_.7, bf16[256,1024]{1,0:T(8,128)(2,1)S(1)} %get-tuple-element.46.refs_2_, bf16[2,2048,256]{2,1,0:T(8,128)(2,1)S(1)} %get-tuple-element.67.refs_3_), custom_call_target="tpu_custom_call" | custom-call | tf_op jit(solution)/shard_map/attention/pallas_call | solution.py:52
  45.3 2.3 %project.5 = (bf16[64,4096]{1,0:T(8,128)(2,1)S(1)}, f32[64,4096]{1,0:T(8,128)S(1)}) custom-call(bf16[128,1024]{1,0:T(8,128)(2,1)S(1)} %attention.3.att_ref, bf16[256,1024]{1,0:T(8,128)(2,1)S(1)} %finish.1.mix_ref, bf16[1024,4096]{1,0:T(8,128)(2,1)S(1)} %get-tuple-element.59.wa_ref, bf16[1024,4096]{1,0:T(8,128)(2,1)S(1)} %get-tuple-element.60.wm_ref), custom_call_target="tpu_custom_call" | custom-call | tf_op jit(solution)/shard_map/project/pallas_call | solution.py:458
  47.6 1.0 %collective-permute-start.15 = (bf16[64,4096]{1,0:T(8,128)(2,1)S(1)}, bf16[64,4096]{1,0:T(8,128)(2,1)S(1)}, u32[]{:S(2)}, u32[]{:S(2)}) collective-permute-start(bf16[64,4096]{1,0:T(8,128)(2,1)S(1)} %get-tuple-element.69), channel_id=1, source_target_pairs={{0,1},{1,0},{2,3},{3,2},{4,5},{5,4},{6,7},{7,6},{8,9},{9,8},{10,11... | collective-permute-start | bytes 1572872 | tf_op jit(solution)/shard_map/ppermute | solution.py:532
  48.6 2.1 %collective-permute-start.20 = (bf16[64,2048]{1,0:T(8,128)(2,1)S(1)}, bf16[64,2048]{1,0:T(8,128)(2,1)S(1)}, u32[]{:S(2)}, u32[]{:S(2)}) collective-permute-start(bf16[64,2048]{1,0:T(8,128)(2,1)S(1)} %add_convert_fusion.1), channel_id=1, source_target_pairs={{0,2},{1,3},{2,0},{3,1},{4,6},{5,7},{6,4},{7,5},{8,10},{9,11},{10,... | collective-permute-start | bytes 786440 | tf_op jit(solution)/shard_map/ppermute | solution.py:535
  50.7 0.9 %collective-permute-start.16 = (bf16[64,1024]{1,0:T(8,128)(2,1)S(1)}, bf16[64,1024]{1,0:T(8,128)(2,1)S(1)}, u32[]{:S(2)}, u32[]{:S(2)}) collective-permute-start(bf16[64,1024]{1,0:T(8,128)(2,1)S(1)} %add_convert_fusion.5), channel_id=1, source_target_pairs={{0,2},{1,3},{2,0},{3,1},{4,6},{5,7},{6,4},{7,5},{8,10},{9,11},{10,... | collective-permute-start | bytes 393224 | tf_op jit(solution)/shard_map/ppermute | solution.py:535
  51.6 14.4 %collective-permute-done.20 = bf16[64,2048]{1,0:T(8,128)(2,1)S(1)} collective-permute-done((bf16[64,2048]{1,0:T(8,128)(2,1)S(1)}, bf16[64,2048]{1,0:T(8,128)(2,1)S(1)}, u32[]{:S(2)}, u32[]{:S(2)}) %collective-permute-start.20) | collective-permute-done | bytes 262176 | tf_op jit(solution)/shard_map/ppermute | solution.py:535
  66.1 2.4 %collective-permute-done.15 = bf16[64,4096]{1,0:T(8,128)(2,1)S(1)} collective-permute-done((bf16[64,4096]{1,0:T(8,128)(2,1)S(1)}, bf16[64,4096]{1,0:T(8,128)(2,1)S(1)}, u32[]{:S(2)}, u32[]{:S(2)}) %collective-permute-start.15) | collective-permute-done | bytes 524320 | tf_op jit(solution)/shard_map/ppermute | solution.py:532
  68.7 0.8 %pad_maximum_fusion = bf16[64,4096]{1,0:T(8,128)(2,1)} fusion(bf16[64,2048]{1,0:T(8,128)(2,1)S(1)} %add_convert_fusion, bf16[64,1024]{1,0:T(8,128)(2,1)S(1)} %get-tuple-element.80, bf16[64,1024]{1,0:T(8,128)(2,1)S(1)} %get-tuple-element.79), kind=kLoop, calls=%fused_computation | loop fusion | flops 1572864 | bytes 1048576 | tf_op jit(solution)/shard_map/concatenate | solution.py:564
  (26 shorter events, 0.9 us)
Async XLA Ops:
  1.0 11.5 %collective-permute-start = (bf16[2,256,256]{2,1,0:T(8,128)(2,1)S(1)}, bf16[2,256,256]{2,1,0:T(8,128)(2,1)S(1)}, u32[]{:S(2)}, u32[]{:S(2)}) collective-permute-start(bf16[2,256,256]{2,1,0:T(8,128)(2,1)S(1)} %pad_maximum_fusion.1.refs_3_), channel_id=1, source_target_pairs={{0,8},{4,12},{8,0},{12,4},{16,24},{20,28},{24,16},{28,20},{1,9},{5... | collective-permute-start | bytes 786440 | tf_op jit(solution)/shard_map/ppermute | solution.py:494
  4.0 13.4 %collective-permute-start.1 = (bf16[2,256,256]{2,1,0:T(8,128)(2,1)S(1)}, bf16[2,256,256]{2,1,0:T(8,128)(2,1)S(1)}, u32[]{:S(2)}, u32[]{:S(2)}) collective-permute-start(bf16[2,256,256]{2,1,0:T(8,128)(2,1)S(1)} %pad_maximum_fusion.1.refs_3_), channel_id=1, source_target_pairs={{0,16},{4,20},{8,24},{12,28},{16,0},{20,4},{24,8},{28,12},{1,17},{... | collective-permute-start | bytes 786440 | tf_op jit(solution)/shard_map/ppermute | solution.py:494
  5.5 11.9 %collective-permute-start.2 = (bf16[2,256,256]{2,1,0:T(8,128)(2,1)S(1)}, bf16[2,256,256]{2,1,0:T(8,128)(2,1)S(1)}, u32[]{:S(2)}, u32[]{:S(2)}) collective-permute-start(bf16[2,256,256]{2,1,0:T(8,128)(2,1)S(1)} %pad_maximum_fusion.1.refs_3_), channel_id=1, source_target_pairs={{0,24},{4,28},{8,16},{12,20},{16,8},{20,12},{24,0},{28,4},{1,25},{... | collective-permute-start | bytes 786440 | tf_op jit(solution)/shard_map/ppermute | solution.py:494
  8.3 9.6 %collective-permute-start.7 = (bf16[2,528,128]{2,1,0:T(8,128)(2,1)S(1)}, bf16[2,528,128]{2,1,0:T(8,128)(2,1)S(1)}, u32[]{:S(2)}, u32[]{:S(2)}) collective-permute-start(bf16[2,528,128]{2,1,0:T(8,128)(2,1)S(1)} %get-tuple-element.44.refs_0_.mine_ref), channel_id=1, source_target_pairs={{0,4},{4,0},{8,12},{12,8},{16,20},{20,16},{24,28},{28,24},{1,5},{5... | collective-permute-start | bytes 811016 | tf_op jit(solution)/shard_map/ppermute | solution.py:497
  8.4 11.2 %collective-permute-start.3 = (bf16[2,256,256]{2,1,0:T(8,128)(2,1)S(1)}, bf16[2,256,256]{2,1,0:T(8,128)(2,1)S(1)}, u32[]{:S(2)}, u32[]{:S(2)}) collective-permute-start(bf16[2,256,256]{2,1,0:T(8,128)(2,1)S(1)} %pad_maximum_fusion.1.refs_3_), channel_id=1, source_target_pairs={{0,4},{4,0},{8,12},{12,8},{16,20},{20,16},{24,28},{28,24},{1,5},{5... | collective-permute-start | bytes 786440 | tf_op jit(solution)/shard_map/ppermute | solution.py:497
  17.4 3.6 %collective-permute-start.4 = (bf16[2,256,256]{2,1,0:T(8,128)(2,1)S(1)}, bf16[2,256,256]{2,1,0:T(8,128)(2,1)S(1)}, u32[]{:S(2)}, u32[]{:S(2)}) collective-permute-start(bf16[2,256,256]{2,1,0:T(8,128)(2,1)S(1)} %collective-permute-done.refs_5_), channel_id=1, source_target_pairs={{0,4},{4,0},{8,12},{12,8},{16,20},{20,16},{24,28},{28,24},{1,5},{5... | collective-permute-start | bytes 786440 | tf_op jit(solution)/shard_map/ppermute | solution.py:497
  17.4 4.1 %collective-permute-start.5 = (bf16[2,256,256]{2,1,0:T(8,128)(2,1)S(1)}, bf16[2,256,256]{2,1,0:T(8,128)(2,1)S(1)}, u32[]{:S(2)}, u32[]{:S(2)}) collective-permute-start(bf16[2,256,256]{2,1,0:T(8,128)(2,1)S(1)} %collective-permute-done.1.refs_7_), channel_id=1, source_target_pairs={{0,4},{4,0},{8,12},{12,8},{16,20},{20,16},{24,28},{28,24},{1,5},{5... | collective-permute-start | bytes 786440 | tf_op jit(solution)/shard_map/ppermute | solution.py:497
  17.9 3.6 %collective-permute-start.6 = (bf16[2,256,256]{2,1,0:T(8,128)(2,1)S(1)}, bf16[2,256,256]{2,1,0:T(8,128)(2,1)S(1)}, u32[]{:S(2)}, u32[]{:S(2)}) collective-permute-start(bf16[2,256,256]{2,1,0:T(8,128)(2,1)S(1)} %collective-permute-done.2.refs_9_), channel_id=1, source_target_pairs={{0,4},{4,0},{8,12},{12,8},{16,20},{20,16},{24,28},{28,24},{1,5},{5... | collective-permute-start | bytes 786440 | tf_op jit(solution)/shard_map/ppermute | solution.py:497
  18.0 7.8 %collective-permute-start.10 = (bf16[528,128]{1,0:T(8,128)(2,1)S(1)}, bf16[528,128]{1,0:T(8,128)(2,1)S(1)}, u32[]{:S(2)}, u32[]{:S(2)}) collective-permute-start(bf16[528,128]{1,0:T(8,128)(2,1)S(1)} %compose.1), channel_id=1, source_target_pairs={{0,24},{4,28},{8,16},{12,20},{16,8},{20,12},{24,0},{28,4},{1,25},{... | collective-permute-start | bytes 405512 | tf_op jit(solution)/shard_map/ppermute | solution.py:494
  19.5 8.4 %collective-permute-start.8 = (bf16[528,128]{1,0:T(8,128)(2,1)S(1)}, bf16[528,128]{1,0:T(8,128)(2,1)S(1)}, u32[]{:S(2)}, u32[]{:S(2)}) collective-permute-start(bf16[528,128]{1,0:T(8,128)(2,1)S(1)} %compose.1), channel_id=1, source_target_pairs={{0,8},{4,12},{8,0},{12,4},{16,24},{20,28},{24,16},{28,20},{1,9},{5... | collective-permute-start | bytes 405512 | tf_op jit(solution)/shard_map/ppermute | solution.py:494
  21.0 6.9 %collective-permute-start.9 = (bf16[528,128]{1,0:T(8,128)(2,1)S(1)}, bf16[528,128]{1,0:T(8,128)(2,1)S(1)}, u32[]{:S(2)}, u32[]{:S(2)}) collective-permute-start(bf16[528,128]{1,0:T(8,128)(2,1)S(1)} %compose.1), channel_id=1, source_target_pairs={{0,16},{4,20},{8,24},{12,28},{16,0},{20,4},{24,8},{28,12},{1,17},{... | collective-permute-start | bytes 405512 | tf_op jit(solution)/shard_map/ppermute | solution.py:494
  27.9 1.4 %collective-permute-start.11 = (bf16[528,128]{1,0:T(8,128)(2,1)S(1)}, bf16[528,128]{1,0:T(8,128)(2,1)S(1)}, u32[]{:S(2)}, u32[]{:S(2)}) collective-permute-start(bf16[528,128]{1,0:T(8,128)(2,1)S(1)} %collective-permute-done.8.refs_4_), channel_id=1, source_target_pairs={{0,4},{4,0},{8,12},{12,8},{16,20},{20,16},{24,28},{28,24},{1,5},{5... | collective-permute-start | bytes 405512 | tf_op jit(solution)/shard_map/ppermute | solution.py:497
  27.9 1.5 %collective-permute-start.12 = (bf16[528,128]{1,0:T(8,128)(2,1)S(1)}, bf16[528,128]{1,0:T(8,128)(2,1)S(1)}, u32[]{:S(2)}, u32[]{:S(2)}) collective-permute-start(bf16[528,128]{1,0:T(8,128)(2,1)S(1)} %collective-permute-done.9.refs_6_), channel_id=1, source_target_pairs={{0,4},{4,0},{8,12},{12,8},{16,20},{20,16},{24,28},{28,24},{1,5},{5... | collective-permute-start | bytes 405512 | tf_op jit(solution)/shard_map/ppermute | solution.py:497
  28.4 1.4 %collective-permute-start.13 = (bf16[528,128]{1,0:T(8,128)(2,1)S(1)}, bf16[528,128]{1,0:T(8,128)(2,1)S(1)}, u32[]{:S(2)}, u32[]{:S(2)}) collective-permute-start(bf16[528,128]{1,0:T(8,128)(2,1)S(1)} %collective-permute-done.10.refs_8_), channel_id=1, source_target_pairs={{0,4},{4,0},{8,12},{12,8},{16,20},{20,16},{24,28},{28,24},{1,5},{5... | collective-permute-start | bytes 405512 | tf_op jit(solution)/shard_map/ppermute | solution.py:497
  31.1 5.7 %collective-permute-start.14 = (bf16[64,1024]{1,0:T(8,128)(2,1)S(1)}, bf16[64,1024]{1,0:T(8,128)(2,1)S(1)}, u32[]{:S(2)}, u32[]{:S(2)}) collective-permute-start(bf16[64,1024]{1,0:T(8,128)(2,1)S(1)} %get-tuple-element.66), channel_id=1, source_target_pairs={{0,1},{1,0},{2,3},{3,2},{4,5},{5,4},{6,7},{7,6},{8,9},{9,8},{10,11... | collective-permute-start | bytes 393224 | tf_op jit(solution)/shard_map/ppermute | solution.py:532
  34.5 6.4 %collective-permute-start.18 = (bf16[64,1024]{1,0:T(8,128)(2,1)S(1)}, bf16[64,1024]{1,0:T(8,128)(2,1)S(1)}, u32[]{:S(2)}, u32[]{:S(2)}) collective-permute-start(bf16[64,1024]{1,0:T(8,128)(2,1)S(1)} %get-tuple-element.73), channel_id=1, source_target_pairs={{0,1},{1,0},{2,3},{3,2},{4,5},{5,4},{6,7},{7,6},{8,9},{9,8},{10,11... | collective-permute-start | bytes 393224 | tf_op jit(solution)/shard_map/ppermute | solution.py:532
  35.0 13.6 %collective-permute-start.17 = (bf16[64,2048]{1,0:T(8,128)(2,1)S(1)}, bf16[64,2048]{1,0:T(8,128)(2,1)S(1)}, u32[]{:S(2)}, u32[]{:S(2)}) collective-permute-start(bf16[64,2048]{1,0:T(8,128)(2,1)S(1)} %get-tuple-element.71), channel_id=1, source_target_pairs={{0,1},{1,0},{2,3},{3,2},{4,5},{5,4},{6,7},{7,6},{8,9},{9,8},{10,11... | collective-permute-start | bytes 786440 | tf_op jit(solution)/shard_map/ppermute | solution.py:532
  41.0 7.6 %collective-permute-start.19 = (bf16[64,1024]{1,0:T(8,128)(2,1)S(1)}, bf16[64,1024]{1,0:T(8,128)(2,1)S(1)}, u32[]{:S(2)}, u32[]{:S(2)}) collective-permute-start(bf16[64,1024]{1,0:T(8,128)(2,1)S(1)} %add_convert_fusion.3), channel_id=1, source_target_pairs={{0,2},{1,3},{2,0},{3,1},{4,6},{5,7},{6,4},{7,5},{8,10},{9,11},{10,... | collective-permute-start | bytes 393224 | tf_op jit(solution)/shard_map/ppermute | solution.py:535
  47.6 20.8 %collective-permute-start.15 = (bf16[64,4096]{1,0:T(8,128)(2,1)S(1)}, bf16[64,4096]{1,0:T(8,128)(2,1)S(1)}, u32[]{:S(2)}, u32[]{:S(2)}) collective-permute-start(bf16[64,4096]{1,0:T(8,128)(2,1)S(1)} %get-tuple-element.69), channel_id=1, source_target_pairs={{0,1},{1,0},{2,3},{3,2},{4,5},{5,4},{6,7},{7,6},{8,9},{9,8},{10,11... | collective-permute-start | bytes 1572872 | tf_op jit(solution)/shard_map/ppermute | solution.py:532
  48.6 17.4 %collective-permute-start.20 = (bf16[64,2048]{1,0:T(8,128)(2,1)S(1)}, bf16[64,2048]{1,0:T(8,128)(2,1)S(1)}, u32[]{:S(2)}, u32[]{:S(2)}) collective-permute-start(bf16[64,2048]{1,0:T(8,128)(2,1)S(1)} %add_convert_fusion.1), channel_id=1, source_target_pairs={{0,2},{1,3},{2,0},{3,1},{4,6},{5,7},{6,4},{7,5},{8,10},{9,11},{10,... | collective-permute-start | bytes 786440 | tf_op jit(solution)/shard_map/ppermute | solution.py:535
  50.7 17.8 %collective-permute-start.16 = (bf16[64,1024]{1,0:T(8,128)(2,1)S(1)}, bf16[64,1024]{1,0:T(8,128)(2,1)S(1)}, u32[]{:S(2)}, u32[]{:S(2)}) collective-permute-start(bf16[64,1024]{1,0:T(8,128)(2,1)S(1)} %add_convert_fusion.5), channel_id=1, source_target_pairs={{0,2},{1,3},{2,0},{3,1},{4,6},{5,7},{6,4},{7,5},{8,10},{9,11},{10,... | collective-permute-start | bytes 393224 | tf_op jit(solution)/shard_map/ppermute | solution.py:535

commit v5 on v4

--- a/solution.py
+++ b/solution.py
@@ -248,17 +248,7 @@
     if later:
         kv, out_ref, qs, sc, mx, ls, acc = refs
     else:
-        *got, weight_ref, out_ref, kv, ready_ref, inv, qs, sc, mx, ls, acc, weight_sem = refs
-        pieces = weight_sem.shape[0]
-        depth = weight_ref.shape[0] // pieces
-        fetches = []
-        for i in range(pieces):
-            here = slice(i * depth, (i + 1) * depth)
-            fetches.append(
-                pltpu.make_async_copy(weight_ref.at[here], ready_ref.at[here], weight_sem.at[i])
-            )
-        for f in fetches:
-            f.start()
+        *got, out_ref, kv, inv, qs, sc, mx, ls, acc = refs
     me = lax.axis_index("ctx")
     z = lax.axis_index("tp")
     keys = q_ref.shape[0]
@@ -294,13 +284,16 @@
     for h in range(kv_heads * group):
         g, i = divmod(h, group)
         qs[g, i * rows : (i + 1) * rows, :] = q_ref[here, h * HEAD_DIM : (h + 1) * HEAD_DIM]
-    row = lax.rem(lax.broadcasted_iota(jnp.int32, (stacked, 1), 0), rows)
+    row = lax.rem(lax.broadcasted_iota(jnp.int32, (min(stacked, 256), 1), 0), rows)
     t_pos = me * keys + side * rows + row
     t_start = doc_start(t_pos, ends)
     scale = LOG2E * HEAD_DIM ** (-0.5)
 
     def lanes(g):
         return slice(g * HEAD_DIM, (g + 1) * HEAD_DIM)
+
+    unit = min(stacked, 256)
+    units = [(g, slice(r, r + unit)) for g in range(kv_heads) for r in range(0, stacked, unit)]
 
     def scores(block, own):
         at = pl.ds(pl.multiple_of(block * keys, keys), keys)
@@ -308,14 +301,14 @@
         shown = u_pos >= t_start
         if own:
             shown = shown & (u_pos <= t_pos)
-        for g in range(kv_heads):
-            s = nt(qs[g], kv[0, at, lanes(g)])
+        for g, r in units:
+            s = nt(qs[g, r, :], kv[0, at, lanes(g)])
             s = jnp.where(shown, s * scale, LOW)
-            sc[block - low_block, g] = s
+            sc[block - low_block, g, r, :] = s
             top = s[:, :128]
             for k in range(128, keys, 128):
                 top = jnp.maximum(top, s[:, k : k + 128])
-            mx[g] = top if own else jnp.maximum(mx[g], top)
+            mx[g, r, :] = top if own else jnp.maximum(mx[g, r, :], top)
 
     scores(me, True)
 
@@ -329,16 +322,16 @@
 
     def weigh(block, own):
         at = pl.ds(pl.multiple_of(block * keys, keys), keys)
-        for g in range(kv_heads):
-            m = mx[g]
+        for g, r in units:
+            m = mx[g, r, :]
             total, pieces = None, []
             for k in range(0, keys, 128):
-                w = jnp.exp2(sc[block - low_block, g, :, k : k + 128] - m)
+                w = jnp.exp2(sc[block - low_block, g, r, k : k + 128] - m)
                 total = w if total is None else total + w
                 pieces.append(w.astype(BF16))
             term = nn(jnp.concatenate(pieces, axis=1), kv[1, at, lanes(g)])
-            ls[g] = total if own else ls[g] + total
-            acc[g] = term if own else acc[g] + term
+            ls[g, r, :] = total if own else ls[g, r, :] + total
+            acc[g, r, :] = term if own else acc[g, r, :] + term
 
     weigh(me, True)
 
@@ -357,12 +350,9 @@
                 at = pl.multiple_of(slot * part, part)
                 src = i * rows + q * part
                 out_ref[pl.ds(at, part), h * HEAD_DIM : (h + 1) * HEAD_DIM] = res[src : src + part]
-    if not later:
-        for f in fetches:
-            f.wait()
-
-
-def attention(page_len, doc_lengths, page_table, queries, kv_heads, got=(), weight=None, kv=None):
+
+
+def attention(page_len, doc_lengths, page_table, queries, kv_heads, got=(), kv=None):
     later = kv is not None
     keys = queries.shape[0]
     rows = keys // 2
@@ -379,21 +369,17 @@
         stat,
         stat,
     ]
-    near, specs = (queries, kv), None
+    near = (queries, kv)
     if not later:
         out.append(jax.ShapeDtypeStruct((2, total, width), BF16))
-        out.append(jax.ShapeDtypeStruct(weight.shape, weight.dtype))
         scratch.insert(0, pltpu.SMEM((page_table.shape[0],), jnp.int32))
-        scratch.append(pltpu.SemaphoreType.DMA((4,)))
-        near = (queries, *got, in_hbm(weight))
-        specs = [VMEM_SPEC] * (1 + len(got)) + [HBM_SPEC]
+        near = (queries, *got)
     return one_step(
         functools.partial(attention_kernel, page_len, later),
         "attention",
         out,
         (Far(doc_lengths, pltpu.SMEM), Far(page_table, pltpu.SMEM)),
         near,
-        specs=specs,
         scratch=scratch,
         cost=((0 if later else 1280) * 1280 * group * rows * 128, 0 if later else 4 << 20, 0),
         room=5 * MIB + 4 * kv_heads * group * rows * keys * blocks,
@@ -470,6 +456,59 @@
     )(att, mix, wa, wm)
 
 
+def pack_kernel(key_ref, value_ref, out_ref, sem):
+    copies = [
+        pltpu.make_async_copy(ref, out_ref.at[i], sem.at[i])
+        for i, ref in enumerate((key_ref, value_ref))
+    ]
+    for c in copies:
+        c.start()
+    for c in copies:
+        c.wait()
+
+
+def pack(keys, values):
+    return pl.pallas_call(
+        pack_kernel,
+        out_shape=jax.ShapeDtypeStruct((2,) + keys.shape, keys.dtype),
+        in_specs=[HBM_SPEC] * 2,
+        out_specs=VMEM_SPEC,
+        scratch_shapes=[pltpu.SemaphoreType.DMA((2,))],
+        compiler_params=pltpu.CompilerParams(vmem_limit_bytes=1 * MIB),
+        cost_estimate=pl.CostEstimate(flops=0, bytes_accessed=0, transcendentals=0),
+        name="pack",
+    )(in_hbm(keys), in_hbm(values))
+
+
+def assemble_kernel(keep_ref, near_ref, *refs):
+    *last, out_ref, held, sem = refs
+    at, copies = 0, []
+    for ref in last:
+        here = slice(at, at + ref.shape[1])
+        total = keep_ref[:, here] + near_ref[:, here].astype(F32) + ref[...].astype(F32)
+        held[:, here] = total.astype(BF16)
+        copies.append(
+            pltpu.make_async_copy(held.at[:, here], out_ref.at[:, here], sem.at[len(copies)])
+        )
+        copies[-1].start()
+        at += ref.shape[1]
+    for c in copies:
+        c.wait()
+
+
+def assemble(keep, near, last):
+    return pl.pallas_call(
+        assemble_kernel,
+        out_shape=jax.ShapeDtypeStruct(keep.shape, BF16),
+        in_specs=[VMEM_SPEC] * (2 + len(last)),
+        out_specs=HBM_SPEC,
+        scratch_shapes=[pltpu.VMEM(keep.shape, BF16), pltpu.SemaphoreType.DMA((len(last),))],
+        compiler_params=pltpu.CompilerParams(vmem_limit_bytes=2 * MIB),
+        cost_estimate=pl.CostEstimate(flops=0, bytes_accessed=0, transcendentals=0),
+        name="assemble",
+    )(keep, near, *last)
+
+
 def shards(
     n_ctx,
     n_tp,
@@ -497,7 +536,7 @@
         return lax.ppermute(a, "ctx", [(i, i ^ 1) for i in range(n_ctx)])
 
     width = key_pages.shape[2]
-    kv = jnp.stack([key_pages.reshape(-1, width), value_pages.reshape(-1, width)])
+    kv = pack(key_pages.reshape(-1, width), value_pages.reshape(-1, width))
     kv, mixer_input = lax.optimization_barrier((kv, mixer_input))
     far = [kv] + [between_chips(kv, j) for j in range(1, chips)]
 
@@ -506,8 +545,8 @@
     )
     st_other = other_core(st)
     chip_state = compose(st, st_other)
-    near_weight, near_queries, near_read = fetch(
-        st, attention_weight, queries, state_read
+    near_weight, far_weight, near_queries, near_read = fetch(
+        st, attention_weight, mixer_weight, queries, state_read
     )
     far_states = [between_chips(chip_state, j) for j in range(1, chips)]
 
@@ -516,7 +555,7 @@
     for a in far:
         got += [a, other_core(a)]
     place = (page_len, doc_lengths, page_table, near_queries, width // HEAD_DIM)
-    att, kv, far_weight = attention(*place, got, mixer_weight)
+    att, kv = attention(*place, got)
     *far_states, att = lax.optimization_barrier((*far_states, att))
     got_states = []
     for a in far_states:
@@ -544,24 +583,17 @@
         if order is not None:
             near_other[k], order = lax.optimization_barrier((near_other[k], order))
         if k == 2:
+            near_other[k], last[0] = lax.optimization_barrier((near_other[k], last[0]))
+        if k == 2:
             near_other[k], last[1] = lax.optimization_barrier((near_other[k], last[1]))
         order = (keep + near_other[k].astype(F32)).astype(BF16)
         if k == 0:
             kv, order = lax.optimization_barrier((kv, order))
         last.append(across(order))
     (later,) = attention(*place, kv=kv)
-    own_widths = (columns // 1,) * 1
-    sums = project(1, later, mix, *weights, 0, own_widths, 256)
-    near_own = [neighbour(a) for a in sums[::2]]
-    near_own = near_own[0] if 1 == 1 else jnp.concatenate(near_own, axis=1)
-    keep_own = sums[1] if 1 == 1 else jnp.concatenate(sums[1::2], axis=1)
-    pieces, at = [], 0
-    for a in last:
-        here = slice(at, at + a.shape[1])
-        own = keep_own[:, here] + near_own[:, here].astype(F32) + a.astype(F32)
-        pieces.append(own.astype(BF16))
-        at += a.shape[1]
-    return jnp.concatenate(pieces, axis=1)
+    send_own, keep_own = project(1, later, mix, *weights, 0, (columns,), 256)
+    near_own = neighbour(send_own)
+    return assemble(keep_own, near_own, last)
 
 
 def solution(mesh):

time: 69.7 us -> 69.1 us (level)
  starting transfers between devices: 20 us -> 17 us
  waiting for transfers between devices: 29.6 us -> 32.2 us
  other arithmetic: 2.12 us -> 0.1 us
  Pallas kernels: 17.6 us -> 19.6 us
    ppermute x3, starting transfers between devices: 5.65 us -> 2.79 us  [across(): return lax.ppermute(a, 'tp', [(i, i ^ 2) for i in range(n_tp)])]
    pallas_call x1, Pallas kernels: 3.59 us -> 6.01 us  [fetch(): pl.pallas_call(functools.partial(fetch_kernel, 4), out_shape=tuple((jax.S...]
    pallas_call x4, Pallas kernels: 9.1 us -> 6.74 us  [one_step(): pl.pallas_call(body, out_shape=tuple(out_shape), in_specs=[HBM_SPEC] * le...]
    pallas_call x0 -> x2, Pallas kernels: none -> 1.88 us  [the longest x1 0.98 us: pack(): pl.pallas_call(pack_kernel, out_shape=jax.ShapeDtypeStruct((2,) + keys.sh...]
    ppermute x3, waiting for transfers between devices: 14.4 us -> 15.8 us  [across(): return lax.ppermute(a, 'tp', [(i, i ^ 2) for i in range(n_tp)])]
    ppermute x4, waiting for transfers between devices: 6.7 us -> 7.98 us  [neighbour(): return lax.ppermute(a, 'tp', [(i, i ^ 1) for i in range(n_tp)])]
    another operation x1 -> x0, other arithmetic: 0.99 us -> none  [shards(): jnp.stack([key_pages.reshape(-1, width), value_pages.reshape(-1, width)])]
    concatenate x1 -> x0, other arithmetic: 0.83 us -> none  [shards(): return jnp.concatenate(pieces, axis=1)]
  transfers between devices with their start and end apart: 21 -> 21, of which waited for: 9 -> 12; matrix products, arithmetic and copies ran while one was open for 0% -> 0% of each run, Pallas kernels for 24% -> 24%
where the time goes in v5:
time: 69.1 us; the launch traced here: 68.9 us
  waiting for transfers between devices  32.2 us (47%)
  Pallas kernels  19.6 us (28%)
  starting transfers between devices  17 us (25%)
    ppermute x3, waiting for transfers between devices, across(): return lax.ppermute(a, 'tp', [(i, i ^ 2) for i in range(n_tp)])  15.8 us
    ppermute x6, starting transfers between devices, between_chips(): return lax.ppermute(a, 'ctx', [(i, i ^ 2 * j) for i in range(n_ctx)])  8.1 us
    ppermute x4, waiting for transfers between devices, neighbour(): return lax.ppermute(a, 'tp', [(i, i ^ 1) for i in range(n_tp)])  7.98 us
    ppermute x6, waiting for transfers between devices, between_chips(): return lax.ppermute(a, 'ctx', [(i, i ^ 2 * j) for i in range(n_ctx)])  7.04 us
    pallas_call x4, Pallas kernels, one_step(): pl.pallas_call(body, out_shape=tuple(out_shape), in_specs=[HBM_SPEC] * le...  6.74 us
    pallas_call x1, Pallas kernels, fetch(): pl.pallas_call(functools.partial(fetch_kernel, 4), out_shape=tuple((jax.S...  6.01 us
    pallas_call x3, Pallas kernels, project(): pl.pallas_call(functools.partial(project_kernel, start, tile, side), out_...  4.86 us
    ppermute x4, starting transfers between devices, neighbour(): return lax.ppermute(a, 'tp', [(i, i ^ 1) for i in range(n_tp)])  4.46 us
  transfers between devices with their start and end apart: 21, of which 12 were waited for; matrix products, arithmetic and copies ran while one was open for 0% of the time, Pallas kernels for 24%

profile of v5, /device:TPU:0, one launch (start us, length us, event | category | flops | bytes accessed | tf_op | source)
XLA Modules:
  0.0 68.9 jit_solution(14542264290654992192)
XLA Ops:
  0.0 1.0 %pack.1.refs_3_ = bf16[2,256,256]{2,1,0:T(8,128)(2,1)S(1)} custom-call(bf16[256,256]{1,0:T(8,128)(2,1)} %bitcast.2, bf16[256,256]{1,0:T(8,128)(2,1)} %bitcast.3), custom_call_target="tpu_custom_call" | custom-call | tf_op jit(solution)/shard_map/pack/pallas_call | solution.py:471
  1.0 3.0 %collective-permute-start = (bf16[2,256,256]{2,1,0:T(8,128)(2,1)S(1)}, bf16[2,256,256]{2,1,0:T(8,128)(2,1)S(1)}, u32[]{:S(2)}, u32[]{:S(2)}) collective-permute-start(bf16[2,256,256]{2,1,0:T(8,128)(2,1)S(1)} %pack.1.refs_3_), channel_id=1, source_target_pairs={{0,8},{4,12},{8,0},{12,4},{16,24},{20,28},{24,16},{28,20},{1,9},{5... | collective-permute-start | bytes 786440 | tf_op jit(solution)/shard_map/ppermute | solution.py:533
  4.0 1.5 %collective-permute-start.1 = (bf16[2,256,256]{2,1,0:T(8,128)(2,1)S(1)}, bf16[2,256,256]{2,1,0:T(8,128)(2,1)S(1)}, u32[]{:S(2)}, u32[]{:S(2)}) collective-permute-start(bf16[2,256,256]{2,1,0:T(8,128)(2,1)S(1)} %pack.1.refs_3_), channel_id=1, source_target_pairs={{0,16},{4,20},{8,24},{12,28},{16,0},{20,4},{24,8},{28,12},{1,17},{... | collective-permute-start | bytes 786440 | tf_op jit(solution)/shard_map/ppermute | solution.py:533
  5.5 2.7 %mixer_local.1 = (f32[256,1024]{1,0:T(8,128)S(1)}, bf16[2,528,128]{2,1,0:T(8,128)(2,1)S(1)}, f32[256,8]{1,0:T(8,128)S(1)}) custom-call(s32[4]{0:T(128)} %refs_0_.5, f32[8]{0:T(128)} %refs_1_.4, bf16[256,1024]{1,0:T(8,128)(2,1)} %refs_2_.1, bf16[256,256]{1,0:T(8,128)(2,1)} %refs_3_.2, bf16[256,256]{1,0:T(8,128)(2,1)} %refs_4_.3, f32[8,256]{1,0:T(8,128)} %refs_5_.1), custom_call_target="tpu_custom_call" | custom-call | tf_op jit(solution)/shard_map/mixer_local/pallas_call | solution.py:52
  8.4 0.5 collective-permute-start.3
  8.9 6.0 %fetch.1 = (bf16[1024,4096]{1,0:T(8,128)(2,1)S(1)}, bf16[1024,4096]{1,0:T(8,128)(2,1)S(1)}, bf16[256,1024]{1,0:T(8,128)(2,1)S(1)}, bf16[256,256]{1,0:T(8,128)(2,1)S(1)}) custom-call(bf16[2,528,128]{2,1,0:T(8,128)(2,1)S(1)} %get-tuple-element.46.refs_0_.mine_ref, bf16[1024,4096]{1,0:T(8,128)(2,1)} %refs_1_.5, bf16[1024,4096]{1,0:T(8,128)(2,1)} %refs_2_.2, ...), custom_call_target="tpu_custom_call" | custom-call | bytes 17432576 | tf_op jit(solution)/shard_map/fetch/pallas_call | solution.py:410
  14.9 2.5 %collective-permute-done.1.refs_7_ = bf16[2,256,256]{2,1,0:T(8,128)(2,1)S(1)} collective-permute-done((bf16[2,256,256]{2,1,0:T(8,128)(2,1)S(1)}, bf16[2,256,256]{2,1,0:T(8,128)(2,1)S(1)}, u32[]{:S(2)}, u32[]{:S(2)}) %collective-permute-start.1) | collective-permute-done | bytes 262176 | tf_op jit(solution)/shard_map/ppermute | solution.py:533
  17.4 0.5 collective-permute-start.5
  18.0 1.6 %collective-permute-start.10 = (bf16[528,128]{1,0:T(8,128)(2,1)S(1)}, bf16[528,128]{1,0:T(8,128)(2,1)S(1)}, u32[]{:S(2)}, u32[]{:S(2)}) collective-permute-start(bf16[528,128]{1,0:T(8,128)(2,1)S(1)} %compose.1), channel_id=1, source_target_pairs={{0,24},{4,28},{8,16},{12,20},{16,8},{20,12},{24,0},{28,4},{1,25},{... | collective-permute-start | bytes 405512 | tf_op jit(solution)/shard_map/ppermute | solution.py:533
  19.5 1.5 %collective-permute-start.8 = (bf16[528,128]{1,0:T(8,128)(2,1)S(1)}, bf16[528,128]{1,0:T(8,128)(2,1)S(1)}, u32[]{:S(2)}, u32[]{:S(2)}) collective-permute-start(bf16[528,128]{1,0:T(8,128)(2,1)S(1)} %compose.1), channel_id=1, source_target_pairs={{0,8},{4,12},{8,0},{12,4},{16,24},{20,28},{24,16},{28,20},{1,9},{5... | collective-permute-start | bytes 405512 | tf_op jit(solution)/shard_map/ppermute | solution.py:533
  21.0 0.5 collective-permute-start.9
  21.5 1.8 %attention.2 = (bf16[128,1024]{1,0:T(8,128)(2,1)S(1)}, bf16[2,2048,256]{2,1,0:T(8,128)(2,1)S(1)}) custom-call(s32[4]{0:T(128)} %refs_0_.5, s32[32]{0:T(128)} %refs_1_.7, bf16[256,1024]{1,0:T(8,128)(2,1)S(1)} %get-tuple-element.48.refs_2_, bf16[2,256,256]{2,1,0:T(8,128)(2,1)S(1)} %pack.1.refs_3_, bf16[2,256,256]{2,1,0:T(8,128)(2,1)S(1)} %collective-permute-done.3.refs_4_, ...), custom_call_target="tpu_custom_call" | custom-call | flops 107374182400 | bytes 4194304 | tf_op jit(solution)/shard_map/attention/pallas_call | solution.py:52
  23.4 1.9 %collective-permute-done.10.refs_8_ = bf16[528,128]{1,0:T(8,128)(2,1)S(1)} collective-permute-done((bf16[528,128]{1,0:T(8,128)(2,1)S(1)}, bf16[528,128]{1,0:T(8,128)(2,1)S(1)}, u32[]{:S(2)}, u32[]{:S(2)}) %collective-permute-start.10) | collective-permute-done | bytes 135200 | tf_op jit(solution)/shard_map/ppermute | solution.py:533
  25.3 2.6 %collective-permute-done.8.refs_4_ = bf16[528,128]{1,0:T(8,128)(2,1)S(1)} collective-permute-done((bf16[528,128]{1,0:T(8,128)(2,1)S(1)}, bf16[528,128]{1,0:T(8,128)(2,1)S(1)}, u32[]{:S(2)}, u32[]{:S(2)}) %collective-permute-start.8) | collective-permute-done | bytes 135200 | tf_op jit(solution)/shard_map/ppermute | solution.py:533
  27.9 0.5 collective-permute-start.12
  28.4 0.8 %collective-permute-done.11.refs_5_ = bf16[528,128]{1,0:T(8,128)(2,1)S(1)} collective-permute-done((bf16[528,128]{1,0:T(8,128)(2,1)S(1)}, bf16[528,128]{1,0:T(8,128)(2,1)S(1)}, u32[]{:S(2)}, u32[]{:S(2)}) %collective-permute-start.11) | collective-permute-done | bytes 135200 | tf_op jit(solution)/shard_map/ppermute | solution.py:536
  29.8 0.5 finish.1.mix_ref
  30.3 0.7 %project.3 = (bf16[64,1024]{1,0:T(8,128)(2,1)S(1)}, f32[64,1024]{1,0:T(8,128)S(1)}) custom-call(bf16[128,1024]{1,0:T(8,128)(2,1)S(1)} %get-tuple-element.64.att_ref, bf16[256,1024]{1,0:T(8,128)(2,1)S(1)} %finish.1.mix_ref, bf16[1024,4096]{1,0:T(8,128)(2,1)S(1)} %get-tuple-element.61.wa_ref, bf16[1024,4096]{1,0:T(8,128)(2,1)S(1)} %get-tuple-element.62.wm_ref), custom_call_target="tpu_custom_call" | custom-call | flops 536870912 | bytes 786432 | tf_op jit(solution)/shard_map/project/pallas_call | solution.py:444
  31.1 1.6 %collective-permute-start.14 = (bf16[64,1024]{1,0:T(8,128)(2,1)S(1)}, bf16[64,1024]{1,0:T(8,128)(2,1)S(1)}, u32[]{:S(2)}, u32[]{:S(2)}) collective-permute-start(bf16[64,1024]{1,0:T(8,128)(2,1)S(1)} %get-tuple-element.68), channel_id=1, source_target_pairs={{0,1},{1,0},{2,3},{3,2},{4,5},{5,4},{6,7},{7,6},{8,9},{9,8},{10,11... | collective-permute-start | bytes 393224 | tf_op jit(solution)/shard_map/ppermute | solution.py:571
  32.7 1.8 %project.4 = (bf16[64,1024]{1,0:T(8,128)(2,1)S(1)}, f32[64,1024]{1,0:T(8,128)S(1)}, bf16[64,2048]{1,0:T(8,128)(2,1)S(1)}, f32[64,2048]{1,0:T(8,128)S(1)}) custom-call(bf16[128,1024]{1,0:T(8,128)(2,1)S(1)} %get-tuple-element.64.att_ref, bf16[256,1024]{1,0:T(8,128)(2,1)S(1)} %finish.1.mix_ref, bf16[1024,4096]{1,0:T(8,128)(2,1)S(1)} %get-tuple-element.61.wa_ref, ...), custom_call_target="tpu_custom_call" | custom-call | flops 1610612736 | bytes 2359296 | tf_op jit(solution)/shard_map/project/pallas_call | solution.py:444
  34.5 0.5 collective-permute-start.17
  35.0 1.6 %collective-permute-start.16 = (bf16[64,2048]{1,0:T(8,128)(2,1)S(1)}, bf16[64,2048]{1,0:T(8,128)(2,1)S(1)}, u32[]{:S(2)}, u32[]{:S(2)}) collective-permute-start(bf16[64,2048]{1,0:T(8,128)(2,1)S(1)} %get-tuple-element.72), channel_id=1, source_target_pairs={{0,1},{1,0},{2,3},{3,2},{4,5},{5,4},{6,7},{7,6},{8,9},{9,8},{10,11... | collective-permute-start | bytes 786440 | tf_op jit(solution)/shard_map/ppermute | solution.py:571
  36.8 2.7 %collective-permute-start.18 = (bf16[64,1024]{1,0:T(8,128)(2,1)S(1)}, bf16[64,1024]{1,0:T(8,128)(2,1)S(1)}, u32[]{:S(2)}, u32[]{:S(2)}) collective-permute-start(bf16[64,1024]{1,0:T(8,128)(2,1)S(1)} %add_convert_fusion.2), channel_id=1, source_target_pairs={{0,2},{1,3},{2,0},{3,1},{4,6},{5,7},{6,4},{7,5},{8,10},{9,11},{10,... | collective-permute-start | bytes 393224 | tf_op jit(solution)/shard_map/ppermute | solution.py:574
  39.5 5.7 %collective-permute-done.17 = bf16[64,1024]{1,0:T(8,128)(2,1)S(1)} collective-permute-done((bf16[64,1024]{1,0:T(8,128)(2,1)S(1)}, bf16[64,1024]{1,0:T(8,128)(2,1)S(1)}, u32[]{:S(2)}, u32[]{:S(2)}) %collective-permute-start.17) | collective-permute-done | bytes 131104 | tf_op jit(solution)/shard_map/ppermute | solution.py:571
  45.3 1.6 %attention.3.att_ref = bf16[128,1024]{1,0:T(8,128)(2,1)S(1)} custom-call(s32[4]{0:T(128)} %refs_0_.5, s32[32]{0:T(128)} %refs_1_.7, bf16[256,1024]{1,0:T(8,128)(2,1)S(1)} %get-tuple-element.48.refs_2_, bf16[2,2048,256]{2,1,0:T(8,128)(2,1)S(1)} %get-tuple-element.69.refs_3_), custom_call_target="tpu_custom_call" | custom-call | tf_op jit(solution)/shard_map/attention/pallas_call | solution.py:52
  46.9 2.3 %project.5 = (bf16[64,4096]{1,0:T(8,128)(2,1)S(1)}, f32[64,4096]{1,0:T(8,128)S(1)}) custom-call(bf16[128,1024]{1,0:T(8,128)(2,1)S(1)} %attention.3.att_ref, bf16[256,1024]{1,0:T(8,128)(2,1)S(1)} %finish.1.mix_ref, bf16[1024,4096]{1,0:T(8,128)(2,1)S(1)} %get-tuple-element.61.wa_ref, bf16[1024,4096]{1,0:T(8,128)(2,1)S(1)} %get-tuple-element.62.wm_ref), custom_call_target="tpu_custom_call" | custom-call | tf_op jit(solution)/shard_map/project/pallas_call | solution.py:444
  49.3 0.7 %collective-permute-start.15 = (bf16[64,4096]{1,0:T(8,128)(2,1)S(1)}, bf16[64,4096]{1,0:T(8,128)(2,1)S(1)}, u32[]{:S(2)}, u32[]{:S(2)}) collective-permute-start(bf16[64,4096]{1,0:T(8,128)(2,1)S(1)} %get-tuple-element.71), channel_id=1, source_target_pairs={{0,1},{1,0},{2,3},{3,2},{4,5},{5,4},{6,7},{7,6},{8,9},{9,8},{10,11... | collective-permute-start | bytes 1572872 | tf_op jit(solution)/shard_map/ppermute | solution.py:571
  50.0 0.9 %collective-permute-done.16 = bf16[64,2048]{1,0:T(8,128)(2,1)S(1)} collective-permute-done((bf16[64,2048]{1,0:T(8,128)(2,1)S(1)}, bf16[64,2048]{1,0:T(8,128)(2,1)S(1)}, u32[]{:S(2)}, u32[]{:S(2)}) %collective-permute-start.16) | collective-permute-done | bytes 262176 | tf_op jit(solution)/shard_map/ppermute | solution.py:571
  50.9 4.4 %collective-permute-done.19.refs_1_ = bf16[64,1024]{1,0:T(8,128)(2,1)S(1)} collective-permute-done((bf16[64,1024]{1,0:T(8,128)(2,1)S(1)}, bf16[64,1024]{1,0:T(8,128)(2,1)S(1)}, u32[]{:S(2)}, u32[]{:S(2)}) %collective-permute-start.19) | collective-permute-done | bytes 131104 | tf_op jit(solution)/shard_map/ppermute | solution.py:574
  55.4 11.4 %collective-permute-done.20.refs_2_ = bf16[64,2048]{1,0:T(8,128)(2,1)S(1)} collective-permute-done((bf16[64,2048]{1,0:T(8,128)(2,1)S(1)}, bf16[64,2048]{1,0:T(8,128)(2,1)S(1)}, u32[]{:S(2)}, u32[]{:S(2)}) %collective-permute-start.20) | collective-permute-done | bytes 262176 | tf_op jit(solution)/shard_map/ppermute | solution.py:574
  66.8 1.2 %collective-permute-done.15.near_ref = bf16[64,4096]{1,0:T(8,128)(2,1)S(1)} collective-permute-done((bf16[64,4096]{1,0:T(8,128)(2,1)S(1)}, bf16[64,4096]{1,0:T(8,128)(2,1)S(1)}, u32[]{:S(2)}, u32[]{:S(2)}) %collective-permute-start.15) | collective-permute-done | bytes 524320 | tf_op jit(solution)/shard_map/ppermute | solution.py:571
  68.0 0.9 %assemble.1 = bf16[64,4096]{1,0:T(8,128)(2,1)} custom-call(f32[64,4096]{1,0:T(8,128)S(1)} %get-tuple-element.70.keep_ref, bf16[64,4096]{1,0:T(8,128)(2,1)S(1)} %collective-permute-done.15.near_ref, bf16[64,1024]{1,0:T(8,128)(2,1)S(1)} %collective-permute-done.18.refs_0_, bf16[64,1024]{1,0:T(8,128)(2,1)S(1)} %collective-permute-done.19.refs_1_, ...), custom_call_target="tpu_custom_call" | custom-call | tf_op jit(solution)/shard_map/assemble/pallas_call | solution.py:500
  (24 shorter events, 1.1 us)
Async XLA Ops:
  1.0 13.9 %collective-permute-start = (bf16[2,256,256]{2,1,0:T(8,128)(2,1)S(1)}, bf16[2,256,256]{2,1,0:T(8,128)(2,1)S(1)}, u32[]{:S(2)}, u32[]{:S(2)}) collective-permute-start(bf16[2,256,256]{2,1,0:T(8,128)(2,1)S(1)} %pack.1.refs_3_), channel_id=1, source_target_pairs={{0,8},{4,12},{8,0},{12,4},{16,24},{20,28},{24,16},{28,20},{1,9},{5... | collective-permute-start | bytes 786440 | tf_op jit(solution)/shard_map/ppermute | solution.py:533
  4.0 13.4 %collective-permute-start.1 = (bf16[2,256,256]{2,1,0:T(8,128)(2,1)S(1)}, bf16[2,256,256]{2,1,0:T(8,128)(2,1)S(1)}, u32[]{:S(2)}, u32[]{:S(2)}) collective-permute-start(bf16[2,256,256]{2,1,0:T(8,128)(2,1)S(1)} %pack.1.refs_3_), channel_id=1, source_target_pairs={{0,16},{4,20},{8,24},{12,28},{16,0},{20,4},{24,8},{28,12},{1,17},{... | collective-permute-start | bytes 786440 | tf_op jit(solution)/shard_map/ppermute | solution.py:533
  5.5 11.9 %collective-permute-start.2 = (bf16[2,256,256]{2,1,0:T(8,128)(2,1)S(1)}, bf16[2,256,256]{2,1,0:T(8,128)(2,1)S(1)}, u32[]{:S(2)}, u32[]{:S(2)}) collective-permute-start(bf16[2,256,256]{2,1,0:T(8,128)(2,1)S(1)} %pack.1.refs_3_), channel_id=1, source_target_pairs={{0,24},{4,28},{8,16},{12,20},{16,8},{20,12},{24,0},{28,4},{1,25},{... | collective-permute-start | bytes 786440 | tf_op jit(solution)/shard_map/ppermute | solution.py:533
  8.3 9.6 %collective-permute-start.7 = (bf16[2,528,128]{2,1,0:T(8,128)(2,1)S(1)}, bf16[2,528,128]{2,1,0:T(8,128)(2,1)S(1)}, u32[]{:S(2)}, u32[]{:S(2)}) collective-permute-start(bf16[2,528,128]{2,1,0:T(8,128)(2,1)S(1)} %get-tuple-element.46.refs_0_.mine_ref), channel_id=1, source_target_pairs={{0,4},{4,0},{8,12},{12,8},{16,20},{20,16},{24,28},{28,24},{1,5},{5... | collective-permute-start | bytes 811016 | tf_op jit(solution)/shard_map/ppermute | solution.py:536
  8.4 11.2 %collective-permute-start.3 = (bf16[2,256,256]{2,1,0:T(8,128)(2,1)S(1)}, bf16[2,256,256]{2,1,0:T(8,128)(2,1)S(1)}, u32[]{:S(2)}, u32[]{:S(2)}) collective-permute-start(bf16[2,256,256]{2,1,0:T(8,128)(2,1)S(1)} %pack.1.refs_3_), channel_id=1, source_target_pairs={{0,4},{4,0},{8,12},{12,8},{16,20},{20,16},{24,28},{28,24},{1,5},{5... | collective-permute-start | bytes 786440 | tf_op jit(solution)/shard_map/ppermute | solution.py:536
  17.4 3.6 %collective-permute-start.4 = (bf16[2,256,256]{2,1,0:T(8,128)(2,1)S(1)}, bf16[2,256,256]{2,1,0:T(8,128)(2,1)S(1)}, u32[]{:S(2)}, u32[]{:S(2)}) collective-permute-start(bf16[2,256,256]{2,1,0:T(8,128)(2,1)S(1)} %collective-permute-done.refs_5_), channel_id=1, source_target_pairs={{0,4},{4,0},{8,12},{12,8},{16,20},{20,16},{24,28},{28,24},{1,5},{5... | collective-permute-start | bytes 786440 | tf_op jit(solution)/shard_map/ppermute | solution.py:536
  17.4 4.1 %collective-permute-start.5 = (bf16[2,256,256]{2,1,0:T(8,128)(2,1)S(1)}, bf16[2,256,256]{2,1,0:T(8,128)(2,1)S(1)}, u32[]{:S(2)}, u32[]{:S(2)}) collective-permute-start(bf16[2,256,256]{2,1,0:T(8,128)(2,1)S(1)} %collective-permute-done.1.refs_7_), channel_id=1, source_target_pairs={{0,4},{4,0},{8,12},{12,8},{16,20},{20,16},{24,28},{28,24},{1,5},{5... | collective-permute-start | bytes 786440 | tf_op jit(solution)/shard_map/ppermute | solution.py:536
  17.9 3.6 %collective-permute-start.6 = (bf16[2,256,256]{2,1,0:T(8,128)(2,1)S(1)}, bf16[2,256,256]{2,1,0:T(8,128)(2,1)S(1)}, u32[]{:S(2)}, u32[]{:S(2)}) collective-permute-start(bf16[2,256,256]{2,1,0:T(8,128)(2,1)S(1)} %collective-permute-done.2.refs_9_), channel_id=1, source_target_pairs={{0,4},{4,0},{8,12},{12,8},{16,20},{20,16},{24,28},{28,24},{1,5},{5... | collective-permute-start | bytes 786440 | tf_op jit(solution)/shard_map/ppermute | solution.py:536
  18.0 7.3 %collective-permute-start.10 = (bf16[528,128]{1,0:T(8,128)(2,1)S(1)}, bf16[528,128]{1,0:T(8,128)(2,1)S(1)}, u32[]{:S(2)}, u32[]{:S(2)}) collective-permute-start(bf16[528,128]{1,0:T(8,128)(2,1)S(1)} %compose.1), channel_id=1, source_target_pairs={{0,24},{4,28},{8,16},{12,20},{16,8},{20,12},{24,0},{28,4},{1,25},{... | collective-permute-start | bytes 405512 | tf_op jit(solution)/shard_map/ppermute | solution.py:533
  19.5 8.4 %collective-permute-start.8 = (bf16[528,128]{1,0:T(8,128)(2,1)S(1)}, bf16[528,128]{1,0:T(8,128)(2,1)S(1)}, u32[]{:S(2)}, u32[]{:S(2)}) collective-permute-start(bf16[528,128]{1,0:T(8,128)(2,1)S(1)} %compose.1), channel_id=1, source_target_pairs={{0,8},{4,12},{8,0},{12,4},{16,24},{20,28},{24,16},{28,20},{1,9},{5... | collective-permute-start | bytes 405512 | tf_op jit(solution)/shard_map/ppermute | solution.py:533
  21.0 6.9 %collective-permute-start.9 = (bf16[528,128]{1,0:T(8,128)(2,1)S(1)}, bf16[528,128]{1,0:T(8,128)(2,1)S(1)}, u32[]{:S(2)}, u32[]{:S(2)}) collective-permute-start(bf16[528,128]{1,0:T(8,128)(2,1)S(1)} %compose.1), channel_id=1, source_target_pairs={{0,16},{4,20},{8,24},{12,28},{16,0},{20,4},{24,8},{28,12},{1,17},{... | collective-permute-start | bytes 405512 | tf_op jit(solution)/shard_map/ppermute | solution.py:533
  27.9 1.4 %collective-permute-start.11 = (bf16[528,128]{1,0:T(8,128)(2,1)S(1)}, bf16[528,128]{1,0:T(8,128)(2,1)S(1)}, u32[]{:S(2)}, u32[]{:S(2)}) collective-permute-start(bf16[528,128]{1,0:T(8,128)(2,1)S(1)} %collective-permute-done.8.refs_4_), channel_id=1, source_target_pairs={{0,4},{4,0},{8,12},{12,8},{16,20},{20,16},{24,28},{28,24},{1,5},{5... | collective-permute-start | bytes 405512 | tf_op jit(solution)/shard_map/ppermute | solution.py:536
  27.9 1.5 %collective-permute-start.12 = (bf16[528,128]{1,0:T(8,128)(2,1)S(1)}, bf16[528,128]{1,0:T(8,128)(2,1)S(1)}, u32[]{:S(2)}, u32[]{:S(2)}) collective-permute-start(bf16[528,128]{1,0:T(8,128)(2,1)S(1)} %collective-permute-done.9.refs_6_), channel_id=1, source_target_pairs={{0,4},{4,0},{8,12},{12,8},{16,20},{20,16},{24,28},{28,24},{1,5},{5... | collective-permute-start | bytes 405512 | tf_op jit(solution)/shard_map/ppermute | solution.py:536
  28.4 1.4 %collective-permute-start.13 = (bf16[528,128]{1,0:T(8,128)(2,1)S(1)}, bf16[528,128]{1,0:T(8,128)(2,1)S(1)}, u32[]{:S(2)}, u32[]{:S(2)}) collective-permute-start(bf16[528,128]{1,0:T(8,128)(2,1)S(1)} %collective-permute-done.10.refs_8_), channel_id=1, source_target_pairs={{0,4},{4,0},{8,12},{12,8},{16,20},{20,16},{24,28},{28,24},{1,5},{5... | collective-permute-start | bytes 405512 | tf_op jit(solution)/shard_map/ppermute | solution.py:536
  31.1 5.7 %collective-permute-start.14 = (bf16[64,1024]{1,0:T(8,128)(2,1)S(1)}, bf16[64,1024]{1,0:T(8,128)(2,1)S(1)}, u32[]{:S(2)}, u32[]{:S(2)}) collective-permute-start(bf16[64,1024]{1,0:T(8,128)(2,1)S(1)} %get-tuple-element.68), channel_id=1, source_target_pairs={{0,1},{1,0},{2,3},{3,2},{4,5},{5,4},{6,7},{7,6},{8,9},{9,8},{10,11... | collective-permute-start | bytes 393224 | tf_op jit(solution)/shard_map/ppermute | solution.py:571
  34.5 10.6 %collective-permute-start.17 = (bf16[64,1024]{1,0:T(8,128)(2,1)S(1)}, bf16[64,1024]{1,0:T(8,128)(2,1)S(1)}, u32[]{:S(2)}, u32[]{:S(2)}) collective-permute-start(bf16[64,1024]{1,0:T(8,128)(2,1)S(1)} %get-tuple-element.74), channel_id=1, source_target_pairs={{0,1},{1,0},{2,3},{3,2},{4,5},{5,4},{6,7},{7,6},{8,9},{9,8},{10,11... | collective-permute-start | bytes 393224 | tf_op jit(solution)/shard_map/ppermute | solution.py:571
  35.0 15.8 %collective-permute-start.16 = (bf16[64,2048]{1,0:T(8,128)(2,1)S(1)}, bf16[64,2048]{1,0:T(8,128)(2,1)S(1)}, u32[]{:S(2)}, u32[]{:S(2)}) collective-permute-start(bf16[64,2048]{1,0:T(8,128)(2,1)S(1)} %get-tuple-element.72), channel_id=1, source_target_pairs={{0,1},{1,0},{2,3},{3,2},{4,5},{5,4},{6,7},{7,6},{8,9},{9,8},{10,11... | collective-permute-start | bytes 786440 | tf_op jit(solution)/shard_map/ppermute | solution.py:571
  36.8 14.1 %collective-permute-start.18 = (bf16[64,1024]{1,0:T(8,128)(2,1)S(1)}, bf16[64,1024]{1,0:T(8,128)(2,1)S(1)}, u32[]{:S(2)}, u32[]{:S(2)}) collective-permute-start(bf16[64,1024]{1,0:T(8,128)(2,1)S(1)} %add_convert_fusion.2), channel_id=1, source_target_pairs={{0,2},{1,3},{2,0},{3,1},{4,6},{5,7},{6,4},{7,5},{8,10},{9,11},{10,... | collective-permute-start | bytes 393224 | tf_op jit(solution)/shard_map/ppermute | solution.py:574
  45.2 10.1 %collective-permute-start.19 = (bf16[64,1024]{1,0:T(8,128)(2,1)S(1)}, bf16[64,1024]{1,0:T(8,128)(2,1)S(1)}, u32[]{:S(2)}, u32[]{:S(2)}) collective-permute-start(bf16[64,1024]{1,0:T(8,128)(2,1)S(1)} %add_convert_fusion.1), channel_id=1, source_target_pairs={{0,2},{1,3},{2,0},{3,1},{4,6},{5,7},{6,4},{7,5},{8,10},{9,11},{10,... | collective-permute-start | bytes 393224 | tf_op jit(solution)/shard_map/ppermute | solution.py:574
  49.3 18.8 %collective-permute-start.15 = (bf16[64,4096]{1,0:T(8,128)(2,1)S(1)}, bf16[64,4096]{1,0:T(8,128)(2,1)S(1)}, u32[]{:S(2)}, u32[]{:S(2)}) collective-permute-start(bf16[64,4096]{1,0:T(8,128)(2,1)S(1)} %get-tuple-element.71), channel_id=1, source_target_pairs={{0,1},{1,0},{2,3},{3,2},{4,5},{5,4},{6,7},{7,6},{8,9},{9,8},{10,11... | collective-permute-start | bytes 1572872 | tf_op jit(solution)/shard_map/ppermute | solution.py:571
  55.3 11.5 %collective-permute-start.20 = (bf16[64,2048]{1,0:T(8,128)(2,1)S(1)}, bf16[64,2048]{1,0:T(8,128)(2,1)S(1)}, u32[]{:S(2)}, u32[]{:S(2)}) collective-permute-start(bf16[64,2048]{1,0:T(8,128)(2,1)S(1)} %add_convert_fusion), channel_id=1, source_target_pairs={{0,2},{1,3},{2,0},{3,1},{4,6},{5,7},{6,4},{7,5},{8,10},{9,11},{10,... | collective-permute-start | bytes 786440 | tf_op jit(solution)/shard_map/ppermute | solution.py:574

commit v6 on v5

--- a/solution.py
+++ b/solution.py
@@ -156,11 +156,12 @@
     )
 
 
-def compose_kernel(mine_ref, other_ref, out_ref):
+def compose_kernel(mine_ref, low_ref, high_ref, out_ref):
     core = lax.axis_index("ctx") & 1
     state_rows = out_ref.shape[0] - 16
     half = state_rows // STATE
-    a, b = mine_ref[core].astype(F32), other_ref[core].astype(F32)
+    a = mine_ref[core].astype(F32)
+    b = jnp.where(core == 0, low_ref[...].astype(F32), high_ref[...].astype(F32))
     first = jnp.where(core == 0, a, b)
     second = jnp.where(core == 0, b, a)
     for i in range(half):
@@ -170,26 +171,26 @@
     out_ref[state_rows:, :] = (first[state_rows:] * second[state_rows:]).astype(BF16)
 
 
-def compose(mine, other):
+def compose(mine, low, high):
     return pl.pallas_call(
         compose_kernel,
         out_shape=jax.ShapeDtypeStruct(mine.shape[1:], BF16),
-        in_specs=[VMEM_SPEC] * 2,
+        in_specs=[VMEM_SPEC] * 3,
         out_specs=VMEM_SPEC,
         compiler_params=pltpu.CompilerParams(vmem_limit_bytes=4 * MIB),
         cost_estimate=pl.CostEstimate(flops=0, bytes_accessed=0, transcendentals=0),
         name="compose",
-    )(mine, other)
-
-
-def finish_kernel(r_ref, base_ref, eg_ref, st_ref, *refs):
+    )(mine, low, high)
+
+
+def finish_kernel(r_ref, base_ref, eg_ref, low_ref, high_ref, *refs):
     *got, out_ref, held, carry = refs
     me = lax.axis_index("ctx")
     core, chip = me & 1, me // 2
     z = lax.axis_index("tp")
     rows = base_ref.shape[0]
     part = rows // 4
-    state_rows = st_ref.shape[1] - 16
+    state_rows = low_ref.shape[0] - 16
     half = state_rows // STATE
     groups = r_ref.shape[1] // STATE
     heads = 2 * half
@@ -215,7 +216,8 @@
     def _():
         for h in range(heads):
             c, hs, gs = where(h)
-            carry[h] = st_ref[c, gs, :].astype(F32) * carry[h] + st_ref[c, hs, :].astype(F32)
+            ref = high_ref if c else low_ref
+            carry[h] = ref[gs, :].astype(F32) * carry[h] + ref[hs, :].astype(F32)
 
     for h in range(heads):
         hc = slice(h * SSM_HEAD_DIM, (h + 1) * SSM_HEAD_DIM)
@@ -227,7 +229,7 @@
             out_ref[pl.ds(at, part), hc] = res[q * part : (q + 1) * part]
 
 
-def finish(base, r, eg, st_other, got):
+def finish(base, r, eg, low, high, got):
     chips = len(got) // 2 + 1
     heads = base.shape[1] // SSM_HEAD_DIM
     return one_step(
@@ -235,7 +237,7 @@
         "finish",
         (jax.ShapeDtypeStruct(base.shape, BF16),),
         (),
-        (r, base, eg, st_other, *got),
+        (r, base, eg, low, high, *got),
         scratch=[
             pltpu.VMEM((chips, 2) + got[0].shape, BF16),
             pltpu.VMEM((heads, STATE, SSM_HEAD_DIM), F32),
@@ -543,24 +545,24 @@
     base, st, eg = mixer_local(
         doc_lengths, skip_gain, mixer_input, state_write, state_read, log_decay
     )
-    st_other = other_core(st)
-    chip_state = compose(st, st_other)
+    low, high = other_core(st[0]), other_core(st[1])
+    chip_state = compose(st, low, high)
     near_weight, far_weight, near_queries, near_read = fetch(
         st, attention_weight, mixer_weight, queries, state_read
     )
     far_states = [between_chips(chip_state, j) for j in range(1, chips)]
 
-    far[1:], near_queries = lax.optimization_barrier((far[1:], near_queries))
+    far[1:], near_queries, _ = lax.optimization_barrier((far[1:], near_queries, chip_state))
+    far[-1], *far_states = lax.optimization_barrier((far[-1], *far_states))
     got = []
     for a in far:
         got += [a, other_core(a)]
     place = (page_len, doc_lengths, page_table, near_queries, width // HEAD_DIM)
     att, kv = attention(*place, got)
-    *far_states, att = lax.optimization_barrier((*far_states, att))
     got_states = []
     for a in far_states:
         got_states += [a, other_core(a)]
-    mix = finish(base, near_read, eg, st_other, got_states)
+    mix = finish(base, near_read, eg, low, high, got_states)
 
     part = tok_rows // n_tp
     columns = attention_weight.shape[1]

time: 69.1 us -> 69 us (level); the launches traced: 68.9 us -> 68 us
  waiting for transfers between devices: 32.2 us -> 25.6 us
  starting transfers between devices: 17 us -> 22.5 us
    ppermute x3, starting transfers between devices: 2.79 us -> 7.34 us  [across(): return lax.ppermute(a, 'tp', [(i, i ^ 2) for i in range(n_tp)])]
    ppermute x6, waiting for transfers between devices: 7.04 us -> 3.82 us  [between_chips(): return lax.ppermute(a, 'ctx', [(i, i ^ 2 * j) for i in range(n_ctx)])]
    ppermute x3, waiting for transfers between devices: 15.8 us -> 13.3 us  [across(): return lax.ppermute(a, 'tp', [(i, i ^ 2) for i in range(n_tp)])]
    ppermute x4, waiting for transfers between devices: 7.98 us -> 6.26 us  [neighbour(): return lax.ppermute(a, 'tp', [(i, i ^ 1) for i in range(n_tp)])]
    ppermute x8 -> x9, waiting for transfers between devices: 1.36 us -> 2.3 us  [other_core(): return lax.ppermute(a, 'ctx', [(i, i ^ 1) for i in range(n_ctx)])]
    ppermute x8 -> x9, starting transfers between devices: 1.6 us -> 2.09 us  [other_core(): return lax.ppermute(a, 'ctx', [(i, i ^ 1) for i in range(n_ctx)])]
  transfers between devices with their start and end apart: 21 -> 22, of which waited for: 12 -> 12; matrix products, arithmetic and copies ran while one was open for 0% -> 0% of each run, Pallas kernels for 24% -> 22%
where the time goes in v6:
time: 69 us; the launch traced here: 68 us
  waiting for transfers between devices  25.6 us (37%)
  starting transfers between devices  22.5 us (33%)
  Pallas kernels  19.6 us (28%)
    ppermute x3, waiting for transfers between devices, across(): return lax.ppermute(a, 'tp', [(i, i ^ 2) for i in range(n_tp)])  13.3 us
    ppermute x6, starting transfers between devices, between_chips(): return lax.ppermute(a, 'ctx', [(i, i ^ 2 * j) for i in range(n_ctx)])  8.2 us
    ppermute x3, starting transfers between devices, across(): return lax.ppermute(a, 'tp', [(i, i ^ 2) for i in range(n_tp)])  7.34 us
    pallas_call x4, Pallas kernels, one_step(): pl.pallas_call(body, out_shape=tuple(out_shape), in_specs=[HBM_SPEC] * le...  6.73 us
    ppermute x4, waiting for transfers between devices, neighbour(): return lax.ppermute(a, 'tp', [(i, i ^ 1) for i in range(n_tp)])  6.26 us
    pallas_call x1, Pallas kernels, fetch(): pl.pallas_call(functools.partial(fetch_kernel, 4), out_shape=tuple((jax.S...  6.01 us
    pallas_call x3, Pallas kernels, project(): pl.pallas_call(functools.partial(project_kernel, start, tile, side), out_...  4.87 us
    ppermute x4, starting transfers between devices, neighbour(): return lax.ppermute(a, 'tp', [(i, i ^ 1) for i in range(n_tp)])  4.83 us
  transfers between devices with their start and end apart: 22, of which 12 were waited for; matrix products, arithmetic and copies ran while one was open for 0% of the time, Pallas kernels for 22%

profile of v6, /device:TPU:0, one launch (start us, length us, event | category | flops | bytes accessed | tf_op | source)
XLA Modules:
  0.0 68.0 jit_solution(442065171558655417)
XLA Ops:
  0.0 1.0 %pack.1.refs_3_ = bf16[2,256,256]{2,1,0:T(8,128)(2,1)S(1)} custom-call(bf16[256,256]{1,0:T(8,128)(2,1)} %bitcast.6, bf16[256,256]{1,0:T(8,128)(2,1)} %bitcast.7), custom_call_target="tpu_custom_call" | custom-call | tf_op jit(solution)/shard_map/pack/pallas_call | solution.py:473
  1.0 4.0 %collective-permute-start.2 = (bf16[2,256,256]{2,1,0:T(8,128)(2,1)S(1)}, bf16[2,256,256]{2,1,0:T(8,128)(2,1)S(1)}, u32[]{:S(2)}, u32[]{:S(2)}) collective-permute-start(bf16[2,256,256]{2,1,0:T(8,128)(2,1)S(1)} %pack.1.refs_3_), channel_id=1, source_target_pairs={{0,24},{4,28},{8,16},{12,20},{16,8},{20,12},{24,0},{28,4},{1,25},{... | collective-permute-start | bytes 786440 | tf_op jit(solution)/shard_map/ppermute | solution.py:535
  5.0 2.8 %mixer_local.1 = (f32[256,1024]{1,0:T(8,128)S(1)}, bf16[2,528,128]{2,1,0:T(8,128)(2,1)S(1)}, f32[256,8]{1,0:T(8,128)S(1)}) custom-call(s32[4]{0:T(128)} %refs_0_.5, f32[8]{0:T(128)} %refs_1_.4, bf16[256,1024]{1,0:T(8,128)(2,1)} %refs_2_.1, bf16[256,256]{1,0:T(8,128)(2,1)} %refs_3_.2, bf16[256,256]{1,0:T(8,128)(2,1)} %refs_4_.3, f32[8,256]{1,0:T(8,128)} %refs_5_.1), custom_call_target="tpu_custom_call" | custom-call | tf_op jit(solution)/shard_map/mixer_local/pallas_call | solution.py:52
  8.3 0.5 collective-permute-start.1
  9.4 2.5 %collective-permute-start.10 = (bf16[528,128]{1,0:T(8,128)(2,1)S(1)}, bf16[528,128]{1,0:T(8,128)(2,1)S(1)}, u32[]{:S(2)}, u32[]{:S(2)}) collective-permute-start(bf16[528,128]{1,0:T(8,128)(2,1)S(1)} %compose.1), channel_id=1, source_target_pairs={{0,24},{4,28},{8,16},{12,20},{16,8},{20,12},{24,0},{28,4},{1,25},{... | collective-permute-start | bytes 405512 | tf_op jit(solution)/shard_map/ppermute | solution.py:535
  12.0 0.5 collective-permute-start.9
  12.5 0.6 collective-permute-start.8
  13.1 6.0 %fetch.1 = (bf16[1024,4096]{1,0:T(8,128)(2,1)S(1)}, bf16[1024,4096]{1,0:T(8,128)(2,1)S(1)}, bf16[256,1024]{1,0:T(8,128)(2,1)S(1)}, bf16[256,256]{1,0:T(8,128)(2,1)S(1)}) custom-call(bf16[2,528,128]{2,1,0:T(8,128)(2,1)S(1)} %get-tuple-element.46.refs_0_.mine_ref, bf16[1024,4096]{1,0:T(8,128)(2,1)} %refs_1_.5, bf16[1024,4096]{1,0:T(8,128)(2,1)} %refs_2_.2, ...), custom_call_target="tpu_custom_call" | custom-call | bytes 17432576 | tf_op jit(solution)/shard_map/fetch/pallas_call | solution.py:412
  19.1 2.7 %collective-permute-done.10.refs_9_ = bf16[528,128]{1,0:T(8,128)(2,1)S(1)} collective-permute-done((bf16[528,128]{1,0:T(8,128)(2,1)S(1)}, bf16[528,128]{1,0:T(8,128)(2,1)S(1)}, u32[]{:S(2)}, u32[]{:S(2)}) %collective-permute-start.10) | collective-permute-done | bytes 135200 | tf_op jit(solution)/shard_map/ppermute | solution.py:535
  21.9 0.8 %collective-permute-done.9.refs_7_ = bf16[528,128]{1,0:T(8,128)(2,1)S(1)} collective-permute-done((bf16[528,128]{1,0:T(8,128)(2,1)S(1)}, bf16[528,128]{1,0:T(8,128)(2,1)S(1)}, u32[]{:S(2)}, u32[]{:S(2)}) %collective-permute-start.9) | collective-permute-done | bytes 135200 | tf_op jit(solution)/shard_map/ppermute | solution.py:535
  23.0 0.5 collective-permute-start.13
  23.5 0.5 collective-permute-start.6
  24.8 1.5 %collective-permute-done.14.refs_10_ = bf16[528,128]{1,0:T(8,128)(2,1)S(1)} collective-permute-done((bf16[528,128]{1,0:T(8,128)(2,1)S(1)}, bf16[528,128]{1,0:T(8,128)(2,1)S(1)}, u32[]{:S(2)}, u32[]{:S(2)}) %collective-permute-start.14) | collective-permute-done | bytes 135200 | tf_op jit(solution)/shard_map/ppermute | solution.py:538
  26.3 0.5 finish.1.mix_ref
  26.9 1.8 %attention.2 = (bf16[128,1024]{1,0:T(8,128)(2,1)S(1)}, bf16[2,2048,256]{2,1,0:T(8,128)(2,1)S(1)}) custom-call(s32[4]{0:T(128)} %refs_0_.5, s32[32]{0:T(128)} %refs_1_.7, bf16[256,1024]{1,0:T(8,128)(2,1)S(1)} %get-tuple-element.48.refs_2_, bf16[2,256,256]{2,1,0:T(8,128)(2,1)S(1)} %pack.1.refs_3_, bf16[2,256,256]{2,1,0:T(8,128)(2,1)S(1)} %collective-permute-done.5.refs_4_, ...), custom_call_target="tpu_custom_call" | custom-call | flops 107374182400 | bytes 4194304 | tf_op jit(solution)/shard_map/attention/pallas_call | solution.py:52
  28.7 0.7 %project.3 = (bf16[64,1024]{1,0:T(8,128)(2,1)S(1)}, f32[64,1024]{1,0:T(8,128)S(1)}) custom-call(bf16[128,1024]{1,0:T(8,128)(2,1)S(1)} %get-tuple-element.64.att_ref, bf16[256,1024]{1,0:T(8,128)(2,1)S(1)} %finish.1.mix_ref, bf16[1024,4096]{1,0:T(8,128)(2,1)S(1)} %get-tuple-element.61.wa_ref, bf16[1024,4096]{1,0:T(8,128)(2,1)S(1)} %get-tuple-element.62.wm_ref), custom_call_target="tpu_custom_call" | custom-call | flops 536870912 | bytes 786432 | tf_op jit(solution)/shard_map/project/pallas_call | solution.py:446
  29.5 1.6 %collective-permute-start.15 = (bf16[64,1024]{1,0:T(8,128)(2,1)S(1)}, bf16[64,1024]{1,0:T(8,128)(2,1)S(1)}, u32[]{:S(2)}, u32[]{:S(2)}) collective-permute-start(bf16[64,1024]{1,0:T(8,128)(2,1)S(1)} %get-tuple-element.68), channel_id=1, source_target_pairs={{0,1},{1,0},{2,3},{3,2},{4,5},{5,4},{6,7},{7,6},{8,9},{9,8},{10,11... | collective-permute-start | bytes 393224 | tf_op jit(solution)/shard_map/ppermute | solution.py:573
  31.1 1.8 %project.4 = (bf16[64,1024]{1,0:T(8,128)(2,1)S(1)}, f32[64,1024]{1,0:T(8,128)S(1)}, bf16[64,2048]{1,0:T(8,128)(2,1)S(1)}, f32[64,2048]{1,0:T(8,128)S(1)}) custom-call(bf16[128,1024]{1,0:T(8,128)(2,1)S(1)} %get-tuple-element.64.att_ref, bf16[256,1024]{1,0:T(8,128)(2,1)S(1)} %finish.1.mix_ref, bf16[1024,4096]{1,0:T(8,128)(2,1)S(1)} %get-tuple-element.61.wa_ref, ...), custom_call_target="tpu_custom_call" | custom-call | flops 1610612736 | bytes 2359296 | tf_op jit(solution)/shard_map/project/pallas_call | solution.py:446
  32.9 0.5 collective-permute-start.18
  33.4 1.6 %collective-permute-start.17 = (bf16[64,2048]{1,0:T(8,128)(2,1)S(1)}, bf16[64,2048]{1,0:T(8,128)(2,1)S(1)}, u32[]{:S(2)}, u32[]{:S(2)}) collective-permute-start(bf16[64,2048]{1,0:T(8,128)(2,1)S(1)} %get-tuple-element.72), channel_id=1, source_target_pairs={{0,1},{1,0},{2,3},{3,2},{4,5},{5,4},{6,7},{7,6},{8,9},{9,8},{10,11... | collective-permute-start | bytes 786440 | tf_op jit(solution)/shard_map/ppermute | solution.py:573
  35.0 0.8 %collective-permute-done.15 = bf16[64,1024]{1,0:T(8,128)(2,1)S(1)} collective-permute-done((bf16[64,1024]{1,0:T(8,128)(2,1)S(1)}, bf16[64,1024]{1,0:T(8,128)(2,1)S(1)}, u32[]{:S(2)}, u32[]{:S(2)}) %collective-permute-start.15) | collective-permute-done | bytes 131104 | tf_op jit(solution)/shard_map/ppermute | solution.py:573
  35.8 2.7 %collective-permute-start.19 = (bf16[64,1024]{1,0:T(8,128)(2,1)S(1)}, bf16[64,1024]{1,0:T(8,128)(2,1)S(1)}, u32[]{:S(2)}, u32[]{:S(2)}) collective-permute-start(bf16[64,1024]{1,0:T(8,128)(2,1)S(1)} %add_convert_fusion.2), channel_id=1, source_target_pairs={{0,2},{1,3},{2,0},{3,1},{4,6},{5,7},{6,4},{7,5},{8,10},{9,11},{10,... | collective-permute-start | bytes 393224 | tf_op jit(solution)/shard_map/ppermute | solution.py:576
  38.5 0.8 %collective-permute-done.18 = bf16[64,1024]{1,0:T(8,128)(2,1)S(1)} collective-permute-done((bf16[64,1024]{1,0:T(8,128)(2,1)S(1)}, bf16[64,1024]{1,0:T(8,128)(2,1)S(1)}, u32[]{:S(2)}, u32[]{:S(2)}) %collective-permute-start.18) | collective-permute-done | bytes 131104 | tf_op jit(solution)/shard_map/ppermute | solution.py:573
  39.3 2.6 %collective-permute-start.20 = (bf16[64,1024]{1,0:T(8,128)(2,1)S(1)}, bf16[64,1024]{1,0:T(8,128)(2,1)S(1)}, u32[]{:S(2)}, u32[]{:S(2)}) collective-permute-start(bf16[64,1024]{1,0:T(8,128)(2,1)S(1)} %add_convert_fusion.1), channel_id=1, source_target_pairs={{0,2},{1,3},{2,0},{3,1},{4,6},{5,7},{6,4},{7,5},{8,10},{9,11},{10,... | collective-permute-start | bytes 393224 | tf_op jit(solution)/shard_map/ppermute | solution.py:576
  41.9 1.6 %attention.3.att_ref = bf16[128,1024]{1,0:T(8,128)(2,1)S(1)} custom-call(s32[4]{0:T(128)} %refs_0_.5, s32[32]{0:T(128)} %refs_1_.7, bf16[256,1024]{1,0:T(8,128)(2,1)S(1)} %get-tuple-element.48.refs_2_, bf16[2,2048,256]{2,1,0:T(8,128)(2,1)S(1)} %get-tuple-element.69.refs_3_), custom_call_target="tpu_custom_call" | custom-call | tf_op jit(solution)/shard_map/attention/pallas_call | solution.py:52
  43.6 2.3 %project.5 = (bf16[64,4096]{1,0:T(8,128)(2,1)S(1)}, f32[64,4096]{1,0:T(8,128)S(1)}) custom-call(bf16[128,1024]{1,0:T(8,128)(2,1)S(1)} %attention.3.att_ref, bf16[256,1024]{1,0:T(8,128)(2,1)S(1)} %finish.1.mix_ref, bf16[1024,4096]{1,0:T(8,128)(2,1)S(1)} %get-tuple-element.61.wa_ref, bf16[1024,4096]{1,0:T(8,128)(2,1)S(1)} %get-tuple-element.62.wm_ref), custom_call_target="tpu_custom_call" | custom-call | tf_op jit(solution)/shard_map/project/pallas_call | solution.py:446
  45.9 1.1 %collective-permute-start.16 = (bf16[64,4096]{1,0:T(8,128)(2,1)S(1)}, bf16[64,4096]{1,0:T(8,128)(2,1)S(1)}, u32[]{:S(2)}, u32[]{:S(2)}) collective-permute-start(bf16[64,4096]{1,0:T(8,128)(2,1)S(1)} %get-tuple-element.71), channel_id=1, source_target_pairs={{0,1},{1,0},{2,3},{3,2},{4,5},{5,4},{6,7},{7,6},{8,9},{9,8},{10,11... | collective-permute-start | bytes 1572872 | tf_op jit(solution)/shard_map/ppermute | solution.py:573
  47.0 3.5 %collective-permute-done.17 = bf16[64,2048]{1,0:T(8,128)(2,1)S(1)} collective-permute-done((bf16[64,2048]{1,0:T(8,128)(2,1)S(1)}, bf16[64,2048]{1,0:T(8,128)(2,1)S(1)}, u32[]{:S(2)}, u32[]{:S(2)}) %collective-permute-start.17) | collective-permute-done | bytes 262176 | tf_op jit(solution)/shard_map/ppermute | solution.py:573
  50.6 2.0 %collective-permute-start.21 = (bf16[64,2048]{1,0:T(8,128)(2,1)S(1)}, bf16[64,2048]{1,0:T(8,128)(2,1)S(1)}, u32[]{:S(2)}, u32[]{:S(2)}) collective-permute-start(bf16[64,2048]{1,0:T(8,128)(2,1)S(1)} %add_convert_fusion), channel_id=1, source_target_pairs={{0,2},{1,3},{2,0},{3,1},{4,6},{5,7},{6,4},{7,5},{8,10},{9,11},{10,... | collective-permute-start | bytes 786440 | tf_op jit(solution)/shard_map/ppermute | solution.py:576
  52.6 13.3 %collective-permute-done.21.refs_2_ = bf16[64,2048]{1,0:T(8,128)(2,1)S(1)} collective-permute-done((bf16[64,2048]{1,0:T(8,128)(2,1)S(1)}, bf16[64,2048]{1,0:T(8,128)(2,1)S(1)}, u32[]{:S(2)}, u32[]{:S(2)}) %collective-permute-start.21) | collective-permute-done | bytes 262176 | tf_op jit(solution)/shard_map/ppermute | solution.py:576
  65.9 1.2 %collective-permute-done.16.near_ref = bf16[64,4096]{1,0:T(8,128)(2,1)S(1)} collective-permute-done((bf16[64,4096]{1,0:T(8,128)(2,1)S(1)}, bf16[64,4096]{1,0:T(8,128)(2,1)S(1)}, u32[]{:S(2)}, u32[]{:S(2)}) %collective-permute-start.16) | collective-permute-done | bytes 524320 | tf_op jit(solution)/shard_map/ppermute | solution.py:573
  67.1 0.9 %assemble.1 = bf16[64,4096]{1,0:T(8,128)(2,1)} custom-call(f32[64,4096]{1,0:T(8,128)S(1)} %get-tuple-element.70.keep_ref, bf16[64,4096]{1,0:T(8,128)(2,1)S(1)} %collective-permute-done.16.near_ref, bf16[64,1024]{1,0:T(8,128)(2,1)S(1)} %collective-permute-done.19.refs_0_, bf16[64,1024]{1,0:T(8,128)(2,1)S(1)} %collective-permute-done.20.refs_1_, ...), custom_call_target="tpu_custom_call" | custom-call | tf_op jit(solution)/shard_map/assemble/pallas_call | solution.py:502
  (27 shorter events, 2.5 us)
Async XLA Ops:
  1.0 11.5 %collective-permute-start.2 = (bf16[2,256,256]{2,1,0:T(8,128)(2,1)S(1)}, bf16[2,256,256]{2,1,0:T(8,128)(2,1)S(1)}, u32[]{:S(2)}, u32[]{:S(2)}) collective-permute-start(bf16[2,256,256]{2,1,0:T(8,128)(2,1)S(1)} %pack.1.refs_3_), channel_id=1, source_target_pairs={{0,24},{4,28},{8,16},{12,20},{16,8},{20,12},{24,0},{28,4},{1,25},{... | collective-permute-start | bytes 786440 | tf_op jit(solution)/shard_map/ppermute | solution.py:535
  7.7 1.4 %collective-permute-start.4 = (bf16[528,128]{1,0:T(8,128)(2,1)S(1)}, bf16[528,128]{1,0:T(8,128)(2,1)S(1)}, u32[]{:S(2)}, u32[]{:S(2)}) collective-permute-start(bf16[528,128]{1,0:T(8,128)(2,1)S(1)} %get-tuple-element.83), channel_id=1, source_target_pairs={{0,4},{4,0},{8,12},{12,8},{16,20},{20,16},{24,28},{28,24},{1,5},{5... | collective-permute-start | bytes 405512 | tf_op jit(solution)/shard_map/ppermute | solution.py:538
  7.8 1.5 %collective-permute-start.3 = (bf16[528,128]{1,0:T(8,128)(2,1)S(1)}, bf16[528,128]{1,0:T(8,128)(2,1)S(1)}, u32[]{:S(2)}, u32[]{:S(2)}) collective-permute-start(bf16[528,128]{1,0:T(8,128)(2,1)S(1)} %get-tuple-element.84), channel_id=1, source_target_pairs={{0,4},{4,0},{8,12},{12,8},{16,20},{20,16},{24,28},{28,24},{1,5},{5... | collective-permute-start | bytes 405512 | tf_op jit(solution)/shard_map/ppermute | solution.py:538
  8.3 10.8 %collective-permute-start.1 = (bf16[2,256,256]{2,1,0:T(8,128)(2,1)S(1)}, bf16[2,256,256]{2,1,0:T(8,128)(2,1)S(1)}, u32[]{:S(2)}, u32[]{:S(2)}) collective-permute-start(bf16[2,256,256]{2,1,0:T(8,128)(2,1)S(1)} %pack.1.refs_3_), channel_id=1, source_target_pairs={{0,16},{4,20},{8,24},{12,28},{16,0},{20,4},{24,8},{28,12},{1,17},{... | collective-permute-start | bytes 786440 | tf_op jit(solution)/shard_map/ppermute | solution.py:535
  8.8 10.3 %collective-permute-start = (bf16[2,256,256]{2,1,0:T(8,128)(2,1)S(1)}, bf16[2,256,256]{2,1,0:T(8,128)(2,1)S(1)}, u32[]{:S(2)}, u32[]{:S(2)}) collective-permute-start(bf16[2,256,256]{2,1,0:T(8,128)(2,1)S(1)} %pack.1.refs_3_), channel_id=1, source_target_pairs={{0,8},{4,12},{8,0},{12,4},{16,24},{20,28},{24,16},{28,20},{1,9},{5... | collective-permute-start | bytes 786440 | tf_op jit(solution)/shard_map/ppermute | solution.py:535
  9.4 12.4 %collective-permute-start.10 = (bf16[528,128]{1,0:T(8,128)(2,1)S(1)}, bf16[528,128]{1,0:T(8,128)(2,1)S(1)}, u32[]{:S(2)}, u32[]{:S(2)}) collective-permute-start(bf16[528,128]{1,0:T(8,128)(2,1)S(1)} %compose.1), channel_id=1, source_target_pairs={{0,24},{4,28},{8,16},{12,20},{16,8},{20,12},{24,0},{28,4},{1,25},{... | collective-permute-start | bytes 405512 | tf_op jit(solution)/shard_map/ppermute | solution.py:535
  12.0 10.7 %collective-permute-start.9 = (bf16[528,128]{1,0:T(8,128)(2,1)S(1)}, bf16[528,128]{1,0:T(8,128)(2,1)S(1)}, u32[]{:S(2)}, u32[]{:S(2)}) collective-permute-start(bf16[528,128]{1,0:T(8,128)(2,1)S(1)} %compose.1), channel_id=1, source_target_pairs={{0,16},{4,20},{8,24},{12,28},{16,0},{20,4},{24,8},{28,12},{1,17},{... | collective-permute-start | bytes 405512 | tf_op jit(solution)/shard_map/ppermute | solution.py:535
  12.5 10.5 %collective-permute-start.8 = (bf16[528,128]{1,0:T(8,128)(2,1)S(1)}, bf16[528,128]{1,0:T(8,128)(2,1)S(1)}, u32[]{:S(2)}, u32[]{:S(2)}) collective-permute-start(bf16[528,128]{1,0:T(8,128)(2,1)S(1)} %compose.1), channel_id=1, source_target_pairs={{0,8},{4,12},{8,0},{12,4},{16,24},{20,28},{24,16},{28,20},{1,9},{5... | collective-permute-start | bytes 405512 | tf_op jit(solution)/shard_map/ppermute | solution.py:535
  23.0 1.4 %collective-permute-start.12 = (bf16[528,128]{1,0:T(8,128)(2,1)S(1)}, bf16[528,128]{1,0:T(8,128)(2,1)S(1)}, u32[]{:S(2)}, u32[]{:S(2)}) collective-permute-start(bf16[528,128]{1,0:T(8,128)(2,1)S(1)} %collective-permute-done.8.refs_5_), channel_id=1, source_target_pairs={{0,4},{4,0},{8,12},{12,8},{16,20},{20,16},{24,28},{28,24},{1,5},{5... | collective-permute-start | bytes 405512 | tf_op jit(solution)/shard_map/ppermute | solution.py:538
  23.0 1.5 %collective-permute-start.13 = (bf16[528,128]{1,0:T(8,128)(2,1)S(1)}, bf16[528,128]{1,0:T(8,128)(2,1)S(1)}, u32[]{:S(2)}, u32[]{:S(2)}) collective-permute-start(bf16[528,128]{1,0:T(8,128)(2,1)S(1)} %collective-permute-done.9.refs_7_), channel_id=1, source_target_pairs={{0,4},{4,0},{8,12},{12,8},{16,20},{20,16},{24,28},{28,24},{1,5},{5... | collective-permute-start | bytes 405512 | tf_op jit(solution)/shard_map/ppermute | solution.py:538
  23.5 3.4 %collective-permute-start.5 = (bf16[2,256,256]{2,1,0:T(8,128)(2,1)S(1)}, bf16[2,256,256]{2,1,0:T(8,128)(2,1)S(1)}, u32[]{:S(2)}, u32[]{:S(2)}) collective-permute-start(bf16[2,256,256]{2,1,0:T(8,128)(2,1)S(1)} %pack.1.refs_3_), channel_id=1, source_target_pairs={{0,4},{4,0},{8,12},{12,8},{16,20},{20,16},{24,28},{28,24},{1,5},{5... | collective-permute-start | bytes 786440 | tf_op jit(solution)/shard_map/ppermute | solution.py:538
  23.5 3.4 %collective-permute-start.6 = (bf16[2,256,256]{2,1,0:T(8,128)(2,1)S(1)}, bf16[2,256,256]{2,1,0:T(8,128)(2,1)S(1)}, u32[]{:S(2)}, u32[]{:S(2)}) collective-permute-start(bf16[2,256,256]{2,1,0:T(8,128)(2,1)S(1)} %collective-permute-done.refs_5_), channel_id=1, source_target_pairs={{0,4},{4,0},{8,12},{12,8},{16,20},{20,16},{24,28},{28,24},{1,5},{5... | collective-permute-start | bytes 786440 | tf_op jit(solution)/shard_map/ppermute | solution.py:538
  24.0 2.9 %collective-permute-start.7 = (bf16[2,256,256]{2,1,0:T(8,128)(2,1)S(1)}, bf16[2,256,256]{2,1,0:T(8,128)(2,1)S(1)}, u32[]{:S(2)}, u32[]{:S(2)}) collective-permute-start(bf16[2,256,256]{2,1,0:T(8,128)(2,1)S(1)} %collective-permute-done.1.refs_7_), channel_id=1, source_target_pairs={{0,4},{4,0},{8,12},{12,8},{16,20},{20,16},{24,28},{28,24},{1,5},{5... | collective-permute-start | bytes 786440 | tf_op jit(solution)/shard_map/ppermute | solution.py:538
  24.3 2.6 %collective-permute-start.11 = (bf16[2,256,256]{2,1,0:T(8,128)(2,1)S(1)}, bf16[2,256,256]{2,1,0:T(8,128)(2,1)S(1)}, u32[]{:S(2)}, u32[]{:S(2)}) collective-permute-start(bf16[2,256,256]{2,1,0:T(8,128)(2,1)S(1)} %collective-permute-done.2.refs_9_), channel_id=1, source_target_pairs={{0,4},{4,0},{8,12},{12,8},{16,20},{20,16},{24,28},{28,24},{1,5},{5... | collective-permute-start | bytes 786440 | tf_op jit(solution)/shard_map/ppermute | solution.py:538
  24.5 1.8 %collective-permute-start.14 = (bf16[528,128]{1,0:T(8,128)(2,1)S(1)}, bf16[528,128]{1,0:T(8,128)(2,1)S(1)}, u32[]{:S(2)}, u32[]{:S(2)}) collective-permute-start(bf16[528,128]{1,0:T(8,128)(2,1)S(1)} %collective-permute-done.10.refs_9_), channel_id=1, source_target_pairs={{0,4},{4,0},{8,12},{12,8},{16,20},{20,16},{24,28},{28,24},{1,5},{5... | collective-permute-start | bytes 405512 | tf_op jit(solution)/shard_map/ppermute | solution.py:538
  29.5 6.3 %collective-permute-start.15 = (bf16[64,1024]{1,0:T(8,128)(2,1)S(1)}, bf16[64,1024]{1,0:T(8,128)(2,1)S(1)}, u32[]{:S(2)}, u32[]{:S(2)}) collective-permute-start(bf16[64,1024]{1,0:T(8,128)(2,1)S(1)} %get-tuple-element.68), channel_id=1, source_target_pairs={{0,1},{1,0},{2,3},{3,2},{4,5},{5,4},{6,7},{7,6},{8,9},{9,8},{10,11... | collective-permute-start | bytes 393224 | tf_op jit(solution)/shard_map/ppermute | solution.py:573
  32.9 6.3 %collective-permute-start.18 = (bf16[64,1024]{1,0:T(8,128)(2,1)S(1)}, bf16[64,1024]{1,0:T(8,128)(2,1)S(1)}, u32[]{:S(2)}, u32[]{:S(2)}) collective-permute-start(bf16[64,1024]{1,0:T(8,128)(2,1)S(1)} %get-tuple-element.74), channel_id=1, source_target_pairs={{0,1},{1,0},{2,3},{3,2},{4,5},{5,4},{6,7},{7,6},{8,9},{9,8},{10,11... | collective-permute-start | bytes 393224 | tf_op jit(solution)/shard_map/ppermute | solution.py:573
  33.4 17.1 %collective-permute-start.17 = (bf16[64,2048]{1,0:T(8,128)(2,1)S(1)}, bf16[64,2048]{1,0:T(8,128)(2,1)S(1)}, u32[]{:S(2)}, u32[]{:S(2)}) collective-permute-start(bf16[64,2048]{1,0:T(8,128)(2,1)S(1)} %get-tuple-element.72), channel_id=1, source_target_pairs={{0,1},{1,0},{2,3},{3,2},{4,5},{5,4},{6,7},{7,6},{8,9},{9,8},{10,11... | collective-permute-start | bytes 786440 | tf_op jit(solution)/shard_map/ppermute | solution.py:573
  35.8 14.7 %collective-permute-start.19 = (bf16[64,1024]{1,0:T(8,128)(2,1)S(1)}, bf16[64,1024]{1,0:T(8,128)(2,1)S(1)}, u32[]{:S(2)}, u32[]{:S(2)}) collective-permute-start(bf16[64,1024]{1,0:T(8,128)(2,1)S(1)} %add_convert_fusion.2), channel_id=1, source_target_pairs={{0,2},{1,3},{2,0},{3,1},{4,6},{5,7},{6,4},{7,5},{8,10},{9,11},{10,... | collective-permute-start | bytes 393224 | tf_op jit(solution)/shard_map/ppermute | solution.py:576
  39.3 11.2 %collective-permute-start.20 = (bf16[64,1024]{1,0:T(8,128)(2,1)S(1)}, bf16[64,1024]{1,0:T(8,128)(2,1)S(1)}, u32[]{:S(2)}, u32[]{:S(2)}) collective-permute-start(bf16[64,1024]{1,0:T(8,128)(2,1)S(1)} %add_convert_fusion.1), channel_id=1, source_target_pairs={{0,2},{1,3},{2,0},{3,1},{4,6},{5,7},{6,4},{7,5},{8,10},{9,11},{10,... | collective-permute-start | bytes 393224 | tf_op jit(solution)/shard_map/ppermute | solution.py:576
  45.9 21.2 %collective-permute-start.16 = (bf16[64,4096]{1,0:T(8,128)(2,1)S(1)}, bf16[64,4096]{1,0:T(8,128)(2,1)S(1)}, u32[]{:S(2)}, u32[]{:S(2)}) collective-permute-start(bf16[64,4096]{1,0:T(8,128)(2,1)S(1)} %get-tuple-element.71), channel_id=1, source_target_pairs={{0,1},{1,0},{2,3},{3,2},{4,5},{5,4},{6,7},{7,6},{8,9},{9,8},{10,11... | collective-permute-start | bytes 1572872 | tf_op jit(solution)/shard_map/ppermute | solution.py:573
  50.6 15.3 %collective-permute-start.21 = (bf16[64,2048]{1,0:T(8,128)(2,1)S(1)}, bf16[64,2048]{1,0:T(8,128)(2,1)S(1)}, u32[]{:S(2)}, u32[]{:S(2)}) collective-permute-start(bf16[64,2048]{1,0:T(8,128)(2,1)S(1)} %add_convert_fusion), channel_id=1, source_target_pairs={{0,2},{1,3},{2,0},{3,1},{4,6},{5,7},{6,4},{7,5},{8,10},{9,11},{10,... | collective-permute-start | bytes 786440 | tf_op jit(solution)/shard_map/ppermute | solution.py:576

commit v7 on v5

--- a/solution.py
+++ b/solution.py
@@ -12,7 +12,7 @@
 STATE = 128
 LOG2E = 1.4426950408889634
 LOW = -1e30
-SHARES = (2, 2, 4)
+SHARES = (2, 3, 3)
 F32 = jnp.float32
 BF16 = jnp.bfloat16
 

time: 69.1 us -> 71.6 us (1.036); the launches traced: 68.9 us -> 70.2 us
  waiting for transfers between devices: 32.2 us -> 33 us
  transfers between devices with their start and end apart: 21 -> 21, of which waited for: 12 -> 11; matrix products, arithmetic and copies ran while one was open for 0% -> 0% of each run, Pallas kernels for 24% -> 23%
where the time goes in v7:
time: 71.6 us; the launch traced here: 70.2 us
  waiting for transfers between devices  33 us (46%)
  Pallas kernels  19.5 us (27%)
  starting transfers between devices  17.4 us (24%)
    ppermute x3, waiting for transfers between devices, across(): return lax.ppermute(a, 'tp', [(i, i ^ 2) for i in range(n_tp)])  16.4 us
    ppermute x4, waiting for transfers between devices, neighbour(): return lax.ppermute(a, 'tp', [(i, i ^ 1) for i in range(n_tp)])  8.14 us
    ppermute x6, starting transfers between devices, between_chips(): return lax.ppermute(a, 'ctx', [(i, i ^ 2 * j) for i in range(n_ctx)])  8.1 us
    ppermute x6, waiting for transfers between devices, between_chips(): return lax.ppermute(a, 'ctx', [(i, i ^ 2 * j) for i in range(n_ctx)])  7.03 us
    pallas_call x4, Pallas kernels, one_step(): pl.pallas_call(body, out_shape=tuple(out_shape), in_specs=[HBM_SPEC] * le...  6.75 us
    pallas_call x1, Pallas kernels, fetch(): pl.pallas_call(functools.partial(fetch_kernel, 4), out_shape=tuple((jax.S...  6.01 us
    pallas_call x3, Pallas kernels, project(): pl.pallas_call(functools.partial(project_kernel, start, tile, side), out_...  4.86 us
    ppermute x4, starting transfers between devices, neighbour(): return lax.ppermute(a, 'tp', [(i, i ^ 1) for i in range(n_tp)])  4.69 us
  transfers between devices with their start and end apart: 21, of which 11 were waited for; matrix products, arithmetic and copies ran while one was open for 0% of the time, Pallas kernels for 23%

profile of v7, /device:TPU:0, one launch (start us, length us, event | category | flops | bytes accessed | tf_op | source)
XLA Modules:
  0.0 70.2 jit_solution(15689481691625097498)
XLA Ops:
  0.0 1.0 %pack.1.refs_3_ = bf16[2,256,256]{2,1,0:T(8,128)(2,1)S(1)} custom-call(bf16[256,256]{1,0:T(8,128)(2,1)} %bitcast.2, bf16[256,256]{1,0:T(8,128)(2,1)} %bitcast.3), custom_call_target="tpu_custom_call" | custom-call | tf_op jit(solution)/shard_map/pack/pallas_call | solution.py:471
  1.0 3.0 %collective-permute-start = (bf16[2,256,256]{2,1,0:T(8,128)(2,1)S(1)}, bf16[2,256,256]{2,1,0:T(8,128)(2,1)S(1)}, u32[]{:S(2)}, u32[]{:S(2)}) collective-permute-start(bf16[2,256,256]{2,1,0:T(8,128)(2,1)S(1)} %pack.1.refs_3_), channel_id=1, source_target_pairs={{0,8},{4,12},{8,0},{12,4},{16,24},{20,28},{24,16},{28,20},{1,9},{5... | collective-permute-start | bytes 786440 | tf_op jit(solution)/shard_map/ppermute | solution.py:533
  4.0 1.5 %collective-permute-start.1 = (bf16[2,256,256]{2,1,0:T(8,128)(2,1)S(1)}, bf16[2,256,256]{2,1,0:T(8,128)(2,1)S(1)}, u32[]{:S(2)}, u32[]{:S(2)}) collective-permute-start(bf16[2,256,256]{2,1,0:T(8,128)(2,1)S(1)} %pack.1.refs_3_), channel_id=1, source_target_pairs={{0,16},{4,20},{8,24},{12,28},{16,0},{20,4},{24,8},{28,12},{1,17},{... | collective-permute-start | bytes 786440 | tf_op jit(solution)/shard_map/ppermute | solution.py:533
  5.5 2.7 %mixer_local.1 = (f32[256,1024]{1,0:T(8,128)S(1)}, bf16[2,528,128]{2,1,0:T(8,128)(2,1)S(1)}, f32[256,8]{1,0:T(8,128)S(1)}) custom-call(s32[4]{0:T(128)} %refs_0_.5, f32[8]{0:T(128)} %refs_1_.4, bf16[256,1024]{1,0:T(8,128)(2,1)} %refs_2_.1, bf16[256,256]{1,0:T(8,128)(2,1)} %refs_3_.2, bf16[256,256]{1,0:T(8,128)(2,1)} %refs_4_.3, f32[8,256]{1,0:T(8,128)} %refs_5_.1), custom_call_target="tpu_custom_call" | custom-call | tf_op jit(solution)/shard_map/mixer_local/pallas_call | solution.py:52
  8.4 0.5 collective-permute-start.3
  8.9 6.0 %fetch.1 = (bf16[1024,4096]{1,0:T(8,128)(2,1)S(1)}, bf16[1024,4096]{1,0:T(8,128)(2,1)S(1)}, bf16[256,1024]{1,0:T(8,128)(2,1)S(1)}, bf16[256,256]{1,0:T(8,128)(2,1)S(1)}) custom-call(bf16[2,528,128]{2,1,0:T(8,128)(2,1)S(1)} %get-tuple-element.46.refs_0_.mine_ref, bf16[1024,4096]{1,0:T(8,128)(2,1)} %refs_1_.5, bf16[1024,4096]{1,0:T(8,128)(2,1)} %refs_2_.2, ...), custom_call_target="tpu_custom_call" | custom-call | bytes 17432576 | tf_op jit(solution)/shard_map/fetch/pallas_call | solution.py:410
  14.9 2.5 %collective-permute-done.1.refs_7_ = bf16[2,256,256]{2,1,0:T(8,128)(2,1)S(1)} collective-permute-done((bf16[2,256,256]{2,1,0:T(8,128)(2,1)S(1)}, bf16[2,256,256]{2,1,0:T(8,128)(2,1)S(1)}, u32[]{:S(2)}, u32[]{:S(2)}) %collective-permute-start.1) | collective-permute-done | bytes 262176 | tf_op jit(solution)/shard_map/ppermute | solution.py:533
  17.4 0.5 collective-permute-start.5
  18.0 1.6 %collective-permute-start.10 = (bf16[528,128]{1,0:T(8,128)(2,1)S(1)}, bf16[528,128]{1,0:T(8,128)(2,1)S(1)}, u32[]{:S(2)}, u32[]{:S(2)}) collective-permute-start(bf16[528,128]{1,0:T(8,128)(2,1)S(1)} %compose.1), channel_id=1, source_target_pairs={{0,24},{4,28},{8,16},{12,20},{16,8},{20,12},{24,0},{28,4},{1,25},{... | collective-permute-start | bytes 405512 | tf_op jit(solution)/shard_map/ppermute | solution.py:533
  19.5 1.5 %collective-permute-start.8 = (bf16[528,128]{1,0:T(8,128)(2,1)S(1)}, bf16[528,128]{1,0:T(8,128)(2,1)S(1)}, u32[]{:S(2)}, u32[]{:S(2)}) collective-permute-start(bf16[528,128]{1,0:T(8,128)(2,1)S(1)} %compose.1), channel_id=1, source_target_pairs={{0,8},{4,12},{8,0},{12,4},{16,24},{20,28},{24,16},{28,20},{1,9},{5... | collective-permute-start | bytes 405512 | tf_op jit(solution)/shard_map/ppermute | solution.py:533
  21.0 0.5 collective-permute-start.9
  21.5 1.8 %attention.2 = (bf16[128,1024]{1,0:T(8,128)(2,1)S(1)}, bf16[2,2048,256]{2,1,0:T(8,128)(2,1)S(1)}) custom-call(s32[4]{0:T(128)} %refs_0_.5, s32[32]{0:T(128)} %refs_1_.7, bf16[256,1024]{1,0:T(8,128)(2,1)S(1)} %get-tuple-element.48.refs_2_, bf16[2,256,256]{2,1,0:T(8,128)(2,1)S(1)} %pack.1.refs_3_, bf16[2,256,256]{2,1,0:T(8,128)(2,1)S(1)} %collective-permute-done.3.refs_4_, ...), custom_call_target="tpu_custom_call" | custom-call | flops 107374182400 | bytes 4194304 | tf_op jit(solution)/shard_map/attention/pallas_call | solution.py:52
  23.4 1.9 %collective-permute-done.10.refs_8_ = bf16[528,128]{1,0:T(8,128)(2,1)S(1)} collective-permute-done((bf16[528,128]{1,0:T(8,128)(2,1)S(1)}, bf16[528,128]{1,0:T(8,128)(2,1)S(1)}, u32[]{:S(2)}, u32[]{:S(2)}) %collective-permute-start.10) | collective-permute-done | bytes 135200 | tf_op jit(solution)/shard_map/ppermute | solution.py:533
  25.3 2.6 %collective-permute-done.8.refs_4_ = bf16[528,128]{1,0:T(8,128)(2,1)S(1)} collective-permute-done((bf16[528,128]{1,0:T(8,128)(2,1)S(1)}, bf16[528,128]{1,0:T(8,128)(2,1)S(1)}, u32[]{:S(2)}, u32[]{:S(2)}) %collective-permute-start.8) | collective-permute-done | bytes 135200 | tf_op jit(solution)/shard_map/ppermute | solution.py:533
  27.9 0.5 collective-permute-start.12
  28.4 0.8 %collective-permute-done.11.refs_5_ = bf16[528,128]{1,0:T(8,128)(2,1)S(1)} collective-permute-done((bf16[528,128]{1,0:T(8,128)(2,1)S(1)}, bf16[528,128]{1,0:T(8,128)(2,1)S(1)}, u32[]{:S(2)}, u32[]{:S(2)}) %collective-permute-start.11) | collective-permute-done | bytes 135200 | tf_op jit(solution)/shard_map/ppermute | solution.py:536
  29.8 0.5 finish.1.mix_ref
  30.3 0.7 %project.3 = (bf16[64,1024]{1,0:T(8,128)(2,1)S(1)}, f32[64,1024]{1,0:T(8,128)S(1)}) custom-call(bf16[128,1024]{1,0:T(8,128)(2,1)S(1)} %get-tuple-element.64.att_ref, bf16[256,1024]{1,0:T(8,128)(2,1)S(1)} %finish.1.mix_ref, bf16[1024,4096]{1,0:T(8,128)(2,1)S(1)} %get-tuple-element.61.wa_ref, bf16[1024,4096]{1,0:T(8,128)(2,1)S(1)} %get-tuple-element.62.wm_ref), custom_call_target="tpu_custom_call" | custom-call | flops 536870912 | bytes 786432 | tf_op jit(solution)/shard_map/project/pallas_call | solution.py:444
  31.1 1.6 %collective-permute-start.14 = (bf16[64,1024]{1,0:T(8,128)(2,1)S(1)}, bf16[64,1024]{1,0:T(8,128)(2,1)S(1)}, u32[]{:S(2)}, u32[]{:S(2)}) collective-permute-start(bf16[64,1024]{1,0:T(8,128)(2,1)S(1)} %get-tuple-element.68), channel_id=1, source_target_pairs={{0,1},{1,0},{2,3},{3,2},{4,5},{5,4},{6,7},{7,6},{8,9},{9,8},{10,11... | collective-permute-start | bytes 393224 | tf_op jit(solution)/shard_map/ppermute | solution.py:571
  32.7 1.8 %project.4 = (bf16[64,1536]{1,0:T(8,128)(2,1)S(1)}, f32[64,1536]{1,0:T(8,128)S(1)}, bf16[64,1536]{1,0:T(8,128)(2,1)S(1)}, f32[64,1536]{1,0:T(8,128)S(1)}) custom-call(bf16[128,1024]{1,0:T(8,128)(2,1)S(1)} %get-tuple-element.64.att_ref, bf16[256,1024]{1,0:T(8,128)(2,1)S(1)} %finish.1.mix_ref, bf16[1024,4096]{1,0:T(8,128)(2,1)S(1)} %get-tuple-element.61.wa_ref, ...), custom_call_target="tpu_custom_call" | custom-call | flops 1610612736 | bytes 2359296 | tf_op jit(solution)/shard_map/project/pallas_call | solution.py:444
  34.5 0.5 collective-permute-start.17
  35.0 1.6 %collective-permute-start.16 = (bf16[64,1536]{1,0:T(8,128)(2,1)S(1)}, bf16[64,1536]{1,0:T(8,128)(2,1)S(1)}, u32[]{:S(2)}, u32[]{:S(2)}) collective-permute-start(bf16[64,1536]{1,0:T(8,128)(2,1)S(1)} %get-tuple-element.72), channel_id=1, source_target_pairs={{0,1},{1,0},{2,3},{3,2},{4,5},{5,4},{6,7},{7,6},{8,9},{9,8},{10,11... | collective-permute-start | bytes 589832 | tf_op jit(solution)/shard_map/ppermute | solution.py:571
  36.8 5.5 %collective-permute-done.17 = bf16[64,1536]{1,0:T(8,128)(2,1)S(1)} collective-permute-done((bf16[64,1536]{1,0:T(8,128)(2,1)S(1)}, bf16[64,1536]{1,0:T(8,128)(2,1)S(1)}, u32[]{:S(2)}, u32[]{:S(2)}) %collective-permute-start.17) | collective-permute-done | bytes 196640 | tf_op jit(solution)/shard_map/ppermute | solution.py:571
  42.4 2.7 %collective-permute-start.19 = (bf16[64,1536]{1,0:T(8,128)(2,1)S(1)}, bf16[64,1536]{1,0:T(8,128)(2,1)S(1)}, u32[]{:S(2)}, u32[]{:S(2)}) collective-permute-start(bf16[64,1536]{1,0:T(8,128)(2,1)S(1)} %add_convert_fusion.1), channel_id=1, source_target_pairs={{0,2},{1,3},{2,0},{3,1},{4,6},{5,7},{6,4},{7,5},{8,10},{9,11},{10,... | collective-permute-start | bytes 589832 | tf_op jit(solution)/shard_map/ppermute | solution.py:574
  45.0 0.3 collective-permute-start.18
  45.4 1.6 %attention.3.att_ref = bf16[128,1024]{1,0:T(8,128)(2,1)S(1)} custom-call(s32[4]{0:T(128)} %refs_0_.5, s32[32]{0:T(128)} %refs_1_.7, bf16[256,1024]{1,0:T(8,128)(2,1)S(1)} %get-tuple-element.48.refs_2_, bf16[2,2048,256]{2,1,0:T(8,128)(2,1)S(1)} %get-tuple-element.69.refs_3_), custom_call_target="tpu_custom_call" | custom-call | tf_op jit(solution)/shard_map/attention/pallas_call | solution.py:52
  47.0 2.3 %project.5 = (bf16[64,4096]{1,0:T(8,128)(2,1)S(1)}, f32[64,4096]{1,0:T(8,128)S(1)}) custom-call(bf16[128,1024]{1,0:T(8,128)(2,1)S(1)} %attention.3.att_ref, bf16[256,1024]{1,0:T(8,128)(2,1)S(1)} %finish.1.mix_ref, bf16[1024,4096]{1,0:T(8,128)(2,1)S(1)} %get-tuple-element.61.wa_ref, bf16[1024,4096]{1,0:T(8,128)(2,1)S(1)} %get-tuple-element.62.wm_ref), custom_call_target="tpu_custom_call" | custom-call | tf_op jit(solution)/shard_map/project/pallas_call | solution.py:444
  49.4 1.0 %collective-permute-start.15 = (bf16[64,4096]{1,0:T(8,128)(2,1)S(1)}, bf16[64,4096]{1,0:T(8,128)(2,1)S(1)}, u32[]{:S(2)}, u32[]{:S(2)}) collective-permute-start(bf16[64,4096]{1,0:T(8,128)(2,1)S(1)} %get-tuple-element.71), channel_id=1, source_target_pairs={{0,1},{1,0},{2,3},{3,2},{4,5},{5,4},{6,7},{7,6},{8,9},{9,8},{10,11... | collective-permute-start | bytes 1572872 | tf_op jit(solution)/shard_map/ppermute | solution.py:571
  50.3 8.1 %collective-permute-done.18.refs_0_ = bf16[64,1024]{1,0:T(8,128)(2,1)S(1)} collective-permute-done((bf16[64,1024]{1,0:T(8,128)(2,1)S(1)}, bf16[64,1024]{1,0:T(8,128)(2,1)S(1)}, u32[]{:S(2)}, u32[]{:S(2)}) %collective-permute-start.18) | collective-permute-done | bytes 131104 | tf_op jit(solution)/shard_map/ppermute | solution.py:574
  58.5 8.3 %collective-permute-done.20.refs_2_ = bf16[64,1536]{1,0:T(8,128)(2,1)S(1)} collective-permute-done((bf16[64,1536]{1,0:T(8,128)(2,1)S(1)}, bf16[64,1536]{1,0:T(8,128)(2,1)S(1)}, u32[]{:S(2)}, u32[]{:S(2)}) %collective-permute-start.20) | collective-permute-done | bytes 196640 | tf_op jit(solution)/shard_map/ppermute | solution.py:574
  66.9 2.4 %collective-permute-done.15.near_ref = bf16[64,4096]{1,0:T(8,128)(2,1)S(1)} collective-permute-done((bf16[64,4096]{1,0:T(8,128)(2,1)S(1)}, bf16[64,4096]{1,0:T(8,128)(2,1)S(1)}, u32[]{:S(2)}, u32[]{:S(2)}) %collective-permute-start.15) | collective-permute-done | bytes 524320 | tf_op jit(solution)/shard_map/ppermute | solution.py:571
  69.3 0.9 %assemble.1 = bf16[64,4096]{1,0:T(8,128)(2,1)} custom-call(f32[64,4096]{1,0:T(8,128)S(1)} %get-tuple-element.70.keep_ref, bf16[64,4096]{1,0:T(8,128)(2,1)S(1)} %collective-permute-done.15.near_ref, bf16[64,1024]{1,0:T(8,128)(2,1)S(1)} %collective-permute-done.18.refs_0_, bf16[64,1536]{1,0:T(8,128)(2,1)S(1)} %collective-permute-done.19.refs_1_, ...), custom_call_target="tpu_custom_call" | custom-call | tf_op jit(solution)/shard_map/assemble/pallas_call | solution.py:500
  (24 shorter events, 1.0 us)
Async XLA Ops:
  1.0 13.9 %collective-permute-start = (bf16[2,256,256]{2,1,0:T(8,128)(2,1)S(1)}, bf16[2,256,256]{2,1,0:T(8,128)(2,1)S(1)}, u32[]{:S(2)}, u32[]{:S(2)}) collective-permute-start(bf16[2,256,256]{2,1,0:T(8,128)(2,1)S(1)} %pack.1.refs_3_), channel_id=1, source_target_pairs={{0,8},{4,12},{8,0},{12,4},{16,24},{20,28},{24,16},{28,20},{1,9},{5... | collective-permute-start | bytes 786440 | tf_op jit(solution)/shard_map/ppermute | solution.py:533
  4.0 13.4 %collective-permute-start.1 = (bf16[2,256,256]{2,1,0:T(8,128)(2,1)S(1)}, bf16[2,256,256]{2,1,0:T(8,128)(2,1)S(1)}, u32[]{:S(2)}, u32[]{:S(2)}) collective-permute-start(bf16[2,256,256]{2,1,0:T(8,128)(2,1)S(1)} %pack.1.refs_3_), channel_id=1, source_target_pairs={{0,16},{4,20},{8,24},{12,28},{16,0},{20,4},{24,8},{28,12},{1,17},{... | collective-permute-start | bytes 786440 | tf_op jit(solution)/shard_map/ppermute | solution.py:533
  5.5 11.9 %collective-permute-start.2 = (bf16[2,256,256]{2,1,0:T(8,128)(2,1)S(1)}, bf16[2,256,256]{2,1,0:T(8,128)(2,1)S(1)}, u32[]{:S(2)}, u32[]{:S(2)}) collective-permute-start(bf16[2,256,256]{2,1,0:T(8,128)(2,1)S(1)} %pack.1.refs_3_), channel_id=1, source_target_pairs={{0,24},{4,28},{8,16},{12,20},{16,8},{20,12},{24,0},{28,4},{1,25},{... | collective-permute-start | bytes 786440 | tf_op jit(solution)/shard_map/ppermute | solution.py:533
  8.3 9.6 %collective-permute-start.7 = (bf16[2,528,128]{2,1,0:T(8,128)(2,1)S(1)}, bf16[2,528,128]{2,1,0:T(8,128)(2,1)S(1)}, u32[]{:S(2)}, u32[]{:S(2)}) collective-permute-start(bf16[2,528,128]{2,1,0:T(8,128)(2,1)S(1)} %get-tuple-element.46.refs_0_.mine_ref), channel_id=1, source_target_pairs={{0,4},{4,0},{8,12},{12,8},{16,20},{20,16},{24,28},{28,24},{1,5},{5... | collective-permute-start | bytes 811016 | tf_op jit(solution)/shard_map/ppermute | solution.py:536
  8.4 11.2 %collective-permute-start.3 = (bf16[2,256,256]{2,1,0:T(8,128)(2,1)S(1)}, bf16[2,256,256]{2,1,0:T(8,128)(2,1)S(1)}, u32[]{:S(2)}, u32[]{:S(2)}) collective-permute-start(bf16[2,256,256]{2,1,0:T(8,128)(2,1)S(1)} %pack.1.refs_3_), channel_id=1, source_target_pairs={{0,4},{4,0},{8,12},{12,8},{16,20},{20,16},{24,28},{28,24},{1,5},{5... | collective-permute-start | bytes 786440 | tf_op jit(solution)/shard_map/ppermute | solution.py:536
  17.4 3.6 %collective-permute-start.4 = (bf16[2,256,256]{2,1,0:T(8,128)(2,1)S(1)}, bf16[2,256,256]{2,1,0:T(8,128)(2,1)S(1)}, u32[]{:S(2)}, u32[]{:S(2)}) collective-permute-start(bf16[2,256,256]{2,1,0:T(8,128)(2,1)S(1)} %collective-permute-done.refs_5_), channel_id=1, source_target_pairs={{0,4},{4,0},{8,12},{12,8},{16,20},{20,16},{24,28},{28,24},{1,5},{5... | collective-permute-start | bytes 786440 | tf_op jit(solution)/shard_map/ppermute | solution.py:536
  17.4 4.1 %collective-permute-start.5 = (bf16[2,256,256]{2,1,0:T(8,128)(2,1)S(1)}, bf16[2,256,256]{2,1,0:T(8,128)(2,1)S(1)}, u32[]{:S(2)}, u32[]{:S(2)}) collective-permute-start(bf16[2,256,256]{2,1,0:T(8,128)(2,1)S(1)} %collective-permute-done.1.refs_7_), channel_id=1, source_target_pairs={{0,4},{4,0},{8,12},{12,8},{16,20},{20,16},{24,28},{28,24},{1,5},{5... | collective-permute-start | bytes 786440 | tf_op jit(solution)/shard_map/ppermute | solution.py:536
  17.9 3.6 %collective-permute-start.6 = (bf16[2,256,256]{2,1,0:T(8,128)(2,1)S(1)}, bf16[2,256,256]{2,1,0:T(8,128)(2,1)S(1)}, u32[]{:S(2)}, u32[]{:S(2)}) collective-permute-start(bf16[2,256,256]{2,1,0:T(8,128)(2,1)S(1)} %collective-permute-done.2.refs_9_), channel_id=1, source_target_pairs={{0,4},{4,0},{8,12},{12,8},{16,20},{20,16},{24,28},{28,24},{1,5},{5... | collective-permute-start | bytes 786440 | tf_op jit(solution)/shard_map/ppermute | solution.py:536
  18.0 7.3 %collective-permute-start.10 = (bf16[528,128]{1,0:T(8,128)(2,1)S(1)}, bf16[528,128]{1,0:T(8,128)(2,1)S(1)}, u32[]{:S(2)}, u32[]{:S(2)}) collective-permute-start(bf16[528,128]{1,0:T(8,128)(2,1)S(1)} %compose.1), channel_id=1, source_target_pairs={{0,24},{4,28},{8,16},{12,20},{16,8},{20,12},{24,0},{28,4},{1,25},{... | collective-permute-start | bytes 405512 | tf_op jit(solution)/shard_map/ppermute | solution.py:533
  19.5 8.4 %collective-permute-start.8 = (bf16[528,128]{1,0:T(8,128)(2,1)S(1)}, bf16[528,128]{1,0:T(8,128)(2,1)S(1)}, u32[]{:S(2)}, u32[]{:S(2)}) collective-permute-start(bf16[528,128]{1,0:T(8,128)(2,1)S(1)} %compose.1), channel_id=1, source_target_pairs={{0,8},{4,12},{8,0},{12,4},{16,24},{20,28},{24,16},{28,20},{1,9},{5... | collective-permute-start | bytes 405512 | tf_op jit(solution)/shard_map/ppermute | solution.py:533
  21.0 6.9 %collective-permute-start.9 = (bf16[528,128]{1,0:T(8,128)(2,1)S(1)}, bf16[528,128]{1,0:T(8,128)(2,1)S(1)}, u32[]{:S(2)}, u32[]{:S(2)}) collective-permute-start(bf16[528,128]{1,0:T(8,128)(2,1)S(1)} %compose.1), channel_id=1, source_target_pairs={{0,16},{4,20},{8,24},{12,28},{16,0},{20,4},{24,8},{28,12},{1,17},{... | collective-permute-start | bytes 405512 | tf_op jit(solution)/shard_map/ppermute | solution.py:533
  27.9 1.4 %collective-permute-start.11 = (bf16[528,128]{1,0:T(8,128)(2,1)S(1)}, bf16[528,128]{1,0:T(8,128)(2,1)S(1)}, u32[]{:S(2)}, u32[]{:S(2)}) collective-permute-start(bf16[528,128]{1,0:T(8,128)(2,1)S(1)} %collective-permute-done.8.refs_4_), channel_id=1, source_target_pairs={{0,4},{4,0},{8,12},{12,8},{16,20},{20,16},{24,28},{28,24},{1,5},{5... | collective-permute-start | bytes 405512 | tf_op jit(solution)/shard_map/ppermute | solution.py:536
  27.9 1.5 %collective-permute-start.12 = (bf16[528,128]{1,0:T(8,128)(2,1)S(1)}, bf16[528,128]{1,0:T(8,128)(2,1)S(1)}, u32[]{:S(2)}, u32[]{:S(2)}) collective-permute-start(bf16[528,128]{1,0:T(8,128)(2,1)S(1)} %collective-permute-done.9.refs_6_), channel_id=1, source_target_pairs={{0,4},{4,0},{8,12},{12,8},{16,20},{20,16},{24,28},{28,24},{1,5},{5... | collective-permute-start | bytes 405512 | tf_op jit(solution)/shard_map/ppermute | solution.py:536
  28.4 1.4 %collective-permute-start.13 = (bf16[528,128]{1,0:T(8,128)(2,1)S(1)}, bf16[528,128]{1,0:T(8,128)(2,1)S(1)}, u32[]{:S(2)}, u32[]{:S(2)}) collective-permute-start(bf16[528,128]{1,0:T(8,128)(2,1)S(1)} %collective-permute-done.10.refs_8_), channel_id=1, source_target_pairs={{0,4},{4,0},{8,12},{12,8},{16,20},{20,16},{24,28},{28,24},{1,5},{5... | collective-permute-start | bytes 405512 | tf_op jit(solution)/shard_map/ppermute | solution.py:536
  31.1 5.7 %collective-permute-start.14 = (bf16[64,1024]{1,0:T(8,128)(2,1)S(1)}, bf16[64,1024]{1,0:T(8,128)(2,1)S(1)}, u32[]{:S(2)}, u32[]{:S(2)}) collective-permute-start(bf16[64,1024]{1,0:T(8,128)(2,1)S(1)} %get-tuple-element.68), channel_id=1, source_target_pairs={{0,1},{1,0},{2,3},{3,2},{4,5},{5,4},{6,7},{7,6},{8,9},{9,8},{10,11... | collective-permute-start | bytes 393224 | tf_op jit(solution)/shard_map/ppermute | solution.py:571
  34.5 7.8 %collective-permute-start.17 = (bf16[64,1536]{1,0:T(8,128)(2,1)S(1)}, bf16[64,1536]{1,0:T(8,128)(2,1)S(1)}, u32[]{:S(2)}, u32[]{:S(2)}) collective-permute-start(bf16[64,1536]{1,0:T(8,128)(2,1)S(1)} %get-tuple-element.74), channel_id=1, source_target_pairs={{0,1},{1,0},{2,3},{3,2},{4,5},{5,4},{6,7},{7,6},{8,9},{9,8},{10,11... | collective-permute-start | bytes 589832 | tf_op jit(solution)/shard_map/ppermute | solution.py:571
  35.0 15.3 %collective-permute-start.16 = (bf16[64,1536]{1,0:T(8,128)(2,1)S(1)}, bf16[64,1536]{1,0:T(8,128)(2,1)S(1)}, u32[]{:S(2)}, u32[]{:S(2)}) collective-permute-start(bf16[64,1536]{1,0:T(8,128)(2,1)S(1)} %get-tuple-element.72), channel_id=1, source_target_pairs={{0,1},{1,0},{2,3},{3,2},{4,5},{5,4},{6,7},{7,6},{8,9},{9,8},{10,11... | collective-permute-start | bytes 589832 | tf_op jit(solution)/shard_map/ppermute | solution.py:571
  42.4 16.0 %collective-permute-start.19 = (bf16[64,1536]{1,0:T(8,128)(2,1)S(1)}, bf16[64,1536]{1,0:T(8,128)(2,1)S(1)}, u32[]{:S(2)}, u32[]{:S(2)}) collective-permute-start(bf16[64,1536]{1,0:T(8,128)(2,1)S(1)} %add_convert_fusion.1), channel_id=1, source_target_pairs={{0,2},{1,3},{2,0},{3,1},{4,6},{5,7},{6,4},{7,5},{8,10},{9,11},{10,... | collective-permute-start | bytes 589832 | tf_op jit(solution)/shard_map/ppermute | solution.py:574
  45.0 13.4 %collective-permute-start.18 = (bf16[64,1024]{1,0:T(8,128)(2,1)S(1)}, bf16[64,1024]{1,0:T(8,128)(2,1)S(1)}, u32[]{:S(2)}, u32[]{:S(2)}) collective-permute-start(bf16[64,1024]{1,0:T(8,128)(2,1)S(1)} %add_convert_fusion.2), channel_id=1, source_target_pairs={{0,2},{1,3},{2,0},{3,1},{4,6},{5,7},{6,4},{7,5},{8,10},{9,11},{10,... | collective-permute-start | bytes 393224 | tf_op jit(solution)/shard_map/ppermute | solution.py:574
  49.4 19.9 %collective-permute-start.15 = (bf16[64,4096]{1,0:T(8,128)(2,1)S(1)}, bf16[64,4096]{1,0:T(8,128)(2,1)S(1)}, u32[]{:S(2)}, u32[]{:S(2)}) collective-permute-start(bf16[64,4096]{1,0:T(8,128)(2,1)S(1)} %get-tuple-element.71), channel_id=1, source_target_pairs={{0,1},{1,0},{2,3},{3,2},{4,5},{5,4},{6,7},{7,6},{8,9},{9,8},{10,11... | collective-permute-start | bytes 1572872 | tf_op jit(solution)/shard_map/ppermute | solution.py:571
  58.5 8.4 %collective-permute-start.20 = (bf16[64,1536]{1,0:T(8,128)(2,1)S(1)}, bf16[64,1536]{1,0:T(8,128)(2,1)S(1)}, u32[]{:S(2)}, u32[]{:S(2)}) collective-permute-start(bf16[64,1536]{1,0:T(8,128)(2,1)S(1)} %add_convert_fusion), channel_id=1, source_target_pairs={{0,2},{1,3},{2,0},{3,1},{4,6},{5,7},{6,4},{7,5},{8,10},{9,11},{10,... | collective-permute-start | bytes 589832 | tf_op jit(solution)/shard_map/ppermute | solution.py:574
